TPU v7x, 128 devices: a whole 4x4x4 slice. The times are simulated.
128 devices in a mesh: tok: 16 (over z, y), mdl: 8 (over x, core).
Axes of the slice: x: 4, y: 4, z: 4, core: 2. Of those that a mesh axis runs over, the one named last changes fastest.
Arguments:
- tokens: bfloat16 [4096, 5120], P('tok'), may hold values from -32 to 32
- norm_gain: bfloat16 [5120], replicated, may hold values from 0.099609375 to 1.8984375
- w_query: bfloat16 [5120, 4096], P(None, 'mdl'), may hold values from -0.078125 to 0.078125
- w_key: bfloat16 [5120, 1024], P(None, 'mdl'), may hold values from -0.3125 to 0.3125
- w_value: bfloat16 [5120, 1024], P(None, 'mdl'), may hold values from -0.078125 to 0.078125
- w_out: bfloat16 [4096, 5120], P('mdl'), may hold values from -0.09375 to 0.09375
- prompt_keys: bfloat16 [6, 4096, 8, 128], P(None, 'tok', 'mdl'), may hold values from -6 to 6
- prompt_values: bfloat16 [6, 4096, 8, 128], P(None, 'tok', 'mdl'), may hold values from -24 to 24
- cache_keys: bfloat16 [128, 2048, 8, 128], P('tok', None, 'mdl'), may hold values from -6 to 6
- cache_values: bfloat16 [128, 2048, 8, 128], P('tok', None, 'mdl'), may hold values from -24 to 24
- cache_length: int32 [128], P('tok'), may hold values from 1 to 2048, as said below
- request_group: int32 [128], replicated, may hold values from 0 to 5
- ancestors: int32 [128, 32, 32], P('tok'), may hold values from 0 to 1, as said below
- accepted: int32 [128, 8], P('tok'), may hold values from -1 to 31, as said below
Outputs:
- attention_out: bfloat16 [4096, 5120], P('tok', 'mdl')
- compact_rows: bfloat16 [128, 8, 5120], P('tok', None, 'mdl')
Inputs may be any that keep to these rules, and one draw needn't show every extreme that they name: `cache_length`: some request has exactly 2048 live slots. ancestors[r, a, b] is 1 where tree slot b is slot a itself or an ancestor of it in request r's draft tree, else 0; each tree has one root, and slots are in no particular order. Entry k of request r is the tree slot of the accepted path's node at depth k, from the root on, for k below the path's length, and -1 after it; a path holds 1 to 8 nodes, and some request's path holds 8.
All inputs are finite; a program needn't handle non-finite values.
Results may differ from a plain program's by a relative error of at most 0.017.
Values may be sent and summed in bfloat16 or wider, within the bound.
No kernel may reach another device: no remote copies, remote signals or barrier semaphores. Data moves between devices by JAX's collectives and lax.ppermute only.
A program may use at most 128 MiB of HBM per device.

v0:
```python
import math

import jax
import jax.numpy as jnp
import numpy as np
from jax import lax
from jax.experimental import pallas as pl
from jax.experimental.pallas import tpu as pltpu
from jax.sharding import PartitionSpec as P


PROMPT = 4096
THETA = 100000000.0
EPS = 1e-05

F32 = jnp.float32
BF16 = jnp.bfloat16

ANY = pl.BlockSpec(memory_space=pl.ANY)
SMEM = pl.BlockSpec(memory_space=pltpu.SMEM)
VM = pl.BlockSpec(memory_space=pltpu.VMEM)
CHUNKS = 5
KB = 512
NT = (((1,), (1,)), ((), ()))


def params(mib):
    return pltpu.CompilerParams(vmem_limit_bytes=mib * 1024 * 1024)


def dot(a, b):
    return jnp.dot(a, b, preferred_element_type=F32)


def dot_nt(a, b):
    return lax.dot_general(a, b, NT, preferred_element_type=F32)


def rotate(x, cosine, sine):
    return x * cosine + pltpu.roll(x, x.shape[1] // 2, 1) * sine


def query_kernel(len_ref, tok_hbm, gain_ref, wq_hbm, anc_ref, inv_ref, q_ref, normed_ref, cos_ref, sin_ref, tok, wq, sems):
    rows, width = tok.shape
    requests = len_ref.shape[0]
    tree = rows // requests
    get_tok = pltpu.make_async_copy(tok_hbm, tok, sems.at[0])
    get_tok.start()
    part = width // CHUNKS
    copies = []
    for i in range(CHUNKS):
        c = pltpu.make_async_copy(
            wq_hbm.at[pl.ds(i * part, part)], wq.at[pl.ds(i * part, part)], sems.at[1 + i]
        )
        c.start()
        copies.append(c)
    depth = jnp.sum(anc_ref[...], axis=1, keepdims=True).astype(F32) - 1.0
    places = jnp.concatenate(
        [
            depth[r * tree : (r + 1) * tree] + (PROMPT + len_ref[r]).astype(F32)
            for r in range(requests)
        ],
        axis=0,
    )
    angles = places * inv_ref[...]
    lane = lax.broadcasted_iota(jnp.int32, angles.shape, 1)
    cosine = jnp.cos(angles)
    sine = jnp.sin(angles)
    sine = jnp.where(lane < angles.shape[1] // 2, -sine, sine)
    cos_ref[...] = cosine
    sin_ref[...] = sine
    get_tok.wait()

    def norm(i, _):
        at = pl.ds(pl.multiple_of(i * 32, 32), 32)
        wide = tok[at, :].astype(F32)
        scale = lax.rsqrt(jnp.mean(wide * wide, axis=1, keepdims=True) + EPS)
        normed_ref[at, :] = (wide * scale * gain_ref[...].astype(F32)).astype(BF16)
        return 0

    lax.fori_loop(0, rows // 32, norm, 0)
    acc = None
    for i in range(CHUNKS):
        copies[i].wait()
        d = dot(normed_ref[:, i * part : (i + 1) * part], wq[i * part : (i + 1) * part, :])
        acc = d if acc is None else acc + d
    hd = inv_ref.shape[1]
    heads = acc.shape[1] // hd
    fold = hd**-0.5 * math.log2(math.e)
    for g in range(heads):
        turned = (rotate(acc[:, g * hd : (g + 1) * hd], cosine, sine) * fold).astype(BF16)
        for r in range(requests):
            q_ref[pl.ds((r * heads + g) * tree, tree), :] = turned[r * tree : (r + 1) * tree]


def query_call(lengths, tokens, gain, w_query, ancestors, inverse):
    rows, width = tokens.shape
    hd = inverse.shape[1]
    heads = w_query.shape[1] // hd
    return pl.pallas_call(
        query_kernel,
        in_specs=[SMEM, ANY, VM, ANY, VM, VM],
        out_specs=[VM, VM, VM, VM],
        out_shape=[
            jax.ShapeDtypeStruct((rows * heads, hd), BF16),
            jax.ShapeDtypeStruct((rows, width), BF16),
            jax.ShapeDtypeStruct((rows, hd), F32),
            jax.ShapeDtypeStruct((rows, hd), F32),
        ],
        scratch_shapes=[
            pltpu.VMEM((rows, width), BF16),
            pltpu.VMEM(w_query.shape, BF16),
            pltpu.SemaphoreType.DMA((1 + CHUNKS,)),
        ],
        compiler_params=params(24),
        name="query_proj",
    )(lengths, tokens, gain, w_query, ancestors, inverse)


def tree_kernel(normed_ref, wk_hbm, wv_hbm, cos_ref, sin_ref, q_ref, anc_ref, out_ref, w, sems):
    rows, tree = anc_ref.shape
    hd = q_ref.shape[1]
    group = q_ref.shape[0] // rows
    qrows = group * tree
    part = w.shape[0] // CHUNKS
    copies = []
    for i in range(CHUNKS):
        at = pl.ds(i * part, part)
        ck = pltpu.make_async_copy(wk_hbm.at[at], w.at[at, pl.ds(0, hd)], sems.at[0, i])
        cv = pltpu.make_async_copy(wv_hbm.at[at], w.at[at, pl.ds(hd, hd)], sems.at[1, i])
        ck.start()
        cv.start()
        copies.append((ck, cv))
    both = None
    for i in range(CHUNKS):
        copies[i][0].wait()
        copies[i][1].wait()
        d = dot(normed_ref[:, i * part : (i + 1) * part], w[i * part : (i + 1) * part, :])
        both = d if both is None else both + d
    new_keys = rotate(both[:, :hd], cos_ref[...], sin_ref[...]).astype(BF16)
    new_values = both[:, hd:].astype(BF16)
    ones = jnp.ones((tree, hd), BF16)
    for r in range(rows // tree):
        at = slice(r * tree, (r + 1) * tree)
        here = pl.ds(r * qrows, qrows)
        scores = dot_nt(q_ref[here, :], new_keys[at])
        seen = jnp.concatenate([anc_ref[at, :]] * group, axis=0)
        weights = jnp.where(seen > 0, jnp.exp2(scores), 0.0).astype(BF16)
        out_ref[here, :] = dot(weights, jnp.concatenate([new_values[at], ones], axis=1))


def tree_call(normed, w_key, w_value, cosine, sine, q, ancestors):
    hd = q.shape[1]
    return pl.pallas_call(
        tree_kernel,
        in_specs=[VM, ANY, ANY, VM, VM, VM, VM],
        out_specs=VM,
        out_shape=jax.ShapeDtypeStruct((q.shape[0], 2 * hd), F32),
        scratch_shapes=[
            pltpu.VMEM((normed.shape[1], 2 * hd), BF16),
            pltpu.SemaphoreType.DMA((2, CHUNKS)),
        ],
        compiler_params=params(16),
        name="tree_attention",
    )(normed, w_key, w_value, cosine, sine, q, ancestors)


def prompt_sum(q, g, pieces, ones):
    weights, values = [], []
    for kref, koff, vref, voff in pieces:
        weights.append(jnp.exp2(dot_nt(q, kref[koff + g])).astype(BF16))
        values.append(jnp.concatenate([vref[voff + g], ones], axis=1))
    return dot(jnp.concatenate(weights, axis=1), jnp.concatenate(values, axis=0))


def pieces_of(kv, kv_r, kv_l, k_o, v_o):
    n = k_o.shape[0]
    return [(kv, 0, kv, n), (kv_r, 0, kv_r, n), (kv_l, 0, kv_l, n), (k_o, 0, v_o, 0)]


def remote_kernel(group_ref, at_ref, q_ref, kv, kv_r, kv_l, k_o, v_o, out_ref, *, requests, shift, n_tok):
    hd = q_ref.shape[1]
    qrows = q_ref.shape[0] // requests
    pieces = pieces_of(kv, kv_r, kv_l, k_o, v_o)
    ones = jnp.ones((k_o.shape[1], hd), BF16)
    diagonal = lax.broadcasted_iota(jnp.int32, (qrows, hd), 0) == lax.broadcasted_iota(
        jnp.int32, (qrows, hd), 1
    )

    base = lax.rem(at_ref[0] + n_tok - shift, n_tok) * requests
    totals = []
    for r in range(requests):
        at = pl.ds(r * qrows, qrows)
        acc = prompt_sum(q_ref[at, :], group_ref[base + r], pieces, ones)
        out_ref[at, :] = acc[:, :hd].astype(BF16)
        totals.append(jnp.sum(jnp.where(diagonal, acc[:, hd:], 0.0), axis=0, keepdims=True))
    total = jnp.concatenate(totals, axis=0)
    high = total.astype(BF16)
    low = (total - high.astype(F32)).astype(BF16)
    out_ref[pl.ds(requests * qrows, 2 * requests), :] = jnp.concatenate([high, low], axis=0)


def remote_call(groups, at, q, prompts, requests, shift, n_tok):
    rows, hd = q.shape
    return pl.pallas_call(
        lambda *refs: remote_kernel(*refs, requests=requests, shift=shift, n_tok=n_tok),
        in_specs=[SMEM, SMEM] + [VM] * 6,
        out_specs=VM,
        out_shape=jax.ShapeDtypeStruct((rows + 2 * requests, hd), BF16),
        compiler_params=params(12),
        name="prompt_remote",
    )(groups, at, q, *prompts)


def home_kernel(
    group_ref, at_ref, len_ref, q_ref, kv, kv_r, kv_l, k_o, v_o, own_ref, ck_hbm, cv_hbm, out_ref,
    keys, values, sems,
):
    requests, _, hd = keys.shape
    qrows = q_ref.shape[0] // requests

    def cache_copies(r, b):
        at = pl.ds(pl.multiple_of(b * KB, KB), KB)
        return (
            pltpu.make_async_copy(ck_hbm.at[r, at], keys.at[r, at], sems.at[0, r, b]),
            pltpu.make_async_copy(cv_hbm.at[r, at], values.at[r, at], sems.at[1, r, b]),
        )

    def live(r):
        return (len_ref[r] + KB - 1) // KB

    for r in range(requests):

        def begin(b, _, r=r):
            for c in cache_copies(r, b):
                c.start()
            return 0

        lax.fori_loop(0, live(r), begin, 0)
    pieces = pieces_of(kv, kv_r, kv_l, k_o, v_o)
    ones = jnp.ones((k_o.shape[1], hd), BF16)
    for r in range(requests):
        at = pl.ds(r * qrows, qrows)
        out_ref[at, :] = own_ref[at, :] + prompt_sum(
            q_ref[at, :], group_ref[at_ref[0] * requests + r], pieces, ones
        )
    column = lax.broadcasted_iota(jnp.int32, (qrows, KB), 1)
    ones = jnp.ones((KB, hd), BF16)
    for r in range(requests):
        at = pl.ds(r * qrows, qrows)

        def block(b, _, r=r, at=at):
            for c in cache_copies(r, b):
                c.wait()
            rows_at = pl.ds(pl.multiple_of(b * KB, KB), KB)
            s = dot_nt(q_ref[at, :], keys[r, rows_at, :])
            p = jnp.where(column < len_ref[r] - b * KB, jnp.exp2(s), 0.0).astype(BF16)
            out_ref[at, :] += dot(p, jnp.concatenate([values[r, rows_at, :], ones], axis=1))
            return 0

        lax.fori_loop(0, live(r), block, 0)


def home_call(groups, at, lengths, q, prompts, own, cache_keys, cache_values):
    requests, slots, _ = cache_keys.shape
    return pl.pallas_call(
        home_kernel,
        in_specs=[SMEM, SMEM, SMEM] + [VM] * 7 + [ANY, ANY],
        out_specs=VM,
        out_shape=jax.ShapeDtypeStruct(own.shape, F32),
        scratch_shapes=[
            pltpu.VMEM(cache_keys.shape, BF16),
            pltpu.VMEM(cache_values.shape, BF16),
            pltpu.SemaphoreType.DMA((2, requests, slots // KB)),
        ],
        compiler_params=params(24),
        name="home_attention",
    )(groups, at, lengths, q, *prompts, own, cache_keys, cache_values)


def merge_kernel(home_ref, a_ref, b_ref, c_ref, out_ref, *, requests):
    hd = a_ref.shape[1]
    qrows = home_ref.shape[0] // requests
    tree = out_ref.shape[0] // requests
    total = None
    for ref in (a_ref, b_ref, c_ref):
        both = ref[pl.ds(requests * qrows, 2 * requests), :].astype(F32)
        t = both[:requests] + both[requests:]
        total = t if total is None else total + t
    diagonal = lax.broadcasted_iota(jnp.int32, (qrows, hd), 0) == lax.broadcasted_iota(
        jnp.int32, (qrows, hd), 1
    )
    for r in range(requests):
        at = pl.ds(r * qrows, qrows)
        num = home_ref[at, pl.ds(0, hd)]
        for ref in (a_ref, b_ref, c_ref):
            num = num + ref[at, :].astype(F32)
        den = home_ref[at, pl.ds(hd, hd)] + jnp.sum(
            jnp.where(diagonal, jnp.broadcast_to(total[r : r + 1], (qrows, hd)), 0.0),
            axis=1,
            keepdims=True,
        )
        out = (num / den).astype(BF16)
        for g in range(qrows // tree):
            out_ref[pl.ds(r * tree, tree), pl.ds(g * hd, hd)] = out[g * tree : (g + 1) * tree]


def merge_call(home, a, b, c, requests, rows):
    hd = a.shape[1]
    return pl.pallas_call(
        lambda *refs: merge_kernel(*refs, requests=requests),
        in_specs=[VM] * 4,
        out_specs=VM,
        out_shape=jax.ShapeDtypeStruct((rows, home.shape[0] // rows * hd), BF16),
        compiler_params=params(8),
        name="merge",
    )(home, a, b, c)


def columns_kernel(mdl_ref, w_hbm, mine_ref, send_ref, sems):
    count, _, cols = mine_ref.shape
    copies = []
    for i in range(count):
        for j, ref in enumerate((mine_ref, send_ref)):
            side = lax.rem(mdl_ref[0] + j, 2)
            start = pl.multiple_of((2 * i + side) * cols, 128)
            c = pltpu.make_async_copy(w_hbm.at[:, pl.ds(start, cols)], ref.at[i], sems.at[j, i])
            c.start()
            copies.append(c)
    for c in copies:
        c.wait()


def columns_call(mdl, w_out, count):
    cols = w_out.shape[1] // (2 * count)
    return pl.pallas_call(
        columns_kernel,
        in_specs=[SMEM, ANY],
        out_specs=[VM, VM],
        out_shape=[jax.ShapeDtypeStruct((count, w_out.shape[0], cols), BF16)] * 2,
        scratch_shapes=[pltpu.SemaphoreType.DMA((2, count))],
        compiler_params=params(8),
        name="out_columns",
    )(mdl, w_out)


def out_kernel(mdl_ref, mine_ref, other_ref, wa, wb, *outs, shifts):
    for shift, out in zip(shifts, outs):
        i = lax.rem(mdl_ref[0] // 2 + shift, wa.shape[0])
        out[...] = (dot(mine_ref[...], wa[i]) + dot(other_ref[...], wb[i])).astype(out.dtype)


def out_call(mdl, mine, other, w_mine, w_other, shifts, dtype):
    shape = (mine.shape[0], w_other.shape[2])
    return pl.pallas_call(
        lambda *refs: out_kernel(*refs, shifts=shifts),
        in_specs=[SMEM] + [VM] * 4,
        out_specs=[VM] * len(shifts),
        out_shape=[jax.ShapeDtypeStruct(shape, dtype)] * len(shifts),
        compiler_params=params(12),
        name="out_proj",
    )(mdl, mine, other, w_mine, w_other)


def last_kernel(acc_ref, at_ref, own_ref, a_ref, b_ref, c_ref, tok_hbm, out_ref, rows_ref, tok, sums, kept, sem):
    cols = own_ref.shape[1]
    requests, most = acc_ref.shape
    tree = own_ref.shape[0] // requests
    get = pltpu.make_async_copy(
        tok_hbm.at[:, pl.ds(pl.multiple_of(at_ref[0] * cols, 128), cols)], tok, sem
    )
    get.start()
    total = own_ref[...] + a_ref[...].astype(F32) + b_ref[...].astype(F32) + c_ref[...].astype(F32)
    rounded = total.astype(BF16)
    out_ref[...] = rounded
    get.wait()
    sums[...] = tok[...].astype(F32) + rounded.astype(F32)
    for r in range(requests):
        for k in range(most):
            slot = acc_ref[r, k]
            row = sums[pl.ds(r * tree + jnp.maximum(slot, 0), 1), :]
            kept[r, pl.ds(k, 1), :] = jnp.where(slot >= 0, row, 0.0)
    rows_ref[...] = kept[...].astype(BF16)


def last_call(accepted, column, own, a, b, c, tokens):
    rows, cols = own.shape
    requests, most = accepted.shape
    return pl.pallas_call(
        last_kernel,
        in_specs=[SMEM, SMEM, VM, VM, VM, VM, ANY],
        out_specs=[VM, VM],
        out_shape=[
            jax.ShapeDtypeStruct((rows, cols), BF16),
            jax.ShapeDtypeStruct((requests, most, cols), BF16),
        ],
        scratch_shapes=[
            pltpu.VMEM((rows, cols), BF16),
            pltpu.VMEM((rows, cols), F32),
            pltpu.VMEM((requests, most, cols), F32),
            pltpu.SemaphoreType.DMA,
        ],
        compiler_params=params(8),
        name="last_sums",
    )(accepted, column, own, a, b, c, tokens)


def shards(
    tokens, norm_gain, w_query, w_key, w_value, w_out, prompt_keys, prompt_values, cache_keys,
    cache_values, cache_length, request_group, ancestors, accepted,
):
    requests, tree = ancestors.shape[:2]
    rows = tokens.shape[0]
    hd = prompt_keys.shape[3]
    n_tok = lax.axis_size("tok")
    n_mdl = lax.axis_size("mdl")
    n_y = 4
    n_x = n_mdl // 2
    tok = lax.axis_index("tok")
    mdl = lax.axis_index("mdl")

    def along_y(v, n):
        perm = [(t, t // n_y * n_y + (t + n) % n_y) for t in range(n_tok)]
        return lax.ppermute(v, "tok", perm)

    def along_z(v, n):
        return lax.ppermute(v, "tok", [(t, (t + n * n_y) % n_tok) for t in range(n_tok)])

    def along_x(v, n):
        return lax.ppermute(v, "mdl", [(m, (m + 2 * n) % n_mdl) for m in range(n_mdl)])

    def other_core(v):
        return lax.ppermute(v, "mdl", [(m, m ^ 1) for m in range(n_mdl)])

    tok_at = jnp.reshape(tok, (1,)).astype(jnp.int32)
    mdl_at = jnp.reshape(mdl, (1,)).astype(jnp.int32)

    squeeze = lambda v: v.reshape(v.shape[0], v.shape[1], v.shape[3])
    groups_n = prompt_keys.shape[0]
    kv = jnp.concatenate([squeeze(prompt_keys), squeeze(prompt_values)], axis=0)
    kv_r = along_y(kv, 1)
    kv_l = along_y(kv, -1)

    exponent = np.arange(hd // 2, dtype=np.float64) * (2.0 / hd)
    inverse = jnp.asarray(np.tile(THETA**-exponent, 2)[None, :], dtype=F32)
    table = ancestors.reshape(rows, tree)
    q, normed, cosine, sine = query_call(
        cache_length, tokens, norm_gain[None, :], w_query, table, inverse
    )
    shifts = (2, 1, -1)
    q_far = [along_z(q, n) for n in shifts]
    own = tree_call(normed, w_key, w_value, cosine, sine, q, table)

    k_o = along_y(kv_r[:groups_n], 1)
    v_o = along_y(kv_l[groups_n:], -1)
    prompts = (kv, kv_r, kv_l, k_o, v_o)

    w_mine, w_send = columns_call(mdl_at, w_out, n_x)
    w_other = other_core(w_send)

    back = []
    for n, qf in zip(shifts, q_far):
        part = remote_call(request_group, tok_at, qf, prompts, requests, n * n_y, n_tok)
        back.append(along_z(part, -n))
    home = home_call(
        request_group, tok_at, cache_length, q, prompts, own, squeeze(cache_keys),
        squeeze(cache_values),
    )
    attended = merge_call(home, *back, requests, rows)

    attended_other = other_core(attended)
    sent = []
    for group in ((2,), (1, -1), (0,)):
        outs = out_call(
            mdl_at, attended, attended_other, w_mine, w_other, [n % n_x for n in group],
            F32 if group == (0,) else BF16,
        )
        sent += [along_x(o, n) if n else o for o, n in zip(outs, group)]
    far, up, down, own_sum = sent
    return tuple(last_call(accepted, mdl_at, own_sum, far, up, down, tokens))


def solution(mesh):
    placed = (
        P("tok", None),
        P(),
        P(None, "mdl"),
        P(None, "mdl"),
        P(None, "mdl"),
        P("mdl", None),
        P(None, "tok", "mdl", None),
        P(None, "tok", "mdl", None),
        P("tok", None, "mdl", None),
        P("tok", None, "mdl", None),
        P("tok"),
        P(),
        P("tok", None, None),
        P("tok", None),
    )

    return jax.shard_map(
        shards,
        mesh=mesh,
        in_specs=placed,
        out_specs=(P("tok", "mdl"), P("tok", None, "mdl")),
        check_vma=False,
    )
```

profile of v0, /device:TPU:0, one launch (start us, length us, event | category | flops | bytes accessed | tf_op | source)
XLA Modules:
  0.0 101.8 jit_solution(12498195846660872057)
XLA Ops:
  0.6 2.5 %copy-done.8 = bf16[512,5120]{1,0:T(8,128)(2,1)S(1)} copy-done((bf16[512,5120]{1,0:T(8,128)(2,1)S(1)}, bf16[512,5120]{1,0:T(8,128)(2,1)}, u32[]{:S(2)}) %copy-start.8) | copy-done | bytes 5242904
  3.2 2.3 %out_columns.1 = (bf16[4,512,640]{2,1,0:T(8,128)(2,1)S(1)}, bf16[4,512,640]{2,1,0:T(8,128)(2,1)}) custom-call(s32[1]{0:T(128)} %bitcast.mdl_ref.refs_0_.at_ref, bf16[512,5120]{1,0:T(8,128)(2,1)S(1)} %copy-done.8), custom_call_target="tpu_custom_call" | custom-call | tf_op jit(solution)/shard_map/out_columns/pallas_call | solution.py:336
  5.7 3.2 %collective-permute-start.1 = (bf16[12,256,128]{2,1,0:T(8,128)(2,1)S(1)}, bf16[12,256,128]{2,1,0:T(8,128)(2,1)S(1)}, u32[]{:S(2)}, u32[]{:S(2)}) collective-permute-start(bf16[12,256,128]{2,1,0:T(8,128)(2,1)S(1)} %pad_maximum_fusion.kv.refs_3_), channel_id=1, source_target_pairs={{0,24},{8,0},{16,8},{24,16},{32,56},{40,32},{48,40},{56,48},{64,88... | collective-permute-start | bytes 2359304 | tf_op jit(solution)/shard_map/ppermute | solution.py:424
  9.0 2.5 %copy-done.9 = bf16[5120,512]{1,0:T(8,128)(2,1)S(1)} copy-done((bf16[5120,512]{1,0:T(8,128)(2,1)S(1)}, bf16[5120,512]{1,0:T(8,128)(2,1)}, u32[]{:S(2)}) %copy-start.9) | copy-done | bytes 5242904
  11.5 6.0 %query_proj.1 = (bf16[1024,128]{1,0:T(8,128)(2,1)}, bf16[256,5120]{1,0:T(8,128)(2,1)S(1)}, f32[256,128]{1,0:T(8,128)S(1)}, f32[256,128]{1,0:T(8,128)S(1)}) custom-call(s32[8]{0:T(128)S(1)} %copy-done.25, bf16[256,5120]{1,0:T(8,128)(2,1)S(1)} %copy-done.6, bf16[1,5120]{1,0:T(2,128)(2,1)S(1)} %broadcast_in_dim.3.gain_ref, bf16[5120,512]{1,0:T(8,128)(2,1)S(1)} %copy-done.9, ...), custom_call_target="tpu_custom_call" | custom-call | tf_op jit(solution)/shard_map/query_proj/pallas_call | solution.py:100
  20.2 3.9 %collective-permute-start.4 = (bf16[1024,128]{1,0:T(8,128)(2,1)}, bf16[1024,128]{1,0:T(8,128)(2,1)S(1)}, u32[]{:S(2)}, u32[]{:S(2)}) collective-permute-start(bf16[1024,128]{1,0:T(8,128)(2,1)} %get-tuple-element.10.q_ref), channel_id=1, source_target_pairs={{0,64},{8,72},{16,80},{24,88},{32,96},{40,104},{48,112},{56,120},{... | collective-permute-start | bytes 786440 | tf_op jit(solution)/shard_map/ppermute | solution.py:427
  24.1 2.2 %collective-permute-done.1.kv_l.refs_5_ = bf16[12,256,128]{2,1,0:T(8,128)(2,1)S(1)} collective-permute-done((bf16[12,256,128]{2,1,0:T(8,128)(2,1)S(1)}, bf16[12,256,128]{2,1,0:T(8,128)(2,1)S(1)}, u32[]{:S(2)}, u32[]{:S(2)}) %collective-permute-start.1) | collective-permute-done | bytes 786464 | tf_op jit(solution)/shard_map/ppermute | solution.py:424
  27.2 3.7 %collective-permute-start.3 = (bf16[6,256,128]{2,1,0:T(8,128)(2,1)}, bf16[6,256,128]{2,1,0:T(8,128)(2,1)}, u32[]{:S(2)}, u32[]{:S(2)}) collective-permute-start(bf16[6,256,128]{2,1,0:T(8,128)(2,1)} %slice.9), channel_id=1, source_target_pairs={{0,24},{8,0},{16,8},{24,16},{32,56},{40,32},{48,40},{56,48},{64,88... | collective-permute-start | bytes 1179656 | tf_op jit(solution)/shard_map/ppermute | solution.py:424
  31.9 1.9 %collective-permute-start.6 = (bf16[1024,128]{1,0:T(8,128)(2,1)}, bf16[1024,128]{1,0:T(8,128)(2,1)}, u32[]{:S(2)}, u32[]{:S(2)}) collective-permute-start(bf16[1024,128]{1,0:T(8,128)(2,1)} %get-tuple-element.10.q_ref), channel_id=1, source_target_pairs={{0,32},{8,40},{16,48},{24,56},{32,64},{40,72},{48,80},{56,88},{64,... | collective-permute-start | bytes 786440 | tf_op jit(solution)/shard_map/ppermute | solution.py:427
  34.5 2.1 %collective-permute-start.8 = (bf16[1024,128]{1,0:T(8,128)(2,1)}, bf16[1024,128]{1,0:T(8,128)(2,1)}, u32[]{:S(2)}, u32[]{:S(2)}) collective-permute-start(bf16[1024,128]{1,0:T(8,128)(2,1)} %get-tuple-element.10.q_ref), channel_id=1, source_target_pairs={{0,96},{8,104},{16,112},{24,120},{32,0},{40,8},{48,16},{56,24},{64... | collective-permute-start | bytes 786440 | tf_op jit(solution)/shard_map/ppermute | solution.py:427
  36.6 2.7 %collective-permute-done.3.v_o.refs_7_ = bf16[6,256,128]{2,1,0:T(8,128)(2,1)} collective-permute-done((bf16[6,256,128]{2,1,0:T(8,128)(2,1)}, bf16[6,256,128]{2,1,0:T(8,128)(2,1)}, u32[]{:S(2)}, u32[]{:S(2)}) %collective-permute-start.3) | collective-permute-done | bytes 393248 | tf_op jit(solution)/shard_map/ppermute | solution.py:424
  39.3 4.4 %collective-permute-done.2.k_o.refs_6_ = bf16[6,256,128]{2,1,0:T(8,128)(2,1)} collective-permute-done((bf16[6,256,128]{2,1,0:T(8,128)(2,1)}, bf16[6,256,128]{2,1,0:T(8,128)(2,1)}, u32[]{:S(2)}, u32[]{:S(2)}) %collective-permute-start.2) | collective-permute-done | bytes 393248 | tf_op jit(solution)/shard_map/ppermute | solution.py:424
  47.0 2.6 %prompt_remote.3 = bf16[1040,128]{1,0:T(8,128)(2,1)S(1)} custom-call(s32[128]{0:T(128)S(1)} %copy-done.23, s32[1]{0:T(128)} %bitcast.1.at_ref.refs_1_, bf16[1024,128]{1,0:T(8,128)(2,1)S(1)} %copy-done.18, bf16[12,256,128]{2,1,0:T(8,128)(2,1)S(1)} %pad_maximum_fusion.kv.refs_3_, bf16[12,256,128]{2,1,0:T(8,128)(2,1)S(1)} %copy-done.4, ...), custom_call_target="tpu_custom_call" | custom-call | tf_op jit(solution)/shard_map/prompt_remote/pallas_call | solution.py:205
  49.6 4.0 %collective-permute-start.5 = (bf16[1040,128]{1,0:T(8,128)(2,1)S(1)}, bf16[1040,128]{1,0:T(8,128)(2,1)S(1)}, u32[]{:S(2)}, u32[]{:S(2)}) collective-permute-start(bf16[1040,128]{1,0:T(8,128)(2,1)S(1)} %prompt_remote.3), channel_id=1, source_target_pairs={{0,64},{8,72},{16,80},{24,88},{32,96},{40,104},{48,112},{56,120},{... | collective-permute-start | bytes 798728 | tf_op jit(solution)/shard_map/ppermute | solution.py:427
  53.5 2.7 %prompt_remote.4 = bf16[1040,128]{1,0:T(8,128)(2,1)S(1)} custom-call(s32[128]{0:T(128)S(1)} %copy-done.23, s32[1]{0:T(128)} %bitcast.1.at_ref.refs_1_, bf16[1024,128]{1,0:T(8,128)(2,1)} %collective-permute-done.6.refs_2_, bf16[12,256,128]{2,1,0:T(8,128)(2,1)S(1)} %pad_maximum_fusion.kv.refs_3_, bf16[12,256,128]{2,1,0:T(8,128)(2,1)S(1)} %copy-done.4, ...), custom_call_target="tpu_custom_call" | custom-call | tf_op jit(solution)/shard_map/prompt_remote/pallas_call | solution.py:205
  57.1 2.7 %prompt_remote.5 = bf16[1040,128]{1,0:T(8,128)(2,1)S(1)} custom-call(s32[128]{0:T(128)S(1)} %copy-done.23, s32[1]{0:T(128)} %bitcast.1.at_ref.refs_1_, bf16[1024,128]{1,0:T(8,128)(2,1)} %collective-permute-done.8.refs_2_, bf16[12,256,128]{2,1,0:T(8,128)(2,1)S(1)} %pad_maximum_fusion.kv.refs_3_, bf16[12,256,128]{2,1,0:T(8,128)(2,1)S(1)} %copy-done.4, ...), custom_call_target="tpu_custom_call" | custom-call | tf_op jit(solution)/shard_map/prompt_remote/pallas_call | solution.py:205
  61.5 4.8 %tree_attention.1.own_ref = f32[1024,256]{1,0:T(8,128)S(1)} custom-call(bf16[256,5120]{1,0:T(8,128)(2,1)S(1)} %copy-done.13, bf16[5120,128]{1,0:T(8,128)(2,1)S(1)} %copy-done.14, bf16[5120,128]{1,0:T(8,128)(2,1)S(1)} %copy-done.15, f32[256,128]{1,0:T(8,128)S(1)} %copy-done.20, f32[256,128]{1,0:T(8,128)S(1)} %copy-done.22, ...), custom_call_target="tpu_custom_call" | custom-call | tf_op jit(solution)/shard_map/tree_attention/pallas_call | solution.py:154
  66.3 10.9 %home_attention.1.refs_0_ = f32[1024,256]{1,0:T(8,128)S(1)} custom-call(s32[128]{0:T(128)S(1)} %copy-done.23, s32[1]{0:T(128)} %bitcast.1.at_ref.refs_1_, s32[8]{0:T(128)S(1)} %copy-done.25, bf16[1024,128]{1,0:T(8,128)(2,1)} %get-tuple-element.10.q_ref, bf16[12,256,128]{2,1,0:T(8,128)(2,1)S(1)} %pad_maximum_fusion.kv.refs_3_, ...), custom_call_target="tpu_custom_call" | custom-call | tf_op jit(solution)/shard_map/home_attention/pallas_call | solution.py:266
  79.1 2.3 %out_proj.4 = bf16[256,640]{1,0:T(8,128)(2,1)S(1)} custom-call(s32[1]{0:T(128)} %bitcast.mdl_ref.refs_0_.at_ref, bf16[256,512]{1,0:T(8,128)(2,1)S(1)} %merge.1.refs_1_, bf16[256,512]{1,0:T(8,128)(2,1)S(1)} %collective-permute-done.10.refs_2_, bf16[4,512,640]{2,1,0:T(8,128)(2,1)S(1)} %get-tuple-element.14.refs_3_, ...), custom_call_target="tpu_custom_call" | custom-call | tf_op jit(solution)/shard_map/out_proj/pallas_call | solution.py:355
  81.4 3.1 %collective-permute-start.12 = (bf16[256,640]{1,0:T(8,128)(2,1)S(1)}, bf16[256,640]{1,0:T(8,128)(2,1)S(1)}, u32[]{:S(2)}, u32[]{:S(2)}) collective-permute-start(bf16[256,640]{1,0:T(8,128)(2,1)S(1)} %out_proj.4), channel_id=1, source_target_pairs={{0,4},{1,5},{2,6},{3,7},{4,0},{5,1},{6,2},{7,3},{8,12},{9,13},{10,... | collective-permute-start | bytes 983048 | tf_op jit(solution)/shard_map/ppermute | solution.py:430
  84.5 2.7 %out_proj.5 = (bf16[256,640]{1,0:T(8,128)(2,1)S(1)}, bf16[256,640]{1,0:T(8,128)(2,1)S(1)}) custom-call(s32[1]{0:T(128)} %bitcast.mdl_ref.refs_0_.at_ref, bf16[256,512]{1,0:T(8,128)(2,1)S(1)} %merge.1.refs_1_, bf16[256,512]{1,0:T(8,128)(2,1)S(1)} %collective-permute-done.10.refs_2_, bf16[4,512,640]{2,1,0:T(8,128)(2,1)S(1)} %get-tuple-element.14.refs_3_, ...), custom_call_target="tpu_custom_call" | custom-call | tf_op jit(solution)/shard_map/out_proj/pallas_call | solution.py:355
  87.9 2.6 %collective-permute-start.14 = (bf16[256,640]{1,0:T(8,128)(2,1)S(1)}, bf16[256,640]{1,0:T(8,128)(2,1)S(1)}, u32[]{:S(2)}, u32[]{:S(2)}) collective-permute-start(bf16[256,640]{1,0:T(8,128)(2,1)S(1)} %get-tuple-element.17), channel_id=1, source_target_pairs={{0,6},{1,7},{2,0},{3,1},{4,2},{5,3},{6,4},{7,5},{8,14},{9,15},{10,... | collective-permute-start | bytes 983048 | tf_op jit(solution)/shard_map/ppermute | solution.py:430
  90.5 2.3 %out_proj.3.own_ref = f32[256,640]{1,0:T(8,128)S(1)} custom-call(s32[1]{0:T(128)} %bitcast.mdl_ref.refs_0_.at_ref, bf16[256,512]{1,0:T(8,128)(2,1)S(1)} %merge.1.refs_1_, bf16[256,512]{1,0:T(8,128)(2,1)S(1)} %collective-permute-done.10.refs_2_, bf16[4,512,640]{2,1,0:T(8,128)(2,1)S(1)} %get-tuple-element.14.refs_3_, ...), custom_call_target="tpu_custom_call" | custom-call | tf_op jit(solution)/shard_map/out_proj/pallas_call | solution.py:355
  93.6 6.2 %collective-permute-done.13.b_ref = bf16[256,640]{1,0:T(8,128)(2,1)S(1)} collective-permute-done((bf16[256,640]{1,0:T(8,128)(2,1)S(1)}, bf16[256,640]{1,0:T(8,128)(2,1)S(1)}, u32[]{:S(2)}, u32[]{:S(2)}) %collective-permute-start.13) | collective-permute-done | bytes 327712 | tf_op jit(solution)/shard_map/ppermute | solution.py:430
  (82 shorter events, 16.3 us)
Async XLA Ops:
  3.1 5.8 %copy-start.16 = (s32[8,32,32]{2,1,0:T(8,128)S(1)}, s32[8,32,32]{2,1,0:T(8,128)}, u32[]{:S(2)}) copy-start(s32[8,32,32]{2,1,0:T(8,128)} %param.27) | copy-start | bytes 98308
  3.1 5.8 %copy-start.25 = (s32[8]{0:T(128)S(1)}, s32[8]{0:T(128)}, u32[]{:S(2)}) copy-start(s32[8]{0:T(128)} %len_ref.3) | copy-start | bytes 100
  5.5 73.6 %collective-permute-start.11 = (bf16[4,512,640]{2,1,0:T(8,128)(2,1)}, bf16[4,512,640]{2,1,0:T(8,128)(2,1)}, u32[]{:S(2)}, u32[]{:S(2)}) collective-permute-start(bf16[4,512,640]{2,1,0:T(8,128)(2,1)} %get-tuple-element.15), channel_id=1, source_target_pairs={{0,1},{1,0},{2,3},{3,2},{4,5},{5,4},{6,7},{7,6},{8,9},{9,8},{10,11... | collective-permute-start | bytes 7864328 | tf_op jit(solution)/shard_map/ppermute | solution.py:433
  5.7 20.6 %collective-permute-start.1 = (bf16[12,256,128]{2,1,0:T(8,128)(2,1)S(1)}, bf16[12,256,128]{2,1,0:T(8,128)(2,1)S(1)}, u32[]{:S(2)}, u32[]{:S(2)}) collective-permute-start(bf16[12,256,128]{2,1,0:T(8,128)(2,1)S(1)} %pad_maximum_fusion.kv.refs_3_), channel_id=1, source_target_pairs={{0,24},{8,0},{16,8},{24,16},{32,56},{40,32},{48,40},{56,48},{64,88... | collective-permute-start | bytes 2359304 | tf_op jit(solution)/shard_map/ppermute | solution.py:424
  8.9 21.9 %collective-permute-start = (bf16[12,256,128]{2,1,0:T(8,128)(2,1)S(1)}, bf16[12,256,128]{2,1,0:T(8,128)(2,1)S(1)}, u32[]{:S(2)}, u32[]{:S(2)}) collective-permute-start(bf16[12,256,128]{2,1,0:T(8,128)(2,1)S(1)} %pad_maximum_fusion.kv.refs_3_), channel_id=1, source_target_pairs={{0,8},{8,16},{16,24},{24,0},{32,40},{40,48},{48,56},{56,32},{64,72... | collective-permute-start | bytes 2359304 | tf_op jit(solution)/shard_map/ppermute | solution.py:424
  11.5 32.3 %copy-start.23 = (s32[128]{0:T(128)S(1)}, s32[128]{0:T(128)}, u32[]{:S(2)}) copy-start(s32[128]{0:T(128)} %refs_0_.5) | copy-start | bytes 1540
  20.2 13.6 %collective-permute-start.4 = (bf16[1024,128]{1,0:T(8,128)(2,1)}, bf16[1024,128]{1,0:T(8,128)(2,1)S(1)}, u32[]{:S(2)}, u32[]{:S(2)}) collective-permute-start(bf16[1024,128]{1,0:T(8,128)(2,1)} %get-tuple-element.10.q_ref), channel_id=1, source_target_pairs={{0,64},{8,72},{16,80},{24,88},{32,96},{40,104},{48,112},{56,120},{... | collective-permute-start | bytes 786440 | tf_op jit(solution)/shard_map/ppermute | solution.py:427
  27.2 12.2 %collective-permute-start.3 = (bf16[6,256,128]{2,1,0:T(8,128)(2,1)}, bf16[6,256,128]{2,1,0:T(8,128)(2,1)}, u32[]{:S(2)}, u32[]{:S(2)}) collective-permute-start(bf16[6,256,128]{2,1,0:T(8,128)(2,1)} %slice.9), channel_id=1, source_target_pairs={{0,24},{8,0},{16,8},{24,16},{32,56},{40,32},{48,40},{56,48},{64,88... | collective-permute-start | bytes 1179656 | tf_op jit(solution)/shard_map/ppermute | solution.py:424
  31.9 11.9 %collective-permute-start.2 = (bf16[6,256,128]{2,1,0:T(8,128)(2,1)}, bf16[6,256,128]{2,1,0:T(8,128)(2,1)}, u32[]{:S(2)}, u32[]{:S(2)}) collective-permute-start(bf16[6,256,128]{2,1,0:T(8,128)(2,1)} %slice.8), channel_id=1, source_target_pairs={{0,8},{8,16},{16,24},{24,0},{32,40},{40,48},{48,56},{56,32},{64,72... | collective-permute-start | bytes 1179656 | tf_op jit(solution)/shard_map/ppermute | solution.py:424
  31.9 21.7 %collective-permute-start.6 = (bf16[1024,128]{1,0:T(8,128)(2,1)}, bf16[1024,128]{1,0:T(8,128)(2,1)}, u32[]{:S(2)}, u32[]{:S(2)}) collective-permute-start(bf16[1024,128]{1,0:T(8,128)(2,1)} %get-tuple-element.10.q_ref), channel_id=1, source_target_pairs={{0,32},{8,40},{16,48},{24,56},{32,64},{40,72},{48,80},{56,88},{64,... | collective-permute-start | bytes 786440 | tf_op jit(solution)/shard_map/ppermute | solution.py:427
  34.5 22.6 %collective-permute-start.8 = (bf16[1024,128]{1,0:T(8,128)(2,1)}, bf16[1024,128]{1,0:T(8,128)(2,1)}, u32[]{:S(2)}, u32[]{:S(2)}) collective-permute-start(bf16[1024,128]{1,0:T(8,128)(2,1)} %get-tuple-element.10.q_ref), channel_id=1, source_target_pairs={{0,96},{8,104},{16,112},{24,120},{32,0},{40,8},{48,16},{56,24},{64... | collective-permute-start | bytes 786440 | tf_op jit(solution)/shard_map/ppermute | solution.py:427
  47.0 14.4 %copy-start.15 = (bf16[5120,128]{1,0:T(8,128)(2,1)S(1)}, bf16[5120,128]{1,0:T(8,128)(2,1)}, u32[]{:S(2)}) copy-start(bf16[5120,128]{1,0:T(8,128)(2,1)} %wv_hbm.1) | copy-start | bytes 3932164
  49.6 27.6 %collective-permute-start.5 = (bf16[1040,128]{1,0:T(8,128)(2,1)S(1)}, bf16[1040,128]{1,0:T(8,128)(2,1)S(1)}, u32[]{:S(2)}, u32[]{:S(2)}) collective-permute-start(bf16[1040,128]{1,0:T(8,128)(2,1)S(1)} %prompt_remote.3), channel_id=1, source_target_pairs={{0,64},{8,72},{16,80},{24,88},{32,96},{40,104},{48,112},{56,120},{... | collective-permute-start | bytes 798728 | tf_op jit(solution)/shard_map/ppermute | solution.py:427
  53.5 7.9 %copy-start.13 = (bf16[256,5120]{1,0:T(8,128)(2,1)S(1)}, bf16[256,5120]{1,0:T(8,128)(2,1)}, u32[]{:S(2)}) copy-start(bf16[256,5120]{1,0:T(8,128)(2,1)} %copy-done.12) | copy-start | bytes 7864324
  53.5 7.9 %copy-start.14 = (bf16[5120,128]{1,0:T(8,128)(2,1)S(1)}, bf16[5120,128]{1,0:T(8,128)(2,1)}, u32[]{:S(2)}) copy-start(bf16[5120,128]{1,0:T(8,128)(2,1)} %wk_hbm.1) | copy-start | bytes 3932164
  56.3 20.9 %collective-permute-start.7 = (bf16[1040,128]{1,0:T(8,128)(2,1)S(1)}, bf16[1040,128]{1,0:T(8,128)(2,1)S(1)}, u32[]{:S(2)}, u32[]{:S(2)}) collective-permute-start(bf16[1040,128]{1,0:T(8,128)(2,1)S(1)} %prompt_remote.4), channel_id=1, source_target_pairs={{0,96},{8,104},{16,112},{24,120},{32,0},{40,8},{48,16},{56,24},{64... | collective-permute-start | bytes 798728 | tf_op jit(solution)/shard_map/ppermute | solution.py:427
  57.1 9.1 %copy-start.11 = (bf16[8,2048,1,128]{3,1,2,0:T(8,128)(2,1)S(1)}, bf16[8,2048,1,128]{3,1,2,0:T(8,128)(2,1)}, u32[]{:S(2)}) copy-start(bf16[8,2048,1,128]{3,1,2,0:T(8,128)(2,1)} %param.24) | copy-start | bytes 12582916
  59.8 17.4 %collective-permute-start.9 = (bf16[1040,128]{1,0:T(8,128)(2,1)S(1)}, bf16[1040,128]{1,0:T(8,128)(2,1)S(1)}, u32[]{:S(2)}, u32[]{:S(2)}) collective-permute-start(bf16[1040,128]{1,0:T(8,128)(2,1)S(1)} %prompt_remote.5), channel_id=1, source_target_pairs={{0,32},{8,40},{16,48},{24,56},{32,64},{40,72},{48,80},{56,88},{64,... | collective-permute-start | bytes 798728 | tf_op jit(solution)/shard_map/ppermute | solution.py:427
  77.5 1.6 %collective-permute-start.10 = (bf16[256,512]{1,0:T(8,128)(2,1)S(1)}, bf16[256,512]{1,0:T(8,128)(2,1)S(1)}, u32[]{:S(2)}, u32[]{:S(2)}) collective-permute-start(bf16[256,512]{1,0:T(8,128)(2,1)S(1)} %merge.1.refs_1_), channel_id=1, source_target_pairs={{0,1},{1,0},{2,3},{3,2},{4,5},{5,4},{6,7},{7,6},{8,9},{9,8},{10,11... | collective-permute-start | bytes 786440 | tf_op jit(solution)/shard_map/ppermute | solution.py:433
  81.4 12.2 %collective-permute-start.12 = (bf16[256,640]{1,0:T(8,128)(2,1)S(1)}, bf16[256,640]{1,0:T(8,128)(2,1)S(1)}, u32[]{:S(2)}, u32[]{:S(2)}) collective-permute-start(bf16[256,640]{1,0:T(8,128)(2,1)S(1)} %out_proj.4), channel_id=1, source_target_pairs={{0,4},{1,5},{2,6},{3,7},{4,0},{5,1},{6,2},{7,3},{8,12},{9,13},{10,... | collective-permute-start | bytes 983048 | tf_op jit(solution)/shard_map/ppermute | solution.py:430
  87.2 12.5 %collective-permute-start.13 = (bf16[256,640]{1,0:T(8,128)(2,1)S(1)}, bf16[256,640]{1,0:T(8,128)(2,1)S(1)}, u32[]{:S(2)}, u32[]{:S(2)}) collective-permute-start(bf16[256,640]{1,0:T(8,128)(2,1)S(1)} %get-tuple-element.16), channel_id=1, source_target_pairs={{0,2},{1,3},{2,4},{3,5},{4,6},{5,7},{6,0},{7,1},{8,10},{9,11},{10,... | collective-permute-start | bytes 983048 | tf_op jit(solution)/shard_map/ppermute | solution.py:430
  87.9 11.9 %copy-start.7 = (bf16[256,5120]{1,0:T(8,128)(2,1)S(1)}, bf16[256,5120]{1,0:T(8,128)(2,1)}, u32[]{:S(2)}) copy-start(bf16[256,5120]{1,0:T(8,128)(2,1)} %tok_hbm.3) | copy-start | bytes 7864324
  87.9 11.9 %copy-start.24 = (s32[8,8]{1,0:T(8,128)S(1)}, s32[8,8]{1,0:T(8,128)}, u32[]{:S(2)}) copy-start(s32[8,8]{1,0:T(8,128)} %acc_ref.1) | copy-start | bytes 772
  87.9 11.9 %collective-permute-start.14 = (bf16[256,640]{1,0:T(8,128)(2,1)S(1)}, bf16[256,640]{1,0:T(8,128)(2,1)S(1)}, u32[]{:S(2)}, u32[]{:S(2)}) collective-permute-start(bf16[256,640]{1,0:T(8,128)(2,1)S(1)} %get-tuple-element.17), channel_id=1, source_target_pairs={{0,6},{1,7},{2,0},{3,1},{4,2},{5,3},{6,4},{7,5},{8,14},{9,15},{10,... | collective-permute-start | bytes 983048 | tf_op jit(solution)/shard_map/ppermute | solution.py:430
  (21 other events, 64.2 us)
where the time goes:
time: 103 us; the launch traced here: 102 us
  Pallas kernels  41.5 us (40%)
  starting transfers between devices  27.7 us (27%)
  waiting for transfers between devices  17.9 us (17%)
  local copies, waits for them, and re-layouts  13.6 us (13%)
  between operations  1.13 us (1%)
    ppermute x6, starting transfers between devices, along_z(): lax.ppermute(v, 'tok', [(t, (t + n * n_y) % n_tok) for t in range(n_tok)])  14.2 us
    unnamed x60, local copies, waits for them, and re-layouts  11.9 us
    pallas_call x1, Pallas kernels, home_call(): pl.pallas_call(home_kernel, in_specs=[SMEM, SMEM, SMEM] + [VM] * 7 + [ANY...  10.9 us
    ppermute x4, waiting for transfers between devices, along_y(): return lax.ppermute(v, 'tok', perm)  9.36 us
    pallas_call x3, Pallas kernels, remote_call(): pl.pallas_call(lambda *refs: remote_kernel(*refs, requests=requests, shif...  8.09 us
    pallas_call x3, Pallas kernels, out_call(): pl.pallas_call(lambda *refs: out_kernel(*refs, shifts=shifts), in_specs=[...  7.36 us
    ppermute x3, waiting for transfers between devices, along_x(): lax.ppermute(v, 'mdl', [(m, (m + 2 * n) % n_mdl) for m in range(n_mdl)])  6.98 us
    ppermute x4, starting transfers between devices, along_y(): return lax.ppermute(v, 'tok', perm)  6.89 us
  transfers between devices with their start and end apart: 15, of which 7 were waited for; matrix products, arithmetic and copies ran while one was open for 2% of the time, Pallas kernels for 34%

commit v1 on v0

v1 whole, which is shorter than its diff:
```python
import math

import jax
import jax.numpy as jnp
import numpy as np
from jax import lax
from jax.experimental import pallas as pl
from jax.experimental.pallas import tpu as pltpu
from jax.sharding import PartitionSpec as P


PROMPT = 4096
THETA = 100000000.0
EPS = 1e-05

F32 = jnp.float32
BF16 = jnp.bfloat16

HBM = pl.BlockSpec(memory_space=pltpu.HBM)
SMEM = pl.BlockSpec(memory_space=pltpu.SMEM)
VM = pl.BlockSpec(memory_space=pltpu.VMEM)
CHUNKS = 5
KB = 256
PIECES = 2
LANES = 8
NT = (((1,), (1,)), ((), ()))


def params(mib):
    return pltpu.CompilerParams(vmem_limit_bytes=mib * 1024 * 1024)


def dot(a, b):
    return jnp.dot(a, b, preferred_element_type=F32)


def dot_nt(a, b):
    return lax.dot_general(a, b, NT, preferred_element_type=F32)


def rotate(x, cosine, sine):
    return x * cosine + pltpu.roll(x, x.shape[1] // 2, 1) * sine


def query_kernel(
    len_hbm, tok_hbm, gain_hbm, wq_hbm, anc_hbm, inv_hbm, q_ref, normed_hbm, turn_hbm,
    lengths, tok, gain, wq, table, inverse, normed_ref, turn, sems, wsems, osems,
):
    rows, width = tok.shape
    requests = lengths.shape[0]
    tree = rows // requests
    firsts = [
        pltpu.make_async_copy(source, target, sems.at[i])
        for i, (source, target) in enumerate(
            ((anc_hbm, table), (len_hbm, lengths), (inv_hbm, inverse), (gain_hbm, gain), (tok_hbm, tok))
        )
    ]
    for c in firsts:
        c.start()
    part = width // CHUNKS
    copies = []
    for i in range(CHUNKS):
        at = pl.ds(i * part, part)
        c = pltpu.make_async_copy(wq_hbm.at[at], wq.at[at], wsems.at[i])
        c.start()
        copies.append(c)
    for c in firsts[:3]:
        c.wait()
    depth = jnp.sum(table[...], axis=1, keepdims=True).astype(F32) - 1.0
    places = jnp.concatenate(
        [
            depth[r * tree : (r + 1) * tree] + (PROMPT + lengths[r]).astype(F32)
            for r in range(requests)
        ],
        axis=0,
    )
    angles = places * inverse[...]
    lane = lax.broadcasted_iota(jnp.int32, angles.shape, 1)
    cosine = jnp.cos(angles)
    sine = jnp.sin(angles)
    sine = jnp.where(lane < angles.shape[1] // 2, -sine, sine)
    turn[0] = cosine
    turn[1] = sine
    put_turn = pltpu.make_async_copy(turn, turn_hbm, osems.at[0])
    put_turn.start()
    for c in firsts[3:]:
        c.wait()
    gains = gain[...].astype(F32)
    gains = jnp.concatenate([gains[i : i + 1] for i in range(gain.shape[0])], axis=1)

    def norm(i, _):
        at = pl.ds(pl.multiple_of(i * 32, 32), 32)
        wide = tok[at, :].astype(F32)
        scale = lax.rsqrt(jnp.mean(wide * wide, axis=1, keepdims=True) + EPS)
        normed_ref[at, :] = (wide * scale * gains).astype(BF16)
        return 0

    lax.fori_loop(0, rows // 32, norm, 0)
    put_normed = pltpu.make_async_copy(normed_ref, normed_hbm, osems.at[1])
    put_normed.start()
    acc = None
    for i in range(CHUNKS):
        copies[i].wait()
        d = dot(normed_ref[:, i * part : (i + 1) * part], wq[i * part : (i + 1) * part, :])
        acc = d if acc is None else acc + d
    hd = inverse.shape[1]
    heads = acc.shape[1] // hd
    fold = hd**-0.5 * math.log2(math.e)
    for g in range(heads):
        turned = (rotate(acc[:, g * hd : (g + 1) * hd], cosine, sine) * fold).astype(BF16)
        for r in range(requests):
            q_ref[pl.ds((r * heads + g) * tree, tree), :] = turned[r * tree : (r + 1) * tree]
    put_turn.wait()
    put_normed.wait()


def query_call(lengths, tokens, gain, w_query, ancestors, inverse):
    rows, width = tokens.shape
    hd = inverse.shape[1]
    heads = w_query.shape[1] // hd
    return pl.pallas_call(
        query_kernel,
        in_specs=[HBM] * 6,
        out_specs=[VM, HBM, HBM],
        out_shape=[
            jax.ShapeDtypeStruct((rows * heads, hd), BF16),
            pltpu.HBM((rows, width), BF16),
            pltpu.HBM((2, rows, hd), F32),
        ],
        scratch_shapes=[
            pltpu.SMEM(lengths.shape, jnp.int32),
            pltpu.VMEM((rows, width), BF16),
            pltpu.VMEM(gain.shape, BF16),
            pltpu.VMEM(w_query.shape, BF16),
            pltpu.VMEM(ancestors.shape, jnp.int32),
            pltpu.VMEM(inverse.shape, F32),
            pltpu.VMEM((rows, width), BF16),
            pltpu.VMEM((2, rows, hd), F32),
            pltpu.SemaphoreType.DMA((5,)),
            pltpu.SemaphoreType.DMA((CHUNKS,)),
            pltpu.SemaphoreType.DMA((2,)),
        ],
        compiler_params=params(24),
        name="query_proj",
    )(lengths, tokens, gain, w_query, ancestors, inverse)


def tree_kernel(
    normed_hbm, wk_hbm, wv_hbm, turn_hbm, q_ref, anc_hbm, out_hbm,
    normed_ref, w, turn, anc_ref, out_ref, sems, osems,
):
    rows, tree = anc_ref.shape
    hd = q_ref.shape[1]
    group = q_ref.shape[0] // rows
    qrows = group * tree
    part = w.shape[0] // CHUNKS
    copies = []
    for i in range(CHUNKS):
        at = pl.ds(i * part, part)
        three = (
            pltpu.make_async_copy(normed_hbm.at[:, at], normed_ref.at[:, at], sems.at[0, i]),
            pltpu.make_async_copy(wk_hbm.at[at], w.at[at, pl.ds(0, hd)], sems.at[1, i]),
            pltpu.make_async_copy(wv_hbm.at[at], w.at[at, pl.ds(hd, hd)], sems.at[2, i]),
        )
        for c in three:
            c.start()
        copies.append(three)
    get_turn = pltpu.make_async_copy(turn_hbm, turn, osems.at[rows // tree])
    get_anc = pltpu.make_async_copy(anc_hbm, anc_ref, osems.at[rows // tree + 1])
    get_turn.start()
    get_anc.start()
    both = None
    for i in range(CHUNKS):
        for c in copies[i]:
            c.wait()
        d = dot(normed_ref[:, i * part : (i + 1) * part], w[i * part : (i + 1) * part, :])
        both = d if both is None else both + d
    get_turn.wait()
    get_anc.wait()
    new_keys = rotate(both[:, :hd], turn[0], turn[1]).astype(BF16)
    new_values = both[:, hd:].astype(BF16)
    ones = jnp.ones((tree, hd), BF16)
    puts = []
    for r in range(rows // tree):
        at = slice(r * tree, (r + 1) * tree)
        here = pl.ds(r * qrows, qrows)
        scores = dot_nt(q_ref[here, :], new_keys[at])
        seen = jnp.concatenate([anc_ref[at, :]] * group, axis=0)
        weights = jnp.where(seen > 0, jnp.exp2(scores), 0.0).astype(BF16)
        out_ref[here, :] = dot(weights, jnp.concatenate([new_values[at], ones], axis=1))
        put = pltpu.make_async_copy(out_ref.at[here], out_hbm.at[here], osems.at[r])
        put.start()
        puts.append(put)
    for put in puts:
        put.wait()


def tree_call(normed, w_key, w_value, turn, q, ancestors):
    rows, tree = ancestors.shape
    hd = q.shape[1]
    return pl.pallas_call(
        tree_kernel,
        in_specs=[HBM, HBM, HBM, HBM, VM, HBM],
        out_specs=HBM,
        out_shape=pltpu.HBM((q.shape[0], 2 * hd), F32),
        scratch_shapes=[
            pltpu.VMEM(normed.shape, BF16),
            pltpu.VMEM((normed.shape[1], 2 * hd), BF16),
            pltpu.VMEM(turn.shape, F32),
            pltpu.VMEM(ancestors.shape, jnp.int32),
            pltpu.VMEM((q.shape[0], 2 * hd), F32),
            pltpu.SemaphoreType.DMA((3, CHUNKS)),
            pltpu.SemaphoreType.DMA((rows // tree + 2,)),
        ],
        compiler_params=params(16),
        name="tree_attention",
    )(normed, w_key, w_value, turn, q, ancestors)


def join_kernel(a_hbm, b_hbm, out_ref, sems):
    n = a_hbm.shape[0]
    copies = [
        pltpu.make_async_copy(ref, out_ref.at[pl.ds(i * n, n)], sems.at[i])
        for i, ref in enumerate((a_hbm, b_hbm))
    ]
    for c in copies:
        c.start()
    for c in copies:
        c.wait()


def join_call(a, b):
    return pl.pallas_call(
        join_kernel,
        in_specs=[HBM, HBM],
        out_specs=VM,
        out_shape=jax.ShapeDtypeStruct((2 * a.shape[0],) + a.shape[1:], a.dtype),
        scratch_shapes=[pltpu.SemaphoreType.DMA((2,))],
        compiler_params=params(4),
        name="join",
    )(a, b)


def halves_kernel(right_ref, left_ref, k_ref, v_ref):
    n = k_ref.shape[0]
    k_ref[...] = right_ref[pl.ds(0, n)]
    v_ref[...] = left_ref[pl.ds(n, n)]


def halves_call(right, left):
    half = jax.ShapeDtypeStruct((right.shape[0] // 2,) + right.shape[1:], right.dtype)
    return pl.pallas_call(
        halves_kernel,
        in_specs=[VM, VM],
        out_specs=[VM, VM],
        out_shape=[half, half],
        compiler_params=params(8),
        name="halves",
    )(right, left)


def prompt_sum(q, g, pieces, ones):
    weights, values = [], []
    for kref, koff, vref, voff in pieces:
        weights.append(jnp.exp2(dot_nt(q, kref[koff + g])).astype(BF16))
        values.append(jnp.concatenate([vref[voff + g], ones], axis=1))
    return dot(jnp.concatenate(weights, axis=1), jnp.concatenate(values, axis=0))


def near_pieces(kv, kv_r, kv_l):
    n = kv.shape[0] // 2
    return [(kv, 0, kv, n), (kv_r, 0, kv_r, n), (kv_l, 0, kv_l, n)]


def source_of(at_ref, requests, shift, n_tok):
    return lax.rem(at_ref[0] + n_tok - shift, n_tok) * requests


def near_kernel(group_ref, at_ref, kv, kv_r, kv_l, *refs, requests, shifts, n_tok):
    hd = kv.shape[2]
    qrows = refs[0].shape[0] // requests
    pieces = near_pieces(kv, kv_r, kv_l)
    ones = jnp.ones((kv.shape[1], hd), BF16)
    for shift, q_ref, out_ref in zip(shifts, refs[: len(shifts)], refs[len(shifts) :]):
        base = source_of(at_ref, requests, shift, n_tok)
        for r in range(requests):
            at = pl.ds(r * qrows, qrows)
            out_ref[at, :] = prompt_sum(q_ref[at, :], group_ref[base + r], pieces, ones)


def near_call(groups, at, qs, kv, kv_r, kv_l, requests, shifts, n_tok):
    rows, hd = qs[0].shape
    n = len(shifts)
    return pl.pallas_call(
        lambda *refs: near_kernel(*refs, requests=requests, shifts=shifts, n_tok=n_tok),
        in_specs=[SMEM, SMEM] + [VM] * (3 + n),
        out_specs=[VM] * n,
        out_shape=[jax.ShapeDtypeStruct((rows, 2 * hd), F32)] * n,
        compiler_params=params(16),
        name="prompt_near",
    )(groups, at, kv, kv_r, kv_l, *qs)


def far_kernel(group_ref, at_ref, k_o, v_o, *refs, requests, shifts, n_tok):
    hd = k_o.shape[2]
    n = len(shifts)
    ones = jnp.ones((k_o.shape[1], hd), BF16)
    for shift, q_ref, near_ref, out_ref in zip(shifts, refs[:n], refs[n : 2 * n], refs[2 * n :]):
        qrows = q_ref.shape[0] // requests
        diagonal = lax.broadcasted_iota(jnp.int32, (qrows, hd), 0) == lax.broadcasted_iota(
            jnp.int32, (qrows, hd), 1
        )
        base = source_of(at_ref, requests, shift, n_tok)
        totals = []
        for r in range(requests):
            at = pl.ds(r * qrows, qrows)
            acc = near_ref[at, :] + prompt_sum(
                q_ref[at, :], group_ref[base + r], [(k_o, 0, v_o, 0)], ones
            )
            out_ref[at, :] = acc[:, :hd].astype(BF16)
            totals.append(jnp.sum(jnp.where(diagonal, acc[:, hd:], 0.0), axis=0, keepdims=True))
        total = jnp.concatenate(totals, axis=0)
        high = total.astype(BF16)
        low = (total - high.astype(F32)).astype(BF16)
        out_ref[pl.ds(requests * qrows, 2 * requests), :] = jnp.concatenate([high, low], axis=0)


def far_call(groups, at, nears, qs, k_o, v_o, requests, shifts, n_tok):
    rows, hd = qs[0].shape
    n = len(shifts)
    return pl.pallas_call(
        lambda *refs: far_kernel(*refs, requests=requests, shifts=shifts, n_tok=n_tok),
        in_specs=[SMEM, SMEM] + [VM] * (2 + 2 * n),
        out_specs=[VM] * n,
        out_shape=[jax.ShapeDtypeStruct((rows + 2 * requests, hd), BF16)] * n,
        compiler_params=params(16),
        name="prompt_far",
    )(groups, at, k_o, v_o, *qs, *nears)


def home_kernel(
    group_ref, at_ref, len_ref, q_ref, kv, kv_r, kv_l, k_o, v_o, own_hbm, ck_hbm, cv_hbm, out_ref,
    own_ref, keys, values, where_ref, sems, own_sem,
):
    requests, slots, hd = keys.shape
    qrows = q_ref.shape[0] // requests
    piece = slots // PIECES

    def copies(r, i):
        at = pl.ds(i * piece, piece)
        return (
            pltpu.make_async_copy(ck_hbm.at[r, at], keys.at[r, at], sems.at[0, r, i]),
            pltpu.make_async_copy(cv_hbm.at[r, at], values.at[r, at], sems.at[1, r, i]),
        )

    def each_copy(act):
        for i in range(PIECES):
            for r in range(requests):
                if i == 0:
                    for c in copies(r, i):
                        act(c)
                else:

                    @pl.when(len_ref[r] > i * piece)
                    def _(r=r, i=i):
                        for c in copies(r, i):
                            act(c)

    get_own = pltpu.make_async_copy(own_hbm, own_ref, own_sem)
    get_own.start()
    each_copy(lambda c: c.start())
    count = 0
    for r in range(requests):

        def note(b, n, r=r):
            where_ref[0, n] = r
            where_ref[1, n] = b * KB
            return n + 1

        count = lax.fori_loop(0, (len_ref[r] + KB - 1) // KB, note, count)
    for j in range(LANES):
        where_ref[0, count + j] = requests - 1
        where_ref[1, count + j] = 0
    pieces = near_pieces(kv, kv_r, kv_l) + [(k_o, 0, v_o, 0)]
    ones = jnp.ones((KB, hd), BF16)
    get_own.wait()
    for r in range(requests):
        at = pl.ds(r * qrows, qrows)
        out_ref[at, :] = own_ref[at, :] + prompt_sum(
            q_ref[at, :], group_ref[at_ref[0] * requests + r], pieces, ones
        )
    column = lax.broadcasted_iota(jnp.int32, (qrows, KB), 1)
    each_copy(lambda c: c.wait())

    def step(i, _):
        parts = []
        for j in range(LANES):
            n = i * LANES + j
            r = where_ref[0, n]
            first = pl.multiple_of(where_ref[1, n], KB)
            at = pl.ds(pl.multiple_of(r * qrows, qrows), qrows)
            limit = jnp.where(n < count, len_ref[r] - first, 0)
            s = dot_nt(q_ref[at, :], keys[r, pl.ds(first, KB), :])
            p = jnp.where(column < limit, jnp.exp2(s), 0.0).astype(BF16)
            both = jnp.concatenate([values[r, pl.ds(first, KB), :], ones], axis=1)
            parts.append((at, dot(p, both)))
        for at, d in parts:
            out_ref[at, :] += d
        return 0

    lax.fori_loop(0, (count + LANES - 1) // LANES, step, 0)


def home_call(groups, at, lengths, q, prompts, own, cache_keys, cache_values):
    requests, slots, _ = cache_keys.shape
    return pl.pallas_call(
        home_kernel,
        in_specs=[SMEM, SMEM, SMEM] + [VM] * 6 + [HBM] * 3,
        out_specs=VM,
        out_shape=jax.ShapeDtypeStruct(own.shape, F32),
        scratch_shapes=[
            pltpu.VMEM(own.shape, F32),
            pltpu.VMEM(cache_keys.shape, BF16),
            pltpu.VMEM(cache_values.shape, BF16),
            pltpu.SMEM((2, requests * slots // KB + LANES), jnp.int32),
            pltpu.SemaphoreType.DMA((2, requests, PIECES)),
            pltpu.SemaphoreType.DMA,
        ],
        compiler_params=params(20),
        name="home_attention",
    )(groups, at, lengths, q, *prompts, own, cache_keys, cache_values)


def merge_kernel(home_ref, a_ref, b_ref, c_ref, out_ref, *, requests):
    hd = a_ref.shape[1]
    qrows = home_ref.shape[0] // requests
    tree = out_ref.shape[0] // requests
    total = None
    for ref in (a_ref, b_ref, c_ref):
        both = ref[pl.ds(requests * qrows, 2 * requests), :].astype(F32)
        t = both[:requests] + both[requests:]
        total = t if total is None else total + t
    diagonal = lax.broadcasted_iota(jnp.int32, (qrows, hd), 0) == lax.broadcasted_iota(
        jnp.int32, (qrows, hd), 1
    )
    for r in range(requests):
        at = pl.ds(r * qrows, qrows)
        num = home_ref[at, pl.ds(0, hd)]
        for ref in (a_ref, b_ref, c_ref):
            num = num + ref[at, :].astype(F32)
        den = home_ref[at, pl.ds(hd, hd)] + jnp.sum(
            jnp.where(diagonal, jnp.broadcast_to(total[r : r + 1], (qrows, hd)), 0.0),
            axis=1,
            keepdims=True,
        )
        out = (num / den).astype(BF16)
        for g in range(qrows // tree):
            out_ref[pl.ds(r * tree, tree), pl.ds(g * hd, hd)] = out[g * tree : (g + 1) * tree]


def merge_call(home, a, b, c, requests, rows):
    hd = a.shape[1]
    return pl.pallas_call(
        lambda *refs: merge_kernel(*refs, requests=requests),
        in_specs=[VM] * 4,
        out_specs=VM,
        out_shape=jax.ShapeDtypeStruct((rows, home.shape[0] // rows * hd), BF16),
        compiler_params=params(8),
        name="merge",
    )(home, a, b, c)


def columns_kernel(mdl_ref, w_hbm, mine_ref, send_ref, sems):
    count, _, cols = mine_ref.shape
    copies = []
    for i in range(count):
        there = lax.rem(mdl_ref[0] // 2 + i, count)
        for j, ref in enumerate((mine_ref, send_ref)):
            side = lax.rem(mdl_ref[0] + j, 2)
            start = pl.multiple_of((2 * there + side) * cols, 128)
            c = pltpu.make_async_copy(w_hbm.at[:, pl.ds(start, cols)], ref.at[i], sems.at[j, i])
            c.start()
            copies.append(c)
    for c in copies:
        c.wait()


def columns_call(mdl, w_out, count):
    cols = w_out.shape[1] // (2 * count)
    return pl.pallas_call(
        columns_kernel,
        in_specs=[SMEM, HBM],
        out_specs=[VM, VM],
        out_shape=[jax.ShapeDtypeStruct((count, w_out.shape[0], cols), BF16)] * 2,
        scratch_shapes=[pltpu.SemaphoreType.DMA((2, count))],
        compiler_params=params(8),
        name="out_columns",
    )(mdl, w_out)


def out_kernel(mine_ref, other_ref, *refs):
    n = len(refs) // 3
    for wa, wb, out in zip(refs[:n], refs[n : 2 * n], refs[2 * n :]):
        out[...] = (dot(mine_ref[...], wa[0]) + dot(other_ref[...], wb[0])).astype(out.dtype)


def out_call(mine, other, w_mine, w_other, shifts, dtype):
    rows, inner = mine.shape
    cols = w_other.shape[2]
    whole = pl.BlockSpec((rows, inner), lambda i: (0, 0))
    chunks = [pl.BlockSpec((1, inner, cols), lambda i, n=n: (n, 0, 0)) for n in shifts]
    return pl.pallas_call(
        out_kernel,
        grid=(1,),
        in_specs=[whole, whole] + chunks * 2,
        out_specs=[pl.BlockSpec((rows, cols), lambda i: (0, 0))] * len(shifts),
        out_shape=[jax.ShapeDtypeStruct((rows, cols), dtype)] * len(shifts),
        compiler_params=params(16),
        name="out_proj",
    )(mine, other, *([w_mine] * len(shifts)), *([w_other] * len(shifts)))


def last_kernel(acc_ref, at_ref, own_ref, a_ref, b_ref, c_ref, tok_hbm, out_ref, rows_ref, tok, sums, kept, sem):
    cols = own_ref.shape[1]
    requests, most = acc_ref.shape
    tree = own_ref.shape[0] // requests
    get = pltpu.make_async_copy(
        tok_hbm.at[:, pl.ds(pl.multiple_of(at_ref[0] * cols, 128), cols)], tok, sem
    )
    get.start()
    total = own_ref[...] + a_ref[...].astype(F32) + b_ref[...].astype(F32) + c_ref[...].astype(F32)
    rounded = total.astype(BF16)
    out_ref[...] = rounded
    get.wait()
    sums[...] = tok[...].astype(F32) + rounded.astype(F32)
    for r in range(requests):
        for k in range(most):
            slot = acc_ref[r, k]
            row = sums[pl.ds(r * tree + jnp.maximum(slot, 0), 1), :]
            kept[r, pl.ds(k, 1), :] = jnp.where(slot >= 0, row, 0.0)
    rows_ref[...] = kept[...].astype(BF16)


def last_call(accepted, column, own, a, b, c, tokens):
    rows, cols = own.shape
    requests, most = accepted.shape
    return pl.pallas_call(
        last_kernel,
        in_specs=[SMEM, SMEM, VM, VM, VM, VM, HBM],
        out_specs=[VM, VM],
        out_shape=[
            jax.ShapeDtypeStruct((rows, cols), BF16),
            jax.ShapeDtypeStruct((requests, most, cols), BF16),
        ],
        scratch_shapes=[
            pltpu.VMEM((rows, cols), BF16),
            pltpu.VMEM((rows, cols), F32),
            pltpu.VMEM((requests, most, cols), F32),
            pltpu.SemaphoreType.DMA,
        ],
        compiler_params=params(8),
        name="last_sums",
    )(accepted, column, own, a, b, c, tokens)


def shards(
    tokens, norm_gain, w_query, w_key, w_value, w_out, prompt_keys, prompt_values, cache_keys,
    cache_values, cache_length, request_group, ancestors, accepted,
):
    requests, tree = ancestors.shape[:2]
    rows = tokens.shape[0]
    hd = prompt_keys.shape[3]
    n_tok = lax.axis_size("tok")
    n_mdl = lax.axis_size("mdl")
    n_y = 4
    n_z = n_tok // n_y
    n_x = n_mdl // 2
    tok = lax.axis_index("tok")
    mdl = lax.axis_index("mdl")

    def along_y(v, n):
        perm = [(t, t // n_y * n_y + (t + n) % n_y) for t in range(n_tok)]
        return lax.ppermute(v, "tok", perm)

    def along_z(v, n):
        return lax.ppermute(v, "tok", [(t, (t + n * n_y) % n_tok) for t in range(n_tok)])

    def along_x(v, n):
        return lax.ppermute(v, "mdl", [(m, (m + 2 * n) % n_mdl) for m in range(n_mdl)])

    def other_core(v):
        return lax.ppermute(v, "mdl", [(m, m ^ 1) for m in range(n_mdl)])

    def in_hbm(v):
        return pltpu.with_memory_space_constraint(v, pltpu.HBM)

    tok_at = jnp.reshape(tok, (1,)).astype(jnp.int32)
    mdl_at = jnp.reshape(mdl, (1,)).astype(jnp.int32)

    squeeze = lambda v: v.reshape(v.shape[0], v.shape[1], v.shape[3])
    kv = join_call(in_hbm(squeeze(prompt_keys)), in_hbm(squeeze(prompt_values)))
    kv_r = along_y(kv, 1)
    kv_l = along_y(kv, -1)

    exponent = np.arange(hd // 2, dtype=np.float64) * (2.0 / hd)
    inverse = jnp.asarray(np.tile(THETA**-exponent, 2)[None, :], dtype=F32)
    table = ancestors.reshape(rows, tree)
    q, normed, turn = query_call(
        *map(
            in_hbm,
            (cache_length, tokens, norm_gain.reshape(-1, hd), w_query, table, inverse),
        )
    )
    shifts = (2, 1, -1)
    q_far = [along_z(q, n) for n in shifts]
    own = tree_call(*map(in_hbm, (normed, w_key, w_value, turn)), q, in_hbm(table))

    k_half, v_half = halves_call(kv_r, kv_l)
    k_o = along_y(k_half, 1)
    v_o = along_y(v_half, -1)
    prompts = (kv, kv_r, kv_l, k_o, v_o)

    w_mine, w_send = columns_call(mdl_at, in_hbm(w_out), n_x)
    w_other = other_core(w_send)

    turns = [n % n_z * n_y for n in shifts]
    nears = near_call(
        request_group, tok_at, q_far, kv, in_hbm(kv_r), in_hbm(kv_l), requests, turns, n_tok
    )
    parts = far_call(request_group, tok_at, nears, q_far, k_o, v_o, requests, turns, n_tok)
    back = [along_z(part, -n) for n, part in zip(shifts, parts)]
    home = home_call(
        request_group, tok_at, cache_length, q, prompts, in_hbm(own),
        in_hbm(squeeze(cache_keys)), in_hbm(squeeze(cache_values)),
    )
    attended = merge_call(home, *back, requests, rows)

    attended_other = other_core(attended)
    sent = []
    for group in ((2,), (1, -1), (0,)):
        outs = out_call(
            attended, attended_other, w_mine, w_other, [n % n_x for n in group],
            F32 if group == (0,) else BF16,
        )
        sent += [along_x(o, n) if n else o for o, n in zip(outs, group)]
    far, up, down, own_sum = sent
    return tuple(last_call(accepted, mdl_at, own_sum, far, up, down, in_hbm(tokens)))


def solution(mesh):
    placed = (
        P("tok", None),
        P(),
        P(None, "mdl"),
        P(None, "mdl"),
        P(None, "mdl"),
        P("mdl", None),
        P(None, "tok", "mdl", None),
        P(None, "tok", "mdl", None),
        P("tok", None, "mdl", None),
        P("tok", None, "mdl", None),
        P("tok"),
        P(),
        P("tok", None, None),
        P("tok", None),
    )

    return jax.shard_map(
        shards,
        mesh=mesh,
        in_specs=placed,
        out_specs=(P("tok", "mdl"), P("tok", None, "mdl")),
        check_vma=False,
    )
```

time: 103 us -> 102 us (level)
  waiting for transfers between devices: 17.9 us -> 29.1 us
  local copies, waits for them, and re-layouts: 13.6 us -> 2.73 us
  starting transfers between devices: 27.7 us -> 25.1 us
  Pallas kernels: 41.5 us -> 42.7 us
    ppermute x6, waiting for transfers between devices: 0.02 us -> 10.2 us  [along_z(): lax.ppermute(v, 'tok', [(t, (t + n * n_y) % n_tok) for t in range(n_tok)])]
    unnamed x60 -> x18, local copies, waits for them, and re-layouts: 11.9 us -> 2.73 us
    ppermute x6, starting transfers between devices: 14.2 us -> 12.1 us  [along_z(): lax.ppermute(v, 'tok', [(t, (t + n * n_y) % n_tok) for t in range(n_tok)])]
    slice x2 -> x0, local copies, waits for them, and re-layouts: 1.64 us -> none  [the longest x1 0.83 us: shards(): k_o = along_y(kv_r[:groups_n], 1)]
    pallas_call x11 -> x12, Pallas kernels: 41.2 us -> 42.5 us  [the longest x1 7.51 us: query_call(): pl.pallas_call(query_kernel, in_specs=[HBM] * 6, out_specs=[VM, HBM, HBM]...]
    ppermute x3, waiting for transfers between devices: 6.98 us -> 8.09 us  [along_x(): lax.ppermute(v, 'mdl', [(m, (m + 2 * n) % n_mdl) for m in range(n_mdl)])]
  transfers between devices with their start and end apart: 15 -> 15, of which waited for: 7 -> 8; matrix products, arithmetic and copies ran while one was open for 2% -> 0% of each run, Pallas kernels for 34% -> 34%
where the time goes in v1:
time: 102 us; the launch traced here: 101 us
  Pallas kernels  42.7 us (42%)
  waiting for transfers between devices  29.1 us (29%)
  starting transfers between devices  25.1 us (25%)
  local copies, waits for them, and re-layouts  2.73 us (3%)
    ppermute x6, starting transfers between devices, along_z(): lax.ppermute(v, 'tok', [(t, (t + n * n_y) % n_tok) for t in range(n_tok)])  12.1 us
    ppermute x6, waiting for transfers between devices, along_z(): lax.ppermute(v, 'tok', [(t, (t + n * n_y) % n_tok) for t in range(n_tok)])  10.2 us
    ppermute x4, waiting for transfers between devices, along_y(): return lax.ppermute(v, 'tok', perm)  9.25 us
    ppermute x3, waiting for transfers between devices, along_x(): lax.ppermute(v, 'mdl', [(m, (m + 2 * n) % n_mdl) for m in range(n_mdl)])  8.09 us
    pallas_call x1, Pallas kernels, query_call(): pl.pallas_call(query_kernel, in_specs=[HBM] * 6, out_specs=[VM, HBM, HBM]...  7.51 us
    pallas_call x1, Pallas kernels, home_call(): pl.pallas_call(home_kernel, in_specs=[SMEM, SMEM, SMEM] + [VM] * 6 + [HBM...  7.26 us
    pallas_call x1, Pallas kernels, tree_call(): pl.pallas_call(tree_kernel, in_specs=[HBM, HBM, HBM, HBM, VM, HBM], out_s...  6.57 us
    ppermute x4, starting transfers between devices, along_y(): return lax.ppermute(v, 'tok', perm)  6.43 us
  transfers between devices with their start and end apart: 15, of which 8 were waited for; matrix products, arithmetic and copies ran while one was open for 0% of the time, Pallas kernels for 34%

profile of v1, /device:TPU:0, one launch (start us, length us, event | category | flops | bytes accessed | tf_op | source)
XLA Modules:
  0.0 100.6 jit_solution(4112456303300216770)
XLA Ops:
  0.6 4.1 %out_columns.1 = (bf16[4,512,640]{2,1,0:T(8,128)(2,1)S(1)}, bf16[4,512,640]{2,1,0:T(8,128)(2,1)}) custom-call(s32[1]{0:T(128)} %bitcast.mdl_ref.at_ref, bf16[512,5120]{1,0:T(8,128)(2,1)} %w_hbm.1), custom_call_target="tpu_custom_call" | custom-call | tf_op jit(solution)/shard_map/out_columns/pallas_call | solution.py:490
  6.0 3.2 %collective-permute-start.1 = (bf16[12,256,128]{2,1,0:T(8,128)(2,1)S(1)}, bf16[12,256,128]{2,1,0:T(8,128)(2,1)S(1)}, u32[]{:S(2)}, u32[]{:S(2)}) collective-permute-start(bf16[12,256,128]{2,1,0:T(8,128)(2,1)S(1)} %join.1.kv.refs_2_), channel_id=1, source_target_pairs={{0,24},{8,0},{16,8},{24,16},{32,56},{40,32},{48,40},{56,48},{64,88... | collective-permute-start | bytes 2359304 | tf_op jit(solution)/shard_map/ppermute | solution.py:583
  9.2 7.5 %query_proj.1 = (bf16[1024,128]{1,0:T(8,128)(2,1)}, bf16[256,5120]{1,0:T(8,128)(2,1)}, f32[2,256,128]{2,1,0:T(8,128)}) custom-call(s32[8]{0:T(128)} %len_ref.1, bf16[256,5120]{1,0:T(8,128)(2,1)} %tok_hbm.3, bf16[40,128]{1,0:T(8,128)(2,1)} %bitcast.14, bf16[5120,512]{1,0:T(8,128)(2,1)} %wq_hbm.1, s32[256,32]{1,0:T(8,128)} %bitcast.10, ...), custom_call_target="tpu_custom_call" | custom-call | tf_op jit(solution)/shard_map/query_proj/pallas_call | solution.py:121
  16.7 4.1 %collective-permute-start.6 = (bf16[1024,128]{1,0:T(8,128)(2,1)}, bf16[1024,128]{1,0:T(8,128)(2,1)S(1)}, u32[]{:S(2)}, u32[]{:S(2)}) collective-permute-start(bf16[1024,128]{1,0:T(8,128)(2,1)} %get-tuple-element.17.q_ref), channel_id=1, source_target_pairs={{0,96},{8,104},{16,112},{24,120},{32,0},{40,8},{48,16},{56,24},{64... | collective-permute-start | bytes 786440 | tf_op jit(solution)/shard_map/ppermute | solution.py:586
  20.8 5.8 %collective-permute-done.1.left_ref.kv_l.refs_4_ = bf16[12,256,128]{2,1,0:T(8,128)(2,1)S(1)} collective-permute-done((bf16[12,256,128]{2,1,0:T(8,128)(2,1)S(1)}, bf16[12,256,128]{2,1,0:T(8,128)(2,1)S(1)}, u32[]{:S(2)}, u32[]{:S(2)}) %collective-permute-start.1) | collective-permute-done | bytes 786464 | tf_op jit(solution)/shard_map/ppermute | solution.py:583
  26.6 3.4 %collective-permute-done.right_ref.kv_r.refs_3_ = bf16[12,256,128]{2,1,0:T(8,128)(2,1)S(1)} collective-permute-done((bf16[12,256,128]{2,1,0:T(8,128)(2,1)S(1)}, bf16[12,256,128]{2,1,0:T(8,128)(2,1)S(1)}, u32[]{:S(2)}, u32[]{:S(2)}) %collective-permute-start) | collective-permute-done | bytes 786464 | tf_op jit(solution)/shard_map/ppermute | solution.py:583
  32.2 3.2 %collective-permute-start.3 = (bf16[6,256,128]{2,1,0:T(8,128)(2,1)}, bf16[6,256,128]{2,1,0:T(8,128)(2,1)}, u32[]{:S(2)}, u32[]{:S(2)}) collective-permute-start(bf16[6,256,128]{2,1,0:T(8,128)(2,1)} %get-tuple-element.19), channel_id=1, source_target_pairs={{0,24},{8,0},{16,8},{24,16},{32,56},{40,32},{48,40},{56,48},{64,88... | collective-permute-start | bytes 1179656 | tf_op jit(solution)/shard_map/ppermute | solution.py:583
  35.4 1.9 %collective-permute-start.5 = (bf16[1024,128]{1,0:T(8,128)(2,1)}, bf16[1024,128]{1,0:T(8,128)(2,1)}, u32[]{:S(2)}, u32[]{:S(2)}) collective-permute-start(bf16[1024,128]{1,0:T(8,128)(2,1)} %get-tuple-element.17.q_ref), channel_id=1, source_target_pairs={{0,32},{8,40},{16,48},{24,56},{32,64},{40,72},{48,80},{56,88},{64,... | collective-permute-start | bytes 786440 | tf_op jit(solution)/shard_map/ppermute | solution.py:586
  38.0 3.6 %collective-permute-start.4 = (bf16[1024,128]{1,0:T(8,128)(2,1)}, bf16[1024,128]{1,0:T(8,128)(2,1)}, u32[]{:S(2)}, u32[]{:S(2)}) collective-permute-start(bf16[1024,128]{1,0:T(8,128)(2,1)} %get-tuple-element.17.q_ref), channel_id=1, source_target_pairs={{0,64},{8,72},{16,80},{24,88},{32,96},{40,104},{48,112},{56,120},{... | collective-permute-start | bytes 786440 | tf_op jit(solution)/shard_map/ppermute | solution.py:586
  41.6 4.4 %collective-permute-done.5.refs_6_.refs_5_ = bf16[1024,128]{1,0:T(8,128)(2,1)} collective-permute-done((bf16[1024,128]{1,0:T(8,128)(2,1)}, bf16[1024,128]{1,0:T(8,128)(2,1)}, u32[]{:S(2)}, u32[]{:S(2)}) %collective-permute-start.5) | collective-permute-done | bytes 262176 | tf_op jit(solution)/shard_map/ppermute | solution.py:586
  46.0 5.8 %collective-permute-done.4.refs_5_.refs_4_ = bf16[1024,128]{1,0:T(8,128)(2,1)} collective-permute-done((bf16[1024,128]{1,0:T(8,128)(2,1)}, bf16[1024,128]{1,0:T(8,128)(2,1)}, u32[]{:S(2)}, u32[]{:S(2)}) %collective-permute-start.4) | collective-permute-done | bytes 262176 | tf_op jit(solution)/shard_map/ppermute | solution.py:586
  52.8 4.2 %prompt_near.1 = (f32[1024,256]{1,0:T(8,128)S(1)}, f32[1024,256]{1,0:T(8,128)S(1)}, f32[1024,256]{1,0:T(8,128)S(1)}) custom-call(s32[128]{0:T(128)S(1)} %copy-done.6, s32[1]{0:T(128)} %bitcast.1.at_ref.refs_1_, bf16[12,256,128]{2,1,0:T(8,128)(2,1)S(1)} %join.1.kv.refs_2_, bf16[12,256,128]{2,1,0:T(8,128)(2,1)} %copy-done.2, bf16[12,256,128]{2,1,0:T(8,128)(2,1)} %copy-done, ...), custom_call_target="tpu_custom_call" | custom-call | tf_op jit(solution)/shard_map/prompt_near/pallas_call | solution.py:294
  57.0 2.4 %prompt_far.1 = (bf16[1040,128]{1,0:T(8,128)(2,1)S(1)}, bf16[1040,128]{1,0:T(8,128)(2,1)S(1)}, bf16[1040,128]{1,0:T(8,128)(2,1)S(1)}) custom-call(s32[128]{0:T(128)S(1)} %copy-done.6, s32[1]{0:T(128)} %bitcast.1.at_ref.refs_1_, bf16[6,256,128]{2,1,0:T(8,128)(2,1)} %collective-permute-done.2.k_o.refs_2_, ...), custom_call_target="tpu_custom_call" | custom-call | tf_op jit(solution)/shard_map/prompt_far/pallas_call | solution.py:331
  60.1 1.8 %collective-permute-start.9 = (bf16[1040,128]{1,0:T(8,128)(2,1)S(1)}, bf16[1040,128]{1,0:T(8,128)(2,1)S(1)}, u32[]{:S(2)}, u32[]{:S(2)}) collective-permute-start(bf16[1040,128]{1,0:T(8,128)(2,1)S(1)} %get-tuple-element.27), channel_id=1, source_target_pairs={{0,32},{8,40},{16,48},{24,56},{32,64},{40,72},{48,80},{56,88},{64,... | collective-permute-start | bytes 798728 | tf_op jit(solution)/shard_map/ppermute | solution.py:586
  62.0 6.6 %tree_attention.1.own_hbm = f32[1024,256]{1,0:T(8,128)} custom-call(bf16[256,5120]{1,0:T(8,128)(2,1)} %get-tuple-element.20.normed_hbm, bf16[5120,128]{1,0:T(8,128)(2,1)} %wk_hbm.1, bf16[5120,128]{1,0:T(8,128)(2,1)} %wv_hbm.1, f32[2,256,128]{2,1,0:T(8,128)} %get-tuple-element.21.turn_hbm, bf16[1024,128]{1,0:T(8,128)(2,1)} %get-tuple-element.17.q_ref, ...), custom_call_target="tpu_custom_call" | custom-call | tf_op jit(solution)/shard_map/tree_attention/pallas_call | solution.py:201
  68.6 7.3 %home_attention.1.refs_0_ = f32[1024,256]{1,0:T(8,128)S(1)} custom-call(s32[128]{0:T(128)S(1)} %copy-done.6, s32[1]{0:T(128)} %bitcast.1.at_ref.refs_1_, s32[8]{0:T(128)S(1)} %copy-done.8, bf16[1024,128]{1,0:T(8,128)(2,1)} %get-tuple-element.17.q_ref, bf16[12,256,128]{2,1,0:T(8,128)(2,1)S(1)} %join.1.kv.refs_2_, bf16[12,256,128]{2,1,0:T(8,128)(2,1)S(1)} %copy-done.3, ...), custom_call_target="tpu_custom_call" | custom-call | tf_op jit(solution)/shard_map/home_attention/pallas_call | solution.py:416
  77.8 1.7 %out_proj.4 = bf16[256,640]{1,0:T(8,128)(2,1)S(1)} custom-call(bf16[256,512]{1,0:T(8,128)(2,1)S(1)} %merge.1.mine_ref, bf16[256,512]{1,0:T(8,128)(2,1)S(1)} %collective-permute-done.10.other_ref, bf16[4,512,640]{2,1,0:T(8,128)(2,1)S(1)} %get-tuple-element.28.refs_0_.refs_1_, bf16[4,512,640]{2,1,0:T(8,128)(2,1)} %collective-permute-done.11.refs_1_.refs_2_.refs_3_), custom_call_target="tpu_custom_call" | custom-call | tf_op jit(solution)/shard_map/out_proj/pallas_call | solution.py:512
  79.4 3.1 %collective-permute-start.12 = (bf16[256,640]{1,0:T(8,128)(2,1)S(1)}, bf16[256,640]{1,0:T(8,128)(2,1)S(1)}, u32[]{:S(2)}, u32[]{:S(2)}) collective-permute-start(bf16[256,640]{1,0:T(8,128)(2,1)S(1)} %out_proj.4), channel_id=1, source_target_pairs={{0,4},{1,5},{2,6},{3,7},{4,0},{5,1},{6,2},{7,3},{8,12},{9,13},{10,... | collective-permute-start | bytes 983048 | tf_op jit(solution)/shard_map/ppermute | solution.py:589
  82.5 2.3 %out_proj.5 = (bf16[256,640]{1,0:T(8,128)(2,1)S(1)}, bf16[256,640]{1,0:T(8,128)(2,1)S(1)}) custom-call(bf16[256,512]{1,0:T(8,128)(2,1)S(1)} %merge.1.mine_ref, bf16[256,512]{1,0:T(8,128)(2,1)S(1)} %collective-permute-done.10.other_ref, bf16[4,512,640]{2,1,0:T(8,128)(2,1)S(1)} %get-tuple-element.28.refs_0_.refs_1_, ...), custom_call_target="tpu_custom_call" | custom-call | tf_op jit(solution)/shard_map/out_proj/pallas_call | solution.py:512
  85.5 2.6 %collective-permute-start.14 = (bf16[256,640]{1,0:T(8,128)(2,1)S(1)}, bf16[256,640]{1,0:T(8,128)(2,1)S(1)}, u32[]{:S(2)}, u32[]{:S(2)}) collective-permute-start(bf16[256,640]{1,0:T(8,128)(2,1)S(1)} %get-tuple-element.31), channel_id=1, source_target_pairs={{0,6},{1,7},{2,0},{3,1},{4,2},{5,3},{6,4},{7,5},{8,14},{9,15},{10,... | collective-permute-start | bytes 983048 | tf_op jit(solution)/shard_map/ppermute | solution.py:589
  88.1 1.7 %out_proj.3.own_ref = f32[256,640]{1,0:T(8,128)S(1)} custom-call(bf16[256,512]{1,0:T(8,128)(2,1)S(1)} %merge.1.mine_ref, bf16[256,512]{1,0:T(8,128)(2,1)S(1)} %collective-permute-done.10.other_ref, bf16[4,512,640]{2,1,0:T(8,128)(2,1)S(1)} %get-tuple-element.28.refs_0_.refs_1_, bf16[4,512,640]{2,1,0:T(8,128)(2,1)} %collective-permute-done.11.refs_1_.refs_2_.refs_3_), custom_call_target="tpu_custom_call" | custom-call | tf_op jit(solution)/shard_map/out_proj/pallas_call | solution.py:512
  89.8 1.8 %collective-permute-done.12.a_ref = bf16[256,640]{1,0:T(8,128)(2,1)S(1)} collective-permute-done((bf16[256,640]{1,0:T(8,128)(2,1)S(1)}, bf16[256,640]{1,0:T(8,128)(2,1)S(1)}, u32[]{:S(2)}, u32[]{:S(2)}) %collective-permute-start.12) | collective-permute-done | bytes 327712 | tf_op jit(solution)/shard_map/ppermute | solution.py:589
  91.6 6.2 %collective-permute-done.13.b_ref = bf16[256,640]{1,0:T(8,128)(2,1)S(1)} collective-permute-done((bf16[256,640]{1,0:T(8,128)(2,1)S(1)}, bf16[256,640]{1,0:T(8,128)(2,1)S(1)}, u32[]{:S(2)}, u32[]{:S(2)}) %collective-permute-start.13) | collective-permute-done | bytes 327712 | tf_op jit(solution)/shard_map/ppermute | solution.py:589
  97.9 2.6 %last_sums.1 = (bf16[256,640]{1,0:T(8,128)(2,1)}, bf16[8,8,640]{2,1,0:T(8,128)(2,1)}) custom-call(s32[8,8]{1,0:T(8,128)S(1)} %copy-done.7, s32[1]{0:T(128)} %bitcast.mdl_ref.at_ref, f32[256,640]{1,0:T(8,128)S(1)} %out_proj.3.own_ref, bf16[256,640]{1,0:T(8,128)(2,1)S(1)} %collective-permute-done.12.a_ref, bf16[256,640]{1,0:T(8,128)(2,1)S(1)} %collective-permute-done.13.b_ref, ...), custom_call_target="tpu_custom_call" | custom-call | tf_op jit(solution)/shard_map/last_sums/pallas_call | solution.py:547
  (37 shorter events, 8.3 us)
Async XLA Ops:
  4.7 73.0 %collective-permute-start.11 = (bf16[4,512,640]{2,1,0:T(8,128)(2,1)}, bf16[4,512,640]{2,1,0:T(8,128)(2,1)}, u32[]{:S(2)}, u32[]{:S(2)}) collective-permute-start(bf16[4,512,640]{2,1,0:T(8,128)(2,1)} %get-tuple-element.29), channel_id=1, source_target_pairs={{0,1},{1,0},{2,3},{3,2},{4,5},{5,4},{6,7},{7,6},{8,9},{9,8},{10,11... | collective-permute-start | bytes 7864328 | tf_op jit(solution)/shard_map/ppermute | solution.py:592
  6.0 20.7 %collective-permute-start.1 = (bf16[12,256,128]{2,1,0:T(8,128)(2,1)S(1)}, bf16[12,256,128]{2,1,0:T(8,128)(2,1)S(1)}, u32[]{:S(2)}, u32[]{:S(2)}) collective-permute-start(bf16[12,256,128]{2,1,0:T(8,128)(2,1)S(1)} %join.1.kv.refs_2_), channel_id=1, source_target_pairs={{0,24},{8,0},{16,8},{24,16},{32,56},{40,32},{48,40},{56,48},{64,88... | collective-permute-start | bytes 2359304 | tf_op jit(solution)/shard_map/ppermute | solution.py:583
  9.2 20.9 %collective-permute-start = (bf16[12,256,128]{2,1,0:T(8,128)(2,1)S(1)}, bf16[12,256,128]{2,1,0:T(8,128)(2,1)S(1)}, u32[]{:S(2)}, u32[]{:S(2)}) collective-permute-start(bf16[12,256,128]{2,1,0:T(8,128)(2,1)S(1)} %join.1.kv.refs_2_), channel_id=1, source_target_pairs={{0,8},{8,16},{16,24},{24,0},{32,40},{40,48},{48,56},{56,32},{64,72... | collective-permute-start | bytes 2359304 | tf_op jit(solution)/shard_map/ppermute | solution.py:583
  9.2 42.6 %copy-start.6 = (s32[128]{0:T(128)S(1)}, s32[128]{0:T(128)}, u32[]{:S(2)}) copy-start(s32[128]{0:T(128)} %refs_0_.3) | copy-start | bytes 1540
  16.7 20.6 %collective-permute-start.6 = (bf16[1024,128]{1,0:T(8,128)(2,1)}, bf16[1024,128]{1,0:T(8,128)(2,1)S(1)}, u32[]{:S(2)}, u32[]{:S(2)}) collective-permute-start(bf16[1024,128]{1,0:T(8,128)(2,1)} %get-tuple-element.17.q_ref), channel_id=1, source_target_pairs={{0,96},{8,104},{16,112},{24,120},{32,0},{40,8},{48,16},{56,24},{64... | collective-permute-start | bytes 786440 | tf_op jit(solution)/shard_map/ppermute | solution.py:586
  30.0 1.2 %copy-start.2 = (bf16[12,256,128]{2,1,0:T(8,128)(2,1)}, bf16[12,256,128]{2,1,0:T(8,128)(2,1)S(1)}, u32[]{:S(2)}) copy-start(bf16[12,256,128]{2,1,0:T(8,128)(2,1)S(1)} %collective-permute-done.right_ref.kv_r.refs_3_) | copy-start | bytes 2359300
  31.3 0.9 copy-start
  32.2 24.9 %collective-permute-start.2 = (bf16[6,256,128]{2,1,0:T(8,128)(2,1)}, bf16[6,256,128]{2,1,0:T(8,128)(2,1)}, u32[]{:S(2)}, u32[]{:S(2)}) collective-permute-start(bf16[6,256,128]{2,1,0:T(8,128)(2,1)} %get-tuple-element.18), channel_id=1, source_target_pairs={{0,8},{8,16},{16,24},{24,0},{32,40},{40,48},{48,56},{56,32},{64,72... | collective-permute-start | bytes 1179656 | tf_op jit(solution)/shard_map/ppermute | solution.py:583
  32.2 24.9 %collective-permute-start.3 = (bf16[6,256,128]{2,1,0:T(8,128)(2,1)}, bf16[6,256,128]{2,1,0:T(8,128)(2,1)}, u32[]{:S(2)}, u32[]{:S(2)}) collective-permute-start(bf16[6,256,128]{2,1,0:T(8,128)(2,1)} %get-tuple-element.19), channel_id=1, source_target_pairs={{0,24},{8,0},{16,8},{24,16},{32,56},{40,32},{48,40},{56,48},{64,88... | collective-permute-start | bytes 1179656 | tf_op jit(solution)/shard_map/ppermute | solution.py:583
  35.4 10.6 %collective-permute-start.5 = (bf16[1024,128]{1,0:T(8,128)(2,1)}, bf16[1024,128]{1,0:T(8,128)(2,1)}, u32[]{:S(2)}, u32[]{:S(2)}) collective-permute-start(bf16[1024,128]{1,0:T(8,128)(2,1)} %get-tuple-element.17.q_ref), channel_id=1, source_target_pairs={{0,32},{8,40},{16,48},{24,56},{32,64},{40,72},{48,80},{56,88},{64,... | collective-permute-start | bytes 786440 | tf_op jit(solution)/shard_map/ppermute | solution.py:586
  37.3 0.7 copy-start.4
  38.0 13.8 %collective-permute-start.4 = (bf16[1024,128]{1,0:T(8,128)(2,1)}, bf16[1024,128]{1,0:T(8,128)(2,1)}, u32[]{:S(2)}, u32[]{:S(2)}) collective-permute-start(bf16[1024,128]{1,0:T(8,128)(2,1)} %get-tuple-element.17.q_ref), channel_id=1, source_target_pairs={{0,64},{8,72},{16,80},{24,88},{32,96},{40,104},{48,112},{56,120},{... | collective-permute-start | bytes 786440 | tf_op jit(solution)/shard_map/ppermute | solution.py:586
  51.8 1.0 copy-start.5
  59.5 16.4 %collective-permute-start.7 = (bf16[1040,128]{1,0:T(8,128)(2,1)S(1)}, bf16[1040,128]{1,0:T(8,128)(2,1)S(1)}, u32[]{:S(2)}, u32[]{:S(2)}) collective-permute-start(bf16[1040,128]{1,0:T(8,128)(2,1)S(1)} %get-tuple-element.25), channel_id=1, source_target_pairs={{0,64},{8,72},{16,80},{24,88},{32,96},{40,104},{48,112},{56,120},{... | collective-permute-start | bytes 798728 | tf_op jit(solution)/shard_map/ppermute | solution.py:586
  60.0 15.9 %collective-permute-start.8 = (bf16[1040,128]{1,0:T(8,128)(2,1)S(1)}, bf16[1040,128]{1,0:T(8,128)(2,1)S(1)}, u32[]{:S(2)}, u32[]{:S(2)}) collective-permute-start(bf16[1040,128]{1,0:T(8,128)(2,1)S(1)} %get-tuple-element.26), channel_id=1, source_target_pairs={{0,96},{8,104},{16,112},{24,120},{32,0},{40,8},{48,16},{56,24},{64... | collective-permute-start | bytes 798728 | tf_op jit(solution)/shard_map/ppermute | solution.py:586
  60.1 15.7 %collective-permute-start.9 = (bf16[1040,128]{1,0:T(8,128)(2,1)S(1)}, bf16[1040,128]{1,0:T(8,128)(2,1)S(1)}, u32[]{:S(2)}, u32[]{:S(2)}) collective-permute-start(bf16[1040,128]{1,0:T(8,128)(2,1)S(1)} %get-tuple-element.27), channel_id=1, source_target_pairs={{0,32},{8,40},{16,48},{24,56},{32,64},{40,72},{48,80},{56,88},{64,... | collective-permute-start | bytes 798728 | tf_op jit(solution)/shard_map/ppermute | solution.py:586
  62.0 6.6 %copy-start.1 = (bf16[12,256,128]{2,1,0:T(8,128)(2,1)S(1)}, bf16[12,256,128]{2,1,0:T(8,128)(2,1)}, u32[]{:S(2)}) copy-start(bf16[12,256,128]{2,1,0:T(8,128)(2,1)} %copy-done) | copy-start | bytes 2359300
  62.0 6.6 %copy-start.3 = (bf16[12,256,128]{2,1,0:T(8,128)(2,1)S(1)}, bf16[12,256,128]{2,1,0:T(8,128)(2,1)}, u32[]{:S(2)}) copy-start(bf16[12,256,128]{2,1,0:T(8,128)(2,1)} %copy-done.2) | copy-start | bytes 2359300
  62.0 6.6 %copy-start.8 = (s32[8]{0:T(128)S(1)}, s32[8]{0:T(128)}, u32[]{:S(2)}) copy-start(s32[8]{0:T(128)} %len_ref.1) | copy-start | bytes 100
  76.1 1.6 %collective-permute-start.10 = (bf16[256,512]{1,0:T(8,128)(2,1)S(1)}, bf16[256,512]{1,0:T(8,128)(2,1)S(1)}, u32[]{:S(2)}, u32[]{:S(2)}) collective-permute-start(bf16[256,512]{1,0:T(8,128)(2,1)S(1)} %merge.1.mine_ref), channel_id=1, source_target_pairs={{0,1},{1,0},{2,3},{3,2},{4,5},{5,4},{6,7},{7,6},{8,9},{9,8},{10,11... | collective-permute-start | bytes 786440 | tf_op jit(solution)/shard_map/ppermute | solution.py:592
  79.4 12.2 %collective-permute-start.12 = (bf16[256,640]{1,0:T(8,128)(2,1)S(1)}, bf16[256,640]{1,0:T(8,128)(2,1)S(1)}, u32[]{:S(2)}, u32[]{:S(2)}) collective-permute-start(bf16[256,640]{1,0:T(8,128)(2,1)S(1)} %out_proj.4), channel_id=1, source_target_pairs={{0,4},{1,5},{2,6},{3,7},{4,0},{5,1},{6,2},{7,3},{8,12},{9,13},{10,... | collective-permute-start | bytes 983048 | tf_op jit(solution)/shard_map/ppermute | solution.py:589
  84.8 13.0 %collective-permute-start.13 = (bf16[256,640]{1,0:T(8,128)(2,1)S(1)}, bf16[256,640]{1,0:T(8,128)(2,1)S(1)}, u32[]{:S(2)}, u32[]{:S(2)}) collective-permute-start(bf16[256,640]{1,0:T(8,128)(2,1)S(1)} %get-tuple-element.30), channel_id=1, source_target_pairs={{0,2},{1,3},{2,4},{3,5},{4,6},{5,7},{6,0},{7,1},{8,10},{9,11},{10,... | collective-permute-start | bytes 983048 | tf_op jit(solution)/shard_map/ppermute | solution.py:589
  85.5 12.4 %copy-start.7 = (s32[8,8]{1,0:T(8,128)S(1)}, s32[8,8]{1,0:T(8,128)}, u32[]{:S(2)}) copy-start(s32[8,8]{1,0:T(8,128)} %acc_ref.1) | copy-start | bytes 772
  85.5 12.4 %collective-permute-start.14 = (bf16[256,640]{1,0:T(8,128)(2,1)S(1)}, bf16[256,640]{1,0:T(8,128)(2,1)S(1)}, u32[]{:S(2)}, u32[]{:S(2)}) collective-permute-start(bf16[256,640]{1,0:T(8,128)(2,1)S(1)} %get-tuple-element.31), channel_id=1, source_target_pairs={{0,6},{1,7},{2,0},{3,1},{4,2},{5,3},{6,4},{7,5},{8,14},{9,15},{10,... | collective-permute-start | bytes 983048 | tf_op jit(solution)/shard_map/ppermute | solution.py:589

commit v2 on v1

--- a/solution.py
+++ b/solution.py
@@ -42,29 +42,37 @@
     return x * cosine + pltpu.roll(x, x.shape[1] // 2, 1) * sine
 
 
-def query_kernel(
-    len_hbm, tok_hbm, gain_hbm, wq_hbm, anc_hbm, inv_hbm, q_ref, normed_hbm, turn_hbm,
-    lengths, tok, gain, wq, table, inverse, normed_ref, turn, sems, wsems, osems,
+def project_kernel(
+    len_hbm, tok_hbm, gain_hbm, wq_hbm, wk_hbm, wv_hbm, anc_hbm, inv_hbm, q_ref, k_ref, v_ref,
+    lengths, tok, gain, w, table, inverse, sems, csems,
 ):
     rows, width = tok.shape
     requests = lengths.shape[0]
     tree = rows // requests
+    hd = inverse.shape[1]
+    inner = wq_hbm.shape[1]
+    part = width // CHUNKS
     firsts = [
         pltpu.make_async_copy(source, target, sems.at[i])
         for i, (source, target) in enumerate(
-            ((anc_hbm, table), (len_hbm, lengths), (inv_hbm, inverse), (gain_hbm, gain), (tok_hbm, tok))
+            ((anc_hbm, table), (len_hbm, lengths), (inv_hbm, inverse), (gain_hbm, gain))
         )
     ]
     for c in firsts:
         c.start()
-    part = width // CHUNKS
     copies = []
     for i in range(CHUNKS):
         at = pl.ds(i * part, part)
-        c = pltpu.make_async_copy(wq_hbm.at[at], wq.at[at], wsems.at[i])
-        c.start()
-        copies.append(c)
-    for c in firsts[:3]:
+        four = (
+            pltpu.make_async_copy(tok_hbm.at[:, at], tok.at[:, at], csems.at[0, i]),
+            pltpu.make_async_copy(wq_hbm.at[at], w.at[at, pl.ds(0, inner)], csems.at[1, i]),
+            pltpu.make_async_copy(wk_hbm.at[at], w.at[at, pl.ds(inner, hd)], csems.at[2, i]),
+            pltpu.make_async_copy(wv_hbm.at[at], w.at[at, pl.ds(inner + hd, hd)], csems.at[3, i]),
+        )
+        for c in four:
+            c.start()
+        copies.append(four)
+    for c in firsts:
         c.wait()
     depth = jnp.sum(table[...], axis=1, keepdims=True).astype(F32) - 1.0
     places = jnp.concatenate(
@@ -78,143 +86,59 @@
     lane = lax.broadcasted_iota(jnp.int32, angles.shape, 1)
     cosine = jnp.cos(angles)
     sine = jnp.sin(angles)
-    sine = jnp.where(lane < angles.shape[1] // 2, -sine, sine)
-    turn[0] = cosine
-    turn[1] = sine
-    put_turn = pltpu.make_async_copy(turn, turn_hbm, osems.at[0])
-    put_turn.start()
-    for c in firsts[3:]:
-        c.wait()
+    sine = jnp.where(lane < hd // 2, -sine, sine)
     gains = gain[...].astype(F32)
-    gains = jnp.concatenate([gains[i : i + 1] for i in range(gain.shape[0])], axis=1)
-
-    def norm(i, _):
-        at = pl.ds(pl.multiple_of(i * 32, 32), 32)
-        wide = tok[at, :].astype(F32)
-        scale = lax.rsqrt(jnp.mean(wide * wide, axis=1, keepdims=True) + EPS)
-        normed_ref[at, :] = (wide * scale * gains).astype(BF16)
-        return 0
-
-    lax.fori_loop(0, rows // 32, norm, 0)
-    put_normed = pltpu.make_async_copy(normed_ref, normed_hbm, osems.at[1])
-    put_normed.start()
+    step = part // gain.shape[1]
     acc = None
+    squares = None
     for i in range(CHUNKS):
-        copies[i].wait()
-        d = dot(normed_ref[:, i * part : (i + 1) * part], wq[i * part : (i + 1) * part, :])
+        for c in copies[i]:
+            c.wait()
+        wide = tok[:, i * part : (i + 1) * part].astype(F32)
+        own_gain = jnp.concatenate([gains[j : j + 1] for j in range(i * step, (i + 1) * step)], axis=1)
+        d = dot((wide * own_gain).astype(BF16), w[i * part : (i + 1) * part, :])
         acc = d if acc is None else acc + d
-    hd = inverse.shape[1]
-    heads = acc.shape[1] // hd
-    fold = hd**-0.5 * math.log2(math.e)
+        square = wide * wide
+        for j in range(step):
+            t = square[:, j * gain.shape[1] : (j + 1) * gain.shape[1]]
+            squares = t if squares is None else squares + t
+    scale = lax.rsqrt(jnp.sum(squares, axis=1, keepdims=True) * (1.0 / width) + EPS)
+    heads = inner // hd
+    scaled = scale * (hd**-0.5 * math.log2(math.e))
     for g in range(heads):
-        turned = (rotate(acc[:, g * hd : (g + 1) * hd], cosine, sine) * fold).astype(BF16)
+        turned = rotate(acc[:, g * hd : (g + 1) * hd] * scaled, cosine, sine).astype(BF16)
         for r in range(requests):
             q_ref[pl.ds((r * heads + g) * tree, tree), :] = turned[r * tree : (r + 1) * tree]
-    put_turn.wait()
-    put_normed.wait()
-
-
-def query_call(lengths, tokens, gain, w_query, ancestors, inverse):
+    k_ref[...] = rotate(acc[:, inner : inner + hd] * scale, cosine, sine).astype(BF16)
+    v_ref[...] = (acc[:, inner + hd :] * scale).astype(BF16)
+
+
+def project_call(lengths, tokens, gain, w_query, w_key, w_value, ancestors, inverse):
     rows, width = tokens.shape
     hd = inverse.shape[1]
-    heads = w_query.shape[1] // hd
-    return pl.pallas_call(
-        query_kernel,
-        in_specs=[HBM] * 6,
-        out_specs=[VM, HBM, HBM],
+    inner = w_query.shape[1]
+    return pl.pallas_call(
+        project_kernel,
+        in_specs=[HBM] * 8,
+        out_specs=[VM, VM, VM],
         out_shape=[
-            jax.ShapeDtypeStruct((rows * heads, hd), BF16),
-            pltpu.HBM((rows, width), BF16),
-            pltpu.HBM((2, rows, hd), F32),
+            jax.ShapeDtypeStruct((rows * inner // hd, hd), BF16),
+            jax.ShapeDtypeStruct((rows, hd), BF16),
+            jax.ShapeDtypeStruct((rows, hd), BF16),
         ],
         scratch_shapes=[
             pltpu.SMEM(lengths.shape, jnp.int32),
             pltpu.VMEM((rows, width), BF16),
             pltpu.VMEM(gain.shape, BF16),
-            pltpu.VMEM(w_query.shape, BF16),
+            pltpu.VMEM((width, inner + 2 * hd), BF16),
             pltpu.VMEM(ancestors.shape, jnp.int32),
             pltpu.VMEM(inverse.shape, F32),
-            pltpu.VMEM((rows, width), BF16),
-            pltpu.VMEM((2, rows, hd), F32),
-            pltpu.SemaphoreType.DMA((5,)),
-            pltpu.SemaphoreType.DMA((CHUNKS,)),
-            pltpu.SemaphoreType.DMA((2,)),
-        ],
-        compiler_params=params(24),
-        name="query_proj",
-    )(lengths, tokens, gain, w_query, ancestors, inverse)
-
-
-def tree_kernel(
-    normed_hbm, wk_hbm, wv_hbm, turn_hbm, q_ref, anc_hbm, out_hbm,
-    normed_ref, w, turn, anc_ref, out_ref, sems, osems,
-):
-    rows, tree = anc_ref.shape
-    hd = q_ref.shape[1]
-    group = q_ref.shape[0] // rows
-    qrows = group * tree
-    part = w.shape[0] // CHUNKS
-    copies = []
-    for i in range(CHUNKS):
-        at = pl.ds(i * part, part)
-        three = (
-            pltpu.make_async_copy(normed_hbm.at[:, at], normed_ref.at[:, at], sems.at[0, i]),
-            pltpu.make_async_copy(wk_hbm.at[at], w.at[at, pl.ds(0, hd)], sems.at[1, i]),
-            pltpu.make_async_copy(wv_hbm.at[at], w.at[at, pl.ds(hd, hd)], sems.at[2, i]),
-        )
-        for c in three:
-            c.start()
-        copies.append(three)
-    get_turn = pltpu.make_async_copy(turn_hbm, turn, osems.at[rows // tree])
-    get_anc = pltpu.make_async_copy(anc_hbm, anc_ref, osems.at[rows // tree + 1])
-    get_turn.start()
-    get_anc.start()
-    both = None
-    for i in range(CHUNKS):
-        for c in copies[i]:
-            c.wait()
-        d = dot(normed_ref[:, i * part : (i + 1) * part], w[i * part : (i + 1) * part, :])
-        both = d if both is None else both + d
-    get_turn.wait()
-    get_anc.wait()
-    new_keys = rotate(both[:, :hd], turn[0], turn[1]).astype(BF16)
-    new_values = both[:, hd:].astype(BF16)
-    ones = jnp.ones((tree, hd), BF16)
-    puts = []
-    for r in range(rows // tree):
-        at = slice(r * tree, (r + 1) * tree)
-        here = pl.ds(r * qrows, qrows)
-        scores = dot_nt(q_ref[here, :], new_keys[at])
-        seen = jnp.concatenate([anc_ref[at, :]] * group, axis=0)
-        weights = jnp.where(seen > 0, jnp.exp2(scores), 0.0).astype(BF16)
-        out_ref[here, :] = dot(weights, jnp.concatenate([new_values[at], ones], axis=1))
-        put = pltpu.make_async_copy(out_ref.at[here], out_hbm.at[here], osems.at[r])
-        put.start()
-        puts.append(put)
-    for put in puts:
-        put.wait()
-
-
-def tree_call(normed, w_key, w_value, turn, q, ancestors):
-    rows, tree = ancestors.shape
-    hd = q.shape[1]
-    return pl.pallas_call(
-        tree_kernel,
-        in_specs=[HBM, HBM, HBM, HBM, VM, HBM],
-        out_specs=HBM,
-        out_shape=pltpu.HBM((q.shape[0], 2 * hd), F32),
-        scratch_shapes=[
-            pltpu.VMEM(normed.shape, BF16),
-            pltpu.VMEM((normed.shape[1], 2 * hd), BF16),
-            pltpu.VMEM(turn.shape, F32),
-            pltpu.VMEM(ancestors.shape, jnp.int32),
-            pltpu.VMEM((q.shape[0], 2 * hd), F32),
-            pltpu.SemaphoreType.DMA((3, CHUNKS)),
-            pltpu.SemaphoreType.DMA((rows // tree + 2,)),
-        ],
-        compiler_params=params(16),
-        name="tree_attention",
-    )(normed, w_key, w_value, turn, q, ancestors)
+            pltpu.SemaphoreType.DMA((4,)),
+            pltpu.SemaphoreType.DMA((4, CHUNKS)),
+        ],
+        compiler_params=params(28),
+        name="projections",
+    )(lengths, tokens, gain, w_query, w_key, w_value, ancestors, inverse)
 
 
 def join_kernel(a_hbm, b_hbm, out_ref, sems):
@@ -339,8 +263,8 @@
 
 
 def home_kernel(
-    group_ref, at_ref, len_ref, q_ref, kv, kv_r, kv_l, k_o, v_o, own_hbm, ck_hbm, cv_hbm, out_ref,
-    own_ref, keys, values, where_ref, sems, own_sem,
+    group_ref, at_ref, len_ref, q_ref, kv, kv_r, kv_l, k_o, v_o, new_k, new_v, anc_hbm, ck_hbm,
+    cv_hbm, out_ref, anc_ref, keys, values, where_ref, sems, anc_sem,
 ):
     requests, slots, hd = keys.shape
     qrows = q_ref.shape[0] // requests
@@ -366,8 +290,9 @@
                         for c in copies(r, i):
                             act(c)
 
-    get_own = pltpu.make_async_copy(own_hbm, own_ref, own_sem)
-    get_own.start()
+    get_anc = pltpu.make_async_copy(anc_hbm, anc_ref, anc_sem)
+    get_anc.start()
+    tree = anc_ref.shape[1]
     each_copy(lambda c: c.start())
     count = 0
     for r in range(requests):
@@ -383,12 +308,16 @@
         where_ref[1, count + j] = 0
     pieces = near_pieces(kv, kv_r, kv_l) + [(k_o, 0, v_o, 0)]
     ones = jnp.ones((KB, hd), BF16)
-    get_own.wait()
+    get_anc.wait()
     for r in range(requests):
         at = pl.ds(r * qrows, qrows)
-        out_ref[at, :] = own_ref[at, :] + prompt_sum(
-            q_ref[at, :], group_ref[at_ref[0] * requests + r], pieces, ones
-        )
+        mine = pl.ds(r * tree, tree)
+        q = q_ref[at, :]
+        seen = jnp.concatenate([anc_ref[mine, :]] * (qrows // tree), axis=0)
+        p = jnp.where(seen > 0, jnp.exp2(dot_nt(q, new_k[mine, :])), 0.0).astype(BF16)
+        out_ref[at, :] = prompt_sum(
+            q, group_ref[at_ref[0] * requests + r], pieces, ones
+        ) + dot(p, jnp.concatenate([new_v[mine, :], ones[:tree]], axis=1))
     column = lax.broadcasted_iota(jnp.int32, (qrows, KB), 1)
     each_copy(lambda c: c.wait())
 
@@ -411,15 +340,15 @@
     lax.fori_loop(0, (count + LANES - 1) // LANES, step, 0)
 
 
-def home_call(groups, at, lengths, q, prompts, own, cache_keys, cache_values):
-    requests, slots, _ = cache_keys.shape
+def home_call(groups, at, lengths, q, prompts, new_k, new_v, ancestors, cache_keys, cache_values):
+    requests, slots, hd = cache_keys.shape
     return pl.pallas_call(
         home_kernel,
-        in_specs=[SMEM, SMEM, SMEM] + [VM] * 6 + [HBM] * 3,
+        in_specs=[SMEM, SMEM, SMEM] + [VM] * 8 + [HBM] * 3,
         out_specs=VM,
-        out_shape=jax.ShapeDtypeStruct(own.shape, F32),
+        out_shape=jax.ShapeDtypeStruct((q.shape[0], 2 * hd), F32),
         scratch_shapes=[
-            pltpu.VMEM(own.shape, F32),
+            pltpu.VMEM(ancestors.shape, jnp.int32),
             pltpu.VMEM(cache_keys.shape, BF16),
             pltpu.VMEM(cache_values.shape, BF16),
             pltpu.SMEM((2, requests * slots // KB + LANES), jnp.int32),
@@ -428,7 +357,7 @@
         ],
         compiler_params=params(20),
         name="home_attention",
-    )(groups, at, lengths, q, *prompts, own, cache_keys, cache_values)
+    )(groups, at, lengths, q, *prompts, new_k, new_v, ancestors, cache_keys, cache_values)
 
 
 def merge_kernel(home_ref, a_ref, b_ref, c_ref, out_ref, *, requests):
@@ -470,8 +399,26 @@
     )(home, a, b, c)
 
 
-def columns_kernel(mdl_ref, w_hbm, mine_ref, send_ref, sems):
+def pick(acc_ref, x, tree):
+    rows = []
+    slot = lax.broadcasted_iota(jnp.int32, (tree, acc_ref.shape[1]), 0)
+    for r in range(acc_ref.shape[0]):
+        chosen = (slot == acc_ref[r : r + 1, :]).astype(F32).astype(BF16)
+        rows.append(
+            lax.dot_general(
+                chosen, x[r * tree : (r + 1) * tree], (((0,), (0,)), ((), ())),
+                preferred_element_type=F32,
+            )
+        )
+    return rows
+
+
+def columns_kernel(mdl_ref, acc_ref, w_hbm, tok_hbm, mine_ref, send_ref, tok_out, tok, sems, sem):
     count, _, cols = mine_ref.shape
+    get = pltpu.make_async_copy(
+        tok_hbm.at[:, pl.ds(pl.multiple_of(mdl_ref[0] * cols, 128), cols)], tok, sem
+    )
+    get.start()
     copies = []
     for i in range(count):
         there = lax.rem(mdl_ref[0] // 2 + i, count)
@@ -481,21 +428,73 @@
             c = pltpu.make_async_copy(w_hbm.at[:, pl.ds(start, cols)], ref.at[i], sems.at[j, i])
             c.start()
             copies.append(c)
+    get.wait()
+    for r, row in enumerate(pick(acc_ref, tok[...], tok.shape[0] // acc_ref.shape[0])):
+        tok_out[r] = row
     for c in copies:
         c.wait()
 
 
-def columns_call(mdl, w_out, count):
+def columns_call(mdl, accepted, w_out, tokens, count):
     cols = w_out.shape[1] // (2 * count)
     return pl.pallas_call(
         columns_kernel,
-        in_specs=[SMEM, HBM],
-        out_specs=[VM, VM],
-        out_shape=[jax.ShapeDtypeStruct((count, w_out.shape[0], cols), BF16)] * 2,
-        scratch_shapes=[pltpu.SemaphoreType.DMA((2, count))],
-        compiler_params=params(8),
+        in_specs=[SMEM, VM, HBM, HBM],
+        out_specs=[VM, VM, VM],
+        out_shape=[jax.ShapeDtypeStruct((count, w_out.shape[0], cols), BF16)] * 2
+        + [jax.ShapeDtypeStruct(accepted.shape + (cols,), F32)],
+        scratch_shapes=[
+            pltpu.VMEM((tokens.shape[0], cols), BF16),
+            pltpu.SemaphoreType.DMA((2, count)),
+            pltpu.SemaphoreType.DMA,
+        ],
+        compiler_params=params(12),
         name="out_columns",
-    )(mdl, w_out)
+    )(mdl, accepted, w_out, tokens)
+
+
+def first_kernel(mine_ref, w_ref, out_ref):
+    out_ref[...] = dot(mine_ref[...], w_ref[0])
+
+
+def out_first(mine, w_mine, shift):
+    rows, inner = mine.shape
+    cols = w_mine.shape[2]
+    return pl.pallas_call(
+        first_kernel,
+        grid=(1,),
+        in_specs=[
+            pl.BlockSpec((rows, inner), lambda i: (0, 0)),
+            pl.BlockSpec((1, inner, cols), lambda i: (shift, 0, 0)),
+        ],
+        out_specs=pl.BlockSpec((rows, cols), lambda i: (0, 0)),
+        out_shape=jax.ShapeDtypeStruct((rows, cols), F32),
+        compiler_params=params(12),
+        name="out_first",
+    )(mine, w_mine)
+
+
+def second_kernel(first_ref, other_ref, w_ref, out_ref):
+    out_ref[...] = (first_ref[...] + dot(other_ref[...], w_ref[0])).astype(BF16)
+
+
+def out_second(first, other, w_other, shift):
+    rows, inner = other.shape
+    cols = w_other.shape[2]
+    flat = lambda i: (0, 0)
+    return pl.pallas_call(
+        second_kernel,
+        grid=(1,),
+        in_specs=[
+            pl.BlockSpec((rows, cols), flat),
+            pl.BlockSpec((rows, inner), flat),
+            pl.BlockSpec((1, inner, cols), lambda i: (shift, 0, 0)),
+        ],
+        out_specs=pl.BlockSpec((rows, cols), flat),
+        out_shape=jax.ShapeDtypeStruct((rows, cols), BF16),
+        compiler_params=params(12),
+        name="out_second",
+    )(first, other, w_other)
 
 
 def out_kernel(mine_ref, other_ref, *refs):
@@ -520,47 +519,27 @@
     )(mine, other, *([w_mine] * len(shifts)), *([w_other] * len(shifts)))
 
 
-def last_kernel(acc_ref, at_ref, own_ref, a_ref, b_ref, c_ref, tok_hbm, out_ref, rows_ref, tok, sums, kept, sem):
-    cols = own_ref.shape[1]
-    requests, most = acc_ref.shape
-    tree = own_ref.shape[0] // requests
-    get = pltpu.make_async_copy(
-        tok_hbm.at[:, pl.ds(pl.multiple_of(at_ref[0] * cols, 128), cols)], tok, sem
-    )
-    get.start()
+def last_kernel(acc_ref, own_ref, a_ref, b_ref, c_ref, tok_ref, out_ref, rows_ref):
     total = own_ref[...] + a_ref[...].astype(F32) + b_ref[...].astype(F32) + c_ref[...].astype(F32)
     rounded = total.astype(BF16)
     out_ref[...] = rounded
-    get.wait()
-    sums[...] = tok[...].astype(F32) + rounded.astype(F32)
-    for r in range(requests):
-        for k in range(most):
-            slot = acc_ref[r, k]
-            row = sums[pl.ds(r * tree + jnp.maximum(slot, 0), 1), :]
-            kept[r, pl.ds(k, 1), :] = jnp.where(slot >= 0, row, 0.0)
-    rows_ref[...] = kept[...].astype(BF16)
-
-
-def last_call(accepted, column, own, a, b, c, tokens):
+    for r, row in enumerate(pick(acc_ref, rounded, own_ref.shape[0] // acc_ref.shape[0])):
+        rows_ref[r] = (tok_ref[r] + row).astype(BF16)
+
+
+def last_call(accepted, own, a, b, c, picked):
     rows, cols = own.shape
-    requests, most = accepted.shape
     return pl.pallas_call(
         last_kernel,
-        in_specs=[SMEM, SMEM, VM, VM, VM, VM, HBM],
+        in_specs=[VM] * 6,
         out_specs=[VM, VM],
         out_shape=[
             jax.ShapeDtypeStruct((rows, cols), BF16),
-            jax.ShapeDtypeStruct((requests, most, cols), BF16),
-        ],
-        scratch_shapes=[
-            pltpu.VMEM((rows, cols), BF16),
-            pltpu.VMEM((rows, cols), F32),
-            pltpu.VMEM((requests, most, cols), F32),
-            pltpu.SemaphoreType.DMA,
+            jax.ShapeDtypeStruct(picked.shape, BF16),
         ],
         compiler_params=params(8),
         name="last_sums",
-    )(accepted, column, own, a, b, c, tokens)
+    )(accepted, own, a, b, c, picked)
 
 
 def shards(
@@ -605,46 +584,51 @@
     exponent = np.arange(hd // 2, dtype=np.float64) * (2.0 / hd)
     inverse = jnp.asarray(np.tile(THETA**-exponent, 2)[None, :], dtype=F32)
     table = ancestors.reshape(rows, tree)
-    q, normed, turn = query_call(
+    q, new_k, new_v = project_call(
         *map(
             in_hbm,
-            (cache_length, tokens, norm_gain.reshape(-1, hd), w_query, table, inverse),
+            (
+                cache_length, tokens, norm_gain.reshape(-1, hd), w_query, w_key, w_value, table,
+                inverse,
+            ),
         )
     )
     shifts = (2, 1, -1)
     q_far = [along_z(q, n) for n in shifts]
-    own = tree_call(*map(in_hbm, (normed, w_key, w_value, turn)), q, in_hbm(table))
+
+    w_mine, w_send, picked = columns_call(mdl_at, accepted, in_hbm(w_out), in_hbm(tokens), n_x)
+    w_other = other_core(w_send)
 
     k_half, v_half = halves_call(kv_r, kv_l)
     k_o = along_y(k_half, 1)
     v_o = along_y(v_half, -1)
     prompts = (kv, kv_r, kv_l, k_o, v_o)
 
-    w_mine, w_send = columns_call(mdl_at, in_hbm(w_out), n_x)
-    w_other = other_core(w_send)
-
     turns = [n % n_z * n_y for n in shifts]
     nears = near_call(
         request_group, tok_at, q_far, kv, in_hbm(kv_r), in_hbm(kv_l), requests, turns, n_tok
     )
-    parts = far_call(request_group, tok_at, nears, q_far, k_o, v_o, requests, turns, n_tok)
+    parts = []
+    for some in (slice(0, 1), slice(1, 3)):
+        parts += far_call(
+            request_group, tok_at, nears[some], q_far[some], k_o, v_o, requests, turns[some],
+            n_tok,
+        )
     back = [along_z(part, -n) for n, part in zip(shifts, parts)]
     home = home_call(
-        request_group, tok_at, cache_length, q, prompts, in_hbm(own),
+        request_group, tok_at, cache_length, q, prompts, new_k, new_v, in_hbm(table),
         in_hbm(squeeze(cache_keys)), in_hbm(squeeze(cache_values)),
     )
     attended = merge_call(home, *back, requests, rows)
 
     attended_other = other_core(attended)
-    sent = []
-    for group in ((2,), (1, -1), (0,)):
-        outs = out_call(
-            attended, attended_other, w_mine, w_other, [n % n_x for n in group],
-            F32 if group == (0,) else BF16,
-        )
-        sent += [along_x(o, n) if n else o for o, n in zip(outs, group)]
-    far, up, down, own_sum = sent
-    return tuple(last_call(accepted, mdl_at, own_sum, far, up, down, in_hbm(tokens)))
+    first = out_first(attended, w_mine, 2)
+    far = along_x(out_second(first, attended_other, w_other, 2), 2)
+    up, down = out_call(attended, attended_other, w_mine, w_other, (1, n_x - 1), BF16)
+    up = along_x(up, 1)
+    down = along_x(down, -1)
+    (own_sum,) = out_call(attended, attended_other, w_mine, w_other, (0,), F32)
+    return tuple(last_call(accepted, own_sum, far, up, down, picked))
 
 
 def solution(mesh):

time: 102 us -> 92.7 us (0.909)
  Pallas kernels: 42.7 us -> 37.5 us
  waiting for transfers between devices: 29.1 us -> 24.6 us
    pallas_call x5 -> x6, Pallas kernels: 28 us -> 22.9 us  [the longest x1 8.77 us: project_call(): pl.pallas_call(project_kernel, in_specs=[HBM] * 8, out_specs=[VM, VM, VM]...]
    ppermute x4, waiting for transfers between devices: 9.25 us -> 5.27 us  [along_y(): return lax.ppermute(v, 'tok', perm)]
    ppermute x6, waiting for transfers between devices: 10.2 us -> 7.45 us  [along_z(): lax.ppermute(v, 'tok', [(t, (t + n * n_y) % n_tok) for t in range(n_tok)])]
    ppermute x3, waiting for transfers between devices: 8.09 us -> 10.7 us  [along_x(): lax.ppermute(v, 'mdl', [(m, (m + 2 * n) % n_mdl) for m in range(n_mdl)])]
    ppermute x6, starting transfers between devices: 12.1 us -> 13.9 us  [along_z(): lax.ppermute(v, 'tok', [(t, (t + n * n_y) % n_tok) for t in range(n_tok)])]
    pallas_call x3 -> x2, Pallas kernels: 5.58 us -> 3.93 us  [out_call(): pl.pallas_call(out_kernel, grid=(1,), in_specs=[whole, whole] + chunks *...]
    pallas_call x1 -> x2, Pallas kernels: 2.43 us -> 3.95 us  [far_call(): pl.pallas_call(lambda *refs: far_kernel(*refs, requests=requests, shifts=...]
    ppermute x3, starting transfers between devices: 6.41 us -> 5.2 us  [along_x(): lax.ppermute(v, 'mdl', [(m, (m + 2 * n) % n_mdl) for m in range(n_mdl)])]
  transfers between devices with their start and end apart: 15 -> 15, of which waited for: 8 -> 8; matrix products, arithmetic and copies ran while one was open for 0% -> 0% of each run, Pallas kernels for 34% -> 33%
where the time goes in v2:
time: 92.7 us; the launch traced here: 92.2 us
  Pallas kernels  37.5 us (40%)
  starting transfers between devices  25.8 us (28%)
  waiting for transfers between devices  24.6 us (27%)
  local copies, waits for them, and re-layouts  3.46 us (4%)
    ppermute x6, starting transfers between devices, along_z(): lax.ppermute(v, 'tok', [(t, (t + n * n_y) % n_tok) for t in range(n_tok)])  13.9 us
    ppermute x3, waiting for transfers between devices, along_x(): lax.ppermute(v, 'mdl', [(m, (m + 2 * n) % n_mdl) for m in range(n_mdl)])  10.7 us
    pallas_call x1, Pallas kernels, project_call(): pl.pallas_call(project_kernel, in_specs=[HBM] * 8, out_specs=[VM, VM, VM]...  8.77 us
    ppermute x6, waiting for transfers between devices, along_z(): lax.ppermute(v, 'tok', [(t, (t + n * n_y) % n_tok) for t in range(n_tok)])  7.45 us
    pallas_call x1, Pallas kernels, home_call(): pl.pallas_call(home_kernel, in_specs=[SMEM, SMEM, SMEM] + [VM] * 8 + [HBM...  7.19 us
    ppermute x4, starting transfers between devices, along_y(): return lax.ppermute(v, 'tok', perm)  6.54 us
    ppermute x4, waiting for transfers between devices, along_y(): return lax.ppermute(v, 'tok', perm)  5.27 us
    ppermute x3, starting transfers between devices, along_x(): lax.ppermute(v, 'mdl', [(m, (m + 2 * n) % n_mdl) for m in range(n_mdl)])  5.2 us
  transfers between devices with their start and end apart: 15, of which 8 were waited for; matrix products, arithmetic and copies ran while one was open for 0% of the time, Pallas kernels for 33%

profile of v2, /device:TPU:0, one launch (start us, length us, event | category | flops | bytes accessed | tf_op | source)
XLA Modules:
  0.0 92.2 jit_solution(8856845408668312766)
XLA Ops:
  1.3 4.2 %out_columns.1 = (bf16[4,512,640]{2,1,0:T(8,128)(2,1)S(1)}, bf16[4,512,640]{2,1,0:T(8,128)(2,1)}, f32[8,8,640]{2,1,0:T(8,128)S(1)}) custom-call(s32[1]{0:T(128)} %bitcast.7.mdl_ref, s32[8,8]{1,0:T(8,128)S(1)} %copy-done.9, bf16[512,5120]{1,0:T(8,128)(2,1)} %w_hbm.1, bf16[256,5120]{1,0:T(8,128)(2,1)} %tok_hbm.3), custom_call_target="tpu_custom_call" | custom-call | tf_op jit(solution)/shard_map/out_columns/pallas_call | solution.py:440
  6.8 1.8 %collective-permute-start = (bf16[12,256,128]{2,1,0:T(8,128)(2,1)S(1)}, bf16[12,256,128]{2,1,0:T(8,128)(2,1)S(1)}, u32[]{:S(2)}, u32[]{:S(2)}) collective-permute-start(bf16[12,256,128]{2,1,0:T(8,128)(2,1)S(1)} %join.1.kv.refs_2_), channel_id=1, source_target_pairs={{0,8},{8,16},{16,24},{24,0},{32,40},{40,48},{48,56},{56,32},{64,72... | collective-permute-start | bytes 2359304 | tf_op jit(solution)/shard_map/ppermute | solution.py:562
  10.1 8.8 %projections.1 = (bf16[1024,128]{1,0:T(8,128)(2,1)}, bf16[256,128]{1,0:T(8,128)(2,1)S(1)}, bf16[256,128]{1,0:T(8,128)(2,1)S(1)}) custom-call(s32[8]{0:T(128)} %len_ref.1, bf16[256,5120]{1,0:T(8,128)(2,1)} %tok_hbm.3, bf16[40,128]{1,0:T(8,128)(2,1)} %bitcast.14, bf16[5120,512]{1,0:T(8,128)(2,1)} %wq_hbm.1, bf16[5120,128]{1,0:T(8,128)(2,1)} %wk_hbm.1, ...), custom_call_target="tpu_custom_call" | custom-call | tf_op jit(solution)/shard_map/projections/pallas_call | solution.py:120
  18.9 4.1 %collective-permute-start.4 = (bf16[1024,128]{1,0:T(8,128)(2,1)}, bf16[1024,128]{1,0:T(8,128)(2,1)S(1)}, u32[]{:S(2)}, u32[]{:S(2)}) collective-permute-start(bf16[1024,128]{1,0:T(8,128)(2,1)} %get-tuple-element.17.q_ref), channel_id=1, source_target_pairs={{0,64},{8,72},{16,80},{24,88},{32,96},{40,104},{48,112},{56,120},{... | collective-permute-start | bytes 786440 | tf_op jit(solution)/shard_map/ppermute | solution.py:565
  22.9 5.2 %collective-permute-done.right_ref.kv_r.refs_3_ = bf16[12,256,128]{2,1,0:T(8,128)(2,1)S(1)} collective-permute-done((bf16[12,256,128]{2,1,0:T(8,128)(2,1)S(1)}, bf16[12,256,128]{2,1,0:T(8,128)(2,1)S(1)}, u32[]{:S(2)}, u32[]{:S(2)}) %collective-permute-start) | collective-permute-done | bytes 786464 | tf_op jit(solution)/shard_map/ppermute | solution.py:562
  30.3 1.6 %collective-permute-start.2 = (bf16[6,256,128]{2,1,0:T(8,128)(2,1)}, bf16[6,256,128]{2,1,0:T(8,128)(2,1)}, u32[]{:S(2)}, u32[]{:S(2)}) collective-permute-start(bf16[6,256,128]{2,1,0:T(8,128)(2,1)} %get-tuple-element.18), channel_id=1, source_target_pairs={{0,8},{8,16},{16,24},{24,0},{32,40},{40,48},{48,56},{56,32},{64,72... | collective-permute-start | bytes 1179656 | tf_op jit(solution)/shard_map/ppermute | solution.py:562
  31.9 1.7 %collective-permute-start.3 = (bf16[6,256,128]{2,1,0:T(8,128)(2,1)}, bf16[6,256,128]{2,1,0:T(8,128)(2,1)}, u32[]{:S(2)}, u32[]{:S(2)}) collective-permute-start(bf16[6,256,128]{2,1,0:T(8,128)(2,1)} %get-tuple-element.19), channel_id=1, source_target_pairs={{0,24},{8,0},{16,8},{24,16},{32,56},{40,32},{48,40},{56,48},{64,88... | collective-permute-start | bytes 1179656 | tf_op jit(solution)/shard_map/ppermute | solution.py:562
  33.6 1.9 %collective-permute-start.5 = (bf16[1024,128]{1,0:T(8,128)(2,1)}, bf16[1024,128]{1,0:T(8,128)(2,1)}, u32[]{:S(2)}, u32[]{:S(2)}) collective-permute-start(bf16[1024,128]{1,0:T(8,128)(2,1)} %get-tuple-element.17.q_ref), channel_id=1, source_target_pairs={{0,32},{8,40},{16,48},{24,56},{32,64},{40,72},{48,80},{56,88},{64,... | collective-permute-start | bytes 786440 | tf_op jit(solution)/shard_map/ppermute | solution.py:565
  36.2 2.1 %collective-permute-start.6 = (bf16[1024,128]{1,0:T(8,128)(2,1)}, bf16[1024,128]{1,0:T(8,128)(2,1)}, u32[]{:S(2)}, u32[]{:S(2)}) collective-permute-start(bf16[1024,128]{1,0:T(8,128)(2,1)} %get-tuple-element.17.q_ref), channel_id=1, source_target_pairs={{0,96},{8,104},{16,112},{24,120},{32,0},{40,8},{48,16},{56,24},{64... | collective-permute-start | bytes 786440 | tf_op jit(solution)/shard_map/ppermute | solution.py:565
  38.4 5.2 %collective-permute-done.5.refs_6_.refs_4_ = bf16[1024,128]{1,0:T(8,128)(2,1)} collective-permute-done((bf16[1024,128]{1,0:T(8,128)(2,1)}, bf16[1024,128]{1,0:T(8,128)(2,1)}, u32[]{:S(2)}, u32[]{:S(2)}) %collective-permute-start.5) | collective-permute-done | bytes 262176 | tf_op jit(solution)/shard_map/ppermute | solution.py:565
  44.7 4.3 %prompt_near.1 = (f32[1024,256]{1,0:T(8,128)S(1)}, f32[1024,256]{1,0:T(8,128)S(1)}, f32[1024,256]{1,0:T(8,128)S(1)}) custom-call(s32[128]{0:T(128)S(1)} %copy-done.11, s32[1]{0:T(128)} %bitcast.at_ref.refs_1_, bf16[12,256,128]{2,1,0:T(8,128)(2,1)S(1)} %join.1.kv.refs_2_, bf16[12,256,128]{2,1,0:T(8,128)(2,1)} %copy-done, bf16[12,256,128]{2,1,0:T(8,128)(2,1)} %copy-done.2, ...), custom_call_target="tpu_custom_call" | custom-call | tf_op jit(solution)/shard_map/prompt_near/pallas_call | solution.py:218
  49.1 2.3 %prompt_far.3 = (bf16[1040,128]{1,0:T(8,128)(2,1)S(1)}, bf16[1040,128]{1,0:T(8,128)(2,1)S(1)}) custom-call(s32[128]{0:T(128)S(1)} %copy-done.11, s32[1]{0:T(128)} %bitcast.at_ref.refs_1_, bf16[6,256,128]{2,1,0:T(8,128)(2,1)} %collective-permute-done.2.k_o.refs_2_, bf16[6,256,128]{2,1,0:T(8,128)(2,1)} %collective-permute-done.3.v_o.refs_3_, ...), custom_call_target="tpu_custom_call" | custom-call | tf_op jit(solution)/shard_map/prompt_far/pallas_call | solution.py:255
  51.3 3.5 %collective-permute-start.8 = (bf16[1040,128]{1,0:T(8,128)(2,1)S(1)}, bf16[1040,128]{1,0:T(8,128)(2,1)S(1)}, u32[]{:S(2)}, u32[]{:S(2)}) collective-permute-start(bf16[1040,128]{1,0:T(8,128)(2,1)S(1)} %get-tuple-element.25), channel_id=1, source_target_pairs={{0,96},{8,104},{16,112},{24,120},{32,0},{40,8},{48,16},{56,24},{64... | collective-permute-start | bytes 798728 | tf_op jit(solution)/shard_map/ppermute | solution.py:565
  54.8 1.7 %prompt_far.2 = bf16[1040,128]{1,0:T(8,128)(2,1)S(1)} custom-call(s32[128]{0:T(128)S(1)} %copy-done.11, s32[1]{0:T(128)} %bitcast.at_ref.refs_1_, bf16[6,256,128]{2,1,0:T(8,128)(2,1)} %collective-permute-done.2.k_o.refs_2_, bf16[6,256,128]{2,1,0:T(8,128)(2,1)} %collective-permute-done.3.v_o.refs_3_, bf16[1024,128]{1,0:T(8,128)(2,1)S(1)} %copy-done.6, ...), custom_call_target="tpu_custom_call" | custom-call | tf_op jit(solution)/shard_map/prompt_far/pallas_call | solution.py:255
  56.5 2.3 %collective-permute-start.7 = (bf16[1040,128]{1,0:T(8,128)(2,1)S(1)}, bf16[1040,128]{1,0:T(8,128)(2,1)S(1)}, u32[]{:S(2)}, u32[]{:S(2)}) collective-permute-start(bf16[1040,128]{1,0:T(8,128)(2,1)S(1)} %prompt_far.2), channel_id=1, source_target_pairs={{0,64},{8,72},{16,80},{24,88},{32,96},{40,104},{48,112},{56,120},{... | collective-permute-start | bytes 798728 | tf_op jit(solution)/shard_map/ppermute | solution.py:565
  58.8 7.2 %home_attention.1.refs_0_ = f32[1024,256]{1,0:T(8,128)S(1)} custom-call(s32[128]{0:T(128)S(1)} %copy-done.11, s32[1]{0:T(128)} %bitcast.at_ref.refs_1_, s32[8]{0:T(128)S(1)} %copy-done.12, bf16[1024,128]{1,0:T(8,128)(2,1)} %get-tuple-element.17.q_ref, bf16[12,256,128]{2,1,0:T(8,128)(2,1)S(1)} %join.1.kv.refs_2_, bf16[12,256,128]{2,1,0:T(8,128)(2,1)S(1)} %copy-done.1, ...), custom_call_target="tpu_custom_call" | custom-call | tf_op jit(solution)/shard_map/home_attention/pallas_call | solution.py:345
  66.0 2.0 %collective-permute-done.9.refs_3_ = bf16[1040,128]{1,0:T(8,128)(2,1)S(1)} collective-permute-done((bf16[1040,128]{1,0:T(8,128)(2,1)S(1)}, bf16[1040,128]{1,0:T(8,128)(2,1)S(1)}, u32[]{:S(2)}, u32[]{:S(2)}) %collective-permute-start.9) | collective-permute-done | bytes 266272 | tf_op jit(solution)/shard_map/ppermute | solution.py:565
  69.9 2.3 %out_proj.3 = (bf16[256,640]{1,0:T(8,128)(2,1)S(1)}, bf16[256,640]{1,0:T(8,128)(2,1)S(1)}) custom-call(bf16[256,512]{1,0:T(8,128)(2,1)S(1)} %merge.1.mine_ref, bf16[256,512]{1,0:T(8,128)(2,1)S(1)} %collective-permute-done.10.other_ref, bf16[4,512,640]{2,1,0:T(8,128)(2,1)S(1)} %get-tuple-element.27.refs_0_.w_ref.refs_1_, ...), custom_call_target="tpu_custom_call" | custom-call | tf_op jit(solution)/shard_map/out_proj/pallas_call | solution.py:511
  73.7 1.7 %collective-permute-start.14 = (bf16[256,640]{1,0:T(8,128)(2,1)S(1)}, bf16[256,640]{1,0:T(8,128)(2,1)S(1)}, u32[]{:S(2)}, u32[]{:S(2)}) collective-permute-start(bf16[256,640]{1,0:T(8,128)(2,1)S(1)} %get-tuple-element.30), channel_id=1, source_target_pairs={{0,6},{1,7},{2,0},{3,1},{4,2},{5,3},{6,4},{7,5},{8,14},{9,15},{10,... | collective-permute-start | bytes 983048 | tf_op jit(solution)/shard_map/ppermute | solution.py:568
  77.0 1.9 %collective-permute-start.12 = (bf16[256,640]{1,0:T(8,128)(2,1)S(1)}, bf16[256,640]{1,0:T(8,128)(2,1)S(1)}, u32[]{:S(2)}, u32[]{:S(2)}) collective-permute-start(bf16[256,640]{1,0:T(8,128)(2,1)S(1)} %out_second.1), channel_id=1, source_target_pairs={{0,4},{1,5},{2,6},{3,7},{4,0},{5,1},{6,2},{7,3},{8,12},{9,13},{10,... | collective-permute-start | bytes 983048 | tf_op jit(solution)/shard_map/ppermute | solution.py:568
  78.9 1.7 %out_proj.2.own_ref = f32[256,640]{1,0:T(8,128)S(1)} custom-call(bf16[256,512]{1,0:T(8,128)(2,1)S(1)} %merge.1.mine_ref, bf16[256,512]{1,0:T(8,128)(2,1)S(1)} %collective-permute-done.10.other_ref, bf16[4,512,640]{2,1,0:T(8,128)(2,1)S(1)} %get-tuple-element.27.refs_0_.w_ref.refs_1_, bf16[4,512,640]{2,1,0:T(8,128)(2,1)} %collective-permute-done.11.refs_1_.w_ref.refs_2_.refs_3_), custom_call_target="tpu_custom_call" | custom-call | tf_op jit(solution)/shard_map/out_proj/pallas_call | solution.py:511
  80.5 2.7 %collective-permute-done.13.b_ref = bf16[256,640]{1,0:T(8,128)(2,1)S(1)} collective-permute-done((bf16[256,640]{1,0:T(8,128)(2,1)S(1)}, bf16[256,640]{1,0:T(8,128)(2,1)S(1)}, u32[]{:S(2)}, u32[]{:S(2)}) %collective-permute-start.13) | collective-permute-done | bytes 327712 | tf_op jit(solution)/shard_map/ppermute | solution.py:568
  83.2 6.3 %collective-permute-done.14.c_ref = bf16[256,640]{1,0:T(8,128)(2,1)S(1)} collective-permute-done((bf16[256,640]{1,0:T(8,128)(2,1)S(1)}, bf16[256,640]{1,0:T(8,128)(2,1)S(1)}, u32[]{:S(2)}, u32[]{:S(2)}) %collective-permute-start.14) | collective-permute-done | bytes 327712 | tf_op jit(solution)/shard_map/ppermute | solution.py:568
  89.5 1.7 %collective-permute-done.12.a_ref = bf16[256,640]{1,0:T(8,128)(2,1)S(1)} collective-permute-done((bf16[256,640]{1,0:T(8,128)(2,1)S(1)}, bf16[256,640]{1,0:T(8,128)(2,1)S(1)}, u32[]{:S(2)}, u32[]{:S(2)}) %collective-permute-start.12) | collective-permute-done | bytes 327712 | tf_op jit(solution)/shard_map/ppermute | solution.py:568
  (46 shorter events, 13.4 us)
Async XLA Ops:
  5.5 1.2 %copy-start.7 = (f32[8,8,640]{2,1,0:T(8,128)}, f32[8,8,640]{2,1,0:T(8,128)S(1)}, u32[]{:S(2)}) copy-start(f32[8,8,640]{2,1,0:T(8,128)S(1)} %get-tuple-element.31.tok_ref) | copy-start | bytes 491524
  5.6 64.4 %collective-permute-start.11 = (bf16[4,512,640]{2,1,0:T(8,128)(2,1)}, bf16[4,512,640]{2,1,0:T(8,128)(2,1)}, u32[]{:S(2)}, u32[]{:S(2)}) collective-permute-start(bf16[4,512,640]{2,1,0:T(8,128)(2,1)} %get-tuple-element.28), channel_id=1, source_target_pairs={{0,1},{1,0},{2,3},{3,2},{4,5},{5,4},{6,7},{7,6},{8,9},{9,8},{10,11... | collective-permute-start | bytes 7864328 | tf_op jit(solution)/shard_map/ppermute | solution.py:571
  6.8 21.4 %collective-permute-start = (bf16[12,256,128]{2,1,0:T(8,128)(2,1)S(1)}, bf16[12,256,128]{2,1,0:T(8,128)(2,1)S(1)}, u32[]{:S(2)}, u32[]{:S(2)}) collective-permute-start(bf16[12,256,128]{2,1,0:T(8,128)(2,1)S(1)} %join.1.kv.refs_2_), channel_id=1, source_target_pairs={{0,8},{8,16},{16,24},{24,0},{32,40},{40,48},{48,56},{56,32},{64,72... | collective-permute-start | bytes 2359304 | tf_op jit(solution)/shard_map/ppermute | solution.py:562
  8.6 19.7 %collective-permute-start.1 = (bf16[12,256,128]{2,1,0:T(8,128)(2,1)S(1)}, bf16[12,256,128]{2,1,0:T(8,128)(2,1)S(1)}, u32[]{:S(2)}, u32[]{:S(2)}) collective-permute-start(bf16[12,256,128]{2,1,0:T(8,128)(2,1)S(1)} %join.1.kv.refs_2_), channel_id=1, source_target_pairs={{0,24},{8,0},{16,8},{24,16},{32,56},{40,32},{48,40},{56,48},{64,88... | collective-permute-start | bytes 2359304 | tf_op jit(solution)/shard_map/ppermute | solution.py:562
  10.1 33.7 %copy-start.11 = (s32[128]{0:T(128)S(1)}, s32[128]{0:T(128)}, u32[]{:S(2)}) copy-start(s32[128]{0:T(128)} %refs_0_.5) | copy-start | bytes 1540
  18.9 16.6 %collective-permute-start.4 = (bf16[1024,128]{1,0:T(8,128)(2,1)}, bf16[1024,128]{1,0:T(8,128)(2,1)S(1)}, u32[]{:S(2)}, u32[]{:S(2)}) collective-permute-start(bf16[1024,128]{1,0:T(8,128)(2,1)} %get-tuple-element.17.q_ref), channel_id=1, source_target_pairs={{0,64},{8,72},{16,80},{24,88},{32,96},{40,104},{48,112},{56,120},{... | collective-permute-start | bytes 786440 | tf_op jit(solution)/shard_map/ppermute | solution.py:565
  28.2 1.2 %copy-start.2 = (bf16[12,256,128]{2,1,0:T(8,128)(2,1)}, bf16[12,256,128]{2,1,0:T(8,128)(2,1)S(1)}, u32[]{:S(2)}) copy-start(bf16[12,256,128]{2,1,0:T(8,128)(2,1)S(1)} %collective-permute-done.1.left_ref.kv_l.refs_4_) | copy-start | bytes 2359300
  30.3 18.7 %collective-permute-start.2 = (bf16[6,256,128]{2,1,0:T(8,128)(2,1)}, bf16[6,256,128]{2,1,0:T(8,128)(2,1)}, u32[]{:S(2)}, u32[]{:S(2)}) collective-permute-start(bf16[6,256,128]{2,1,0:T(8,128)(2,1)} %get-tuple-element.18), channel_id=1, source_target_pairs={{0,8},{8,16},{16,24},{24,0},{32,40},{40,48},{48,56},{56,32},{64,72... | collective-permute-start | bytes 1179656 | tf_op jit(solution)/shard_map/ppermute | solution.py:562
  31.9 17.1 %collective-permute-start.3 = (bf16[6,256,128]{2,1,0:T(8,128)(2,1)}, bf16[6,256,128]{2,1,0:T(8,128)(2,1)}, u32[]{:S(2)}, u32[]{:S(2)}) collective-permute-start(bf16[6,256,128]{2,1,0:T(8,128)(2,1)} %get-tuple-element.19), channel_id=1, source_target_pairs={{0,24},{8,0},{16,8},{24,16},{32,56},{40,32},{48,40},{56,48},{64,88... | collective-permute-start | bytes 1179656 | tf_op jit(solution)/shard_map/ppermute | solution.py:562
  33.6 9.9 %collective-permute-start.5 = (bf16[1024,128]{1,0:T(8,128)(2,1)}, bf16[1024,128]{1,0:T(8,128)(2,1)}, u32[]{:S(2)}, u32[]{:S(2)}) collective-permute-start(bf16[1024,128]{1,0:T(8,128)(2,1)} %get-tuple-element.17.q_ref), channel_id=1, source_target_pairs={{0,32},{8,40},{16,48},{24,56},{32,64},{40,72},{48,80},{56,88},{64,... | collective-permute-start | bytes 786440 | tf_op jit(solution)/shard_map/ppermute | solution.py:565
  36.2 7.5 %collective-permute-start.6 = (bf16[1024,128]{1,0:T(8,128)(2,1)}, bf16[1024,128]{1,0:T(8,128)(2,1)}, u32[]{:S(2)}, u32[]{:S(2)}) collective-permute-start(bf16[1024,128]{1,0:T(8,128)(2,1)} %get-tuple-element.17.q_ref), channel_id=1, source_target_pairs={{0,96},{8,104},{16,112},{24,120},{32,0},{40,8},{48,16},{56,24},{64... | collective-permute-start | bytes 786440 | tf_op jit(solution)/shard_map/ppermute | solution.py:565
  44.7 10.1 %copy-start.6 = (bf16[1024,128]{1,0:T(8,128)(2,1)S(1)}, bf16[1024,128]{1,0:T(8,128)(2,1)}, u32[]{:S(2)}) copy-start(bf16[1024,128]{1,0:T(8,128)(2,1)} %copy-done.4) | copy-start | bytes 786436
  49.0 9.8 %copy-start.1 = (bf16[12,256,128]{2,1,0:T(8,128)(2,1)S(1)}, bf16[12,256,128]{2,1,0:T(8,128)(2,1)}, u32[]{:S(2)}) copy-start(bf16[12,256,128]{2,1,0:T(8,128)(2,1)} %copy-done) | copy-start | bytes 2359300
  49.0 9.7 %copy-start.3 = (bf16[12,256,128]{2,1,0:T(8,128)(2,1)S(1)}, bf16[12,256,128]{2,1,0:T(8,128)(2,1)}, u32[]{:S(2)}) copy-start(bf16[12,256,128]{2,1,0:T(8,128)(2,1)} %copy-done.2) | copy-start | bytes 2359300
  49.1 9.7 %copy-start.12 = (s32[8]{0:T(128)S(1)}, s32[8]{0:T(128)}, u32[]{:S(2)}) copy-start(s32[8]{0:T(128)} %len_ref.1) | copy-start | bytes 100
  51.3 14.7 %collective-permute-start.8 = (bf16[1040,128]{1,0:T(8,128)(2,1)S(1)}, bf16[1040,128]{1,0:T(8,128)(2,1)S(1)}, u32[]{:S(2)}, u32[]{:S(2)}) collective-permute-start(bf16[1040,128]{1,0:T(8,128)(2,1)S(1)} %get-tuple-element.25), channel_id=1, source_target_pairs={{0,96},{8,104},{16,112},{24,120},{32,0},{40,8},{48,16},{56,24},{64... | collective-permute-start | bytes 798728 | tf_op jit(solution)/shard_map/ppermute | solution.py:565
  54.8 13.2 %collective-permute-start.9 = (bf16[1040,128]{1,0:T(8,128)(2,1)S(1)}, bf16[1040,128]{1,0:T(8,128)(2,1)S(1)}, u32[]{:S(2)}, u32[]{:S(2)}) collective-permute-start(bf16[1040,128]{1,0:T(8,128)(2,1)S(1)} %get-tuple-element.26), channel_id=1, source_target_pairs={{0,32},{8,40},{16,48},{24,56},{32,64},{40,72},{48,80},{56,88},{64,... | collective-permute-start | bytes 798728 | tf_op jit(solution)/shard_map/ppermute | solution.py:565
  56.5 11.5 %collective-permute-start.7 = (bf16[1040,128]{1,0:T(8,128)(2,1)S(1)}, bf16[1040,128]{1,0:T(8,128)(2,1)S(1)}, u32[]{:S(2)}, u32[]{:S(2)}) collective-permute-start(bf16[1040,128]{1,0:T(8,128)(2,1)S(1)} %prompt_far.2), channel_id=1, source_target_pairs={{0,64},{8,72},{16,80},{24,88},{32,96},{40,104},{48,112},{56,120},{... | collective-permute-start | bytes 798728 | tf_op jit(solution)/shard_map/ppermute | solution.py:565
  68.3 1.6 %collective-permute-start.10 = (bf16[256,512]{1,0:T(8,128)(2,1)S(1)}, bf16[256,512]{1,0:T(8,128)(2,1)S(1)}, u32[]{:S(2)}, u32[]{:S(2)}) collective-permute-start(bf16[256,512]{1,0:T(8,128)(2,1)S(1)} %merge.1.mine_ref), channel_id=1, source_target_pairs={{0,1},{1,0},{2,3},{3,2},{4,5},{5,4},{6,7},{7,6},{8,9},{9,8},{10,11... | collective-permute-start | bytes 786440 | tf_op jit(solution)/shard_map/ppermute | solution.py:571
  72.2 11.0 %collective-permute-start.13 = (bf16[256,640]{1,0:T(8,128)(2,1)S(1)}, bf16[256,640]{1,0:T(8,128)(2,1)S(1)}, u32[]{:S(2)}, u32[]{:S(2)}) collective-permute-start(bf16[256,640]{1,0:T(8,128)(2,1)S(1)} %get-tuple-element.29), channel_id=1, source_target_pairs={{0,2},{1,3},{2,4},{3,5},{4,6},{5,7},{6,0},{7,1},{8,10},{9,11},{10,... | collective-permute-start | bytes 983048 | tf_op jit(solution)/shard_map/ppermute | solution.py:568
  73.7 15.8 %collective-permute-start.14 = (bf16[256,640]{1,0:T(8,128)(2,1)S(1)}, bf16[256,640]{1,0:T(8,128)(2,1)S(1)}, u32[]{:S(2)}, u32[]{:S(2)}) collective-permute-start(bf16[256,640]{1,0:T(8,128)(2,1)S(1)} %get-tuple-element.30), channel_id=1, source_target_pairs={{0,6},{1,7},{2,0},{3,1},{4,2},{5,3},{6,4},{7,5},{8,14},{9,15},{10,... | collective-permute-start | bytes 983048 | tf_op jit(solution)/shard_map/ppermute | solution.py:568
  77.0 14.3 %copy-start.8 = (f32[8,8,640]{2,1,0:T(8,128)S(1)}, f32[8,8,640]{2,1,0:T(8,128)}, u32[]{:S(2)}) copy-start(f32[8,8,640]{2,1,0:T(8,128)} %copy-done.7) | copy-start | bytes 491524
  77.0 14.3 %copy-start.10 = (s32[8,8]{1,0:T(8,128)S(1)}, s32[8,8]{1,0:T(8,128)}, u32[]{:S(2)}) copy-start(s32[8,8]{1,0:T(8,128)} %acc_ref.3) | copy-start | bytes 772
  77.0 14.2 %collective-permute-start.12 = (bf16[256,640]{1,0:T(8,128)(2,1)S(1)}, bf16[256,640]{1,0:T(8,128)(2,1)S(1)}, u32[]{:S(2)}, u32[]{:S(2)}) collective-permute-start(bf16[256,640]{1,0:T(8,128)(2,1)S(1)} %out_second.1), channel_id=1, source_target_pairs={{0,4},{1,5},{2,6},{3,7},{4,0},{5,1},{6,2},{7,3},{8,12},{9,13},{10,... | collective-permute-start | bytes 983048 | tf_op jit(solution)/shard_map/ppermute | solution.py:568
  (4 other events, 3.3 us)

commit v3 on v2

--- a/solution.py
+++ b/solution.py
@@ -19,7 +19,8 @@
 HBM = pl.BlockSpec(memory_space=pltpu.HBM)
 SMEM = pl.BlockSpec(memory_space=pltpu.SMEM)
 VM = pl.BlockSpec(memory_space=pltpu.VMEM)
-CHUNKS = 5
+CHUNKS = 4
+AHEAD = 1
 KB = 256
 PIECES = 2
 LANES = 8
@@ -60,18 +61,26 @@
     ]
     for c in firsts:
         c.start()
+    get_tok = pltpu.make_async_copy(tok_hbm, tok, sems.at[4])
+    get_tok.start()
     copies = []
     for i in range(CHUNKS):
         at = pl.ds(i * part, part)
-        four = (
-            pltpu.make_async_copy(tok_hbm.at[:, at], tok.at[:, at], csems.at[0, i]),
-            pltpu.make_async_copy(wq_hbm.at[at], w.at[at, pl.ds(0, inner)], csems.at[1, i]),
-            pltpu.make_async_copy(wk_hbm.at[at], w.at[at, pl.ds(inner, hd)], csems.at[2, i]),
-            pltpu.make_async_copy(wv_hbm.at[at], w.at[at, pl.ds(inner + hd, hd)], csems.at[3, i]),
-        )
-        for c in four:
-            c.start()
-        copies.append(four)
+        copies.append(
+            (
+                pltpu.make_async_copy(wq_hbm.at[at], w.at[at, pl.ds(0, inner)], csems.at[0, i]),
+                pltpu.make_async_copy(wk_hbm.at[at], w.at[at, pl.ds(inner, hd)], csems.at[1, i]),
+                pltpu.make_async_copy(wv_hbm.at[at], w.at[at, pl.ds(inner + hd, hd)], csems.at[2, i]),
+            )
+        )
+
+    def begin(i):
+        if i < CHUNKS:
+            for c in copies[i]:
+                c.start()
+
+    for i in range(AHEAD):
+        begin(i)
     for c in firsts:
         c.wait()
     depth = jnp.sum(table[...], axis=1, keepdims=True).astype(F32) - 1.0
@@ -88,29 +97,30 @@
     sine = jnp.sin(angles)
     sine = jnp.where(lane < hd // 2, -sine, sine)
     gains = gain[...].astype(F32)
-    step = part // gain.shape[1]
+    gains = jnp.concatenate([gains[i : i + 1] for i in range(gain.shape[0])], axis=1)
+    get_tok.wait()
+    begin(AHEAD)
+
+    wide = tok[...].astype(F32)
+    scale = lax.rsqrt(jnp.mean(wide * wide, axis=1, keepdims=True) + EPS)
     acc = None
-    squares = None
     for i in range(CHUNKS):
         for c in copies[i]:
             c.wait()
-        wide = tok[:, i * part : (i + 1) * part].astype(F32)
-        own_gain = jnp.concatenate([gains[j : j + 1] for j in range(i * step, (i + 1) * step)], axis=1)
-        d = dot((wide * own_gain).astype(BF16), w[i * part : (i + 1) * part, :])
+        begin(AHEAD + 1 + i)
+        at = slice(i * part, (i + 1) * part)
+        normed = (tok[:, at].astype(F32) * scale * gains[:, at]).astype(BF16)
+        d = dot(normed, w[at, :])
         acc = d if acc is None else acc + d
-        square = wide * wide
-        for j in range(step):
-            t = square[:, j * gain.shape[1] : (j + 1) * gain.shape[1]]
-            squares = t if squares is None else squares + t
-    scale = lax.rsqrt(jnp.sum(squares, axis=1, keepdims=True) * (1.0 / width) + EPS)
     heads = inner // hd
-    scaled = scale * (hd**-0.5 * math.log2(math.e))
+    fold = hd**-0.5 * math.log2(math.e)
     for g in range(heads):
-        turned = rotate(acc[:, g * hd : (g + 1) * hd] * scaled, cosine, sine).astype(BF16)
+        turned = rotate(acc[:, g * hd : (g + 1) * hd], cosine, sine)
+        turned = (turned * fold).astype(BF16)
         for r in range(requests):
             q_ref[pl.ds((r * heads + g) * tree, tree), :] = turned[r * tree : (r + 1) * tree]
-    k_ref[...] = rotate(acc[:, inner : inner + hd] * scale, cosine, sine).astype(BF16)
-    v_ref[...] = (acc[:, inner + hd :] * scale).astype(BF16)
+    k_ref[...] = rotate(acc[:, inner : inner + hd], cosine, sine).astype(BF16)
+    v_ref[...] = acc[:, inner + hd :].astype(BF16)
 
 
 def project_call(lengths, tokens, gain, w_query, w_key, w_value, ancestors, inverse):
@@ -133,8 +143,8 @@
             pltpu.VMEM((width, inner + 2 * hd), BF16),
             pltpu.VMEM(ancestors.shape, jnp.int32),
             pltpu.VMEM(inverse.shape, F32),
-            pltpu.SemaphoreType.DMA((4,)),
-            pltpu.SemaphoreType.DMA((4, CHUNKS)),
+            pltpu.SemaphoreType.DMA((5,)),
+            pltpu.SemaphoreType.DMA((3, CHUNKS)),
         ],
         compiler_params=params(28),
         name="projections",
@@ -165,20 +175,27 @@
     )(a, b)
 
 
-def halves_kernel(right_ref, left_ref, k_ref, v_ref):
+def halves_kernel(right_hbm, left_hbm, k_ref, v_ref, sems):
     n = k_ref.shape[0]
-    k_ref[...] = right_ref[pl.ds(0, n)]
-    v_ref[...] = left_ref[pl.ds(n, n)]
+    copies = (
+        pltpu.make_async_copy(right_hbm.at[pl.ds(0, n)], k_ref, sems.at[0]),
+        pltpu.make_async_copy(left_hbm.at[pl.ds(n, n)], v_ref, sems.at[1]),
+    )
+    for c in copies:
+        c.start()
+    for c in copies:
+        c.wait()
 
 
 def halves_call(right, left):
     half = jax.ShapeDtypeStruct((right.shape[0] // 2,) + right.shape[1:], right.dtype)
     return pl.pallas_call(
         halves_kernel,
-        in_specs=[VM, VM],
+        in_specs=[pl.BlockSpec(memory_space=pl.ANY)] * 2,
         out_specs=[VM, VM],
         out_shape=[half, half],
-        compiler_params=params(8),
+        scratch_shapes=[pltpu.SemaphoreType.DMA((2,))],
+        compiler_params=params(4),
         name="halves",
     )(right, left)
 
@@ -413,7 +430,9 @@
     return rows
 
 
-def columns_kernel(mdl_ref, acc_ref, w_hbm, tok_hbm, mine_ref, send_ref, tok_out, tok, sems, sem):
+def columns_kernel(
+    mdl_ref, acc_ref, w_hbm, tok_hbm, mine_ref, send_ref, tok_out, tok, rows_ref, sems, sem, put_sem
+):
     count, _, cols = mine_ref.shape
     get = pltpu.make_async_copy(
         tok_hbm.at[:, pl.ds(pl.multiple_of(mdl_ref[0] * cols, 128), cols)], tok, sem
@@ -430,9 +449,12 @@
             copies.append(c)
     get.wait()
     for r, row in enumerate(pick(acc_ref, tok[...], tok.shape[0] // acc_ref.shape[0])):
-        tok_out[r] = row
+        rows_ref[r] = row
+    put = pltpu.make_async_copy(rows_ref, tok_out, put_sem)
+    put.start()
     for c in copies:
         c.wait()
+    put.wait()
 
 
 def columns_call(mdl, accepted, w_out, tokens, count):
@@ -440,12 +462,14 @@
     return pl.pallas_call(
         columns_kernel,
         in_specs=[SMEM, VM, HBM, HBM],
-        out_specs=[VM, VM, VM],
+        out_specs=[VM, VM, HBM],
         out_shape=[jax.ShapeDtypeStruct((count, w_out.shape[0], cols), BF16)] * 2
-        + [jax.ShapeDtypeStruct(accepted.shape + (cols,), F32)],
+        + [pltpu.HBM(accepted.shape + (cols,), F32)],
         scratch_shapes=[
             pltpu.VMEM((tokens.shape[0], cols), BF16),
+            pltpu.VMEM(accepted.shape + (cols,), F32),
             pltpu.SemaphoreType.DMA((2, count)),
+            pltpu.SemaphoreType.DMA,
             pltpu.SemaphoreType.DMA,
         ],
         compiler_params=params(12),
@@ -453,48 +477,49 @@
     )(mdl, accepted, w_out, tokens)
 
 
-def first_kernel(mine_ref, w_ref, out_ref):
+def first_kernel(mine_ref, w_ref, other_hbm, out_ref, other_ref, sem, *, shift):
+    get = pltpu.make_async_copy(other_hbm.at[shift], other_ref, sem)
+    get.start()
     out_ref[...] = dot(mine_ref[...], w_ref[0])
-
-
-def out_first(mine, w_mine, shift):
+    get.wait()
+
+
+def out_first(mine, w_mine, w_other, shift):
     rows, inner = mine.shape
     cols = w_mine.shape[2]
-    return pl.pallas_call(
-        first_kernel,
+    flat = lambda i: (0, 0)
+    return pl.pallas_call(
+        lambda *refs: first_kernel(*refs, shift=shift),
         grid=(1,),
         in_specs=[
-            pl.BlockSpec((rows, inner), lambda i: (0, 0)),
+            pl.BlockSpec((rows, inner), flat),
             pl.BlockSpec((1, inner, cols), lambda i: (shift, 0, 0)),
-        ],
-        out_specs=pl.BlockSpec((rows, cols), lambda i: (0, 0)),
-        out_shape=jax.ShapeDtypeStruct((rows, cols), F32),
+            HBM,
+        ],
+        out_specs=[pl.BlockSpec((rows, cols), flat), pl.BlockSpec((inner, cols), flat)],
+        out_shape=[
+            jax.ShapeDtypeStruct((rows, cols), F32),
+            jax.ShapeDtypeStruct((inner, cols), BF16),
+        ],
+        scratch_shapes=[pltpu.SemaphoreType.DMA],
         compiler_params=params(12),
         name="out_first",
-    )(mine, w_mine)
+    )(mine, w_mine, w_other)
 
 
 def second_kernel(first_ref, other_ref, w_ref, out_ref):
-    out_ref[...] = (first_ref[...] + dot(other_ref[...], w_ref[0])).astype(BF16)
-
-
-def out_second(first, other, w_other, shift):
-    rows, inner = other.shape
-    cols = w_other.shape[2]
-    flat = lambda i: (0, 0)
+    out_ref[...] = (first_ref[...] + dot(other_ref[...], w_ref[...])).astype(BF16)
+
+
+def out_second(first, other, w):
     return pl.pallas_call(
         second_kernel,
-        grid=(1,),
-        in_specs=[
-            pl.BlockSpec((rows, cols), flat),
-            pl.BlockSpec((rows, inner), flat),
-            pl.BlockSpec((1, inner, cols), lambda i: (shift, 0, 0)),
-        ],
-        out_specs=pl.BlockSpec((rows, cols), flat),
-        out_shape=jax.ShapeDtypeStruct((rows, cols), BF16),
+        in_specs=[VM] * 3,
+        out_specs=VM,
+        out_shape=jax.ShapeDtypeStruct(first.shape, BF16),
         compiler_params=params(12),
         name="out_second",
-    )(first, other, w_other)
+    )(first, other, w)
 
 
 def out_kernel(mine_ref, other_ref, *refs):
@@ -622,8 +647,8 @@
     attended = merge_call(home, *back, requests, rows)
 
     attended_other = other_core(attended)
-    first = out_first(attended, w_mine, 2)
-    far = along_x(out_second(first, attended_other, w_other, 2), 2)
+    first, w_second = out_first(attended, w_mine, in_hbm(w_other), 2)
+    far = along_x(out_second(first, attended_other, w_second), 2)
     up, down = out_call(attended, attended_other, w_mine, w_other, (1, n_x - 1), BF16)
     up = along_x(up, 1)
     down = along_x(down, -1)

time: 92.7 us -> 99.3 us (1.071)
  waiting for transfers between devices: 24.6 us -> 33.8 us
  starting transfers between devices: 25.8 us -> 24 us
    ppermute x6, waiting for transfers between devices: 7.45 us -> 12.3 us  [along_z(): lax.ppermute(v, 'tok', [(t, (t + n * n_y) % n_tok) for t in range(n_tok)])]
    ppermute x4, waiting for transfers between devices: 5.27 us -> 9.32 us  [along_y(): return lax.ppermute(v, 'tok', perm)]
    ppermute x6, starting transfers between devices: 13.9 us -> 12.2 us  [along_z(): lax.ppermute(v, 'tok', [(t, (t + n * n_y) % n_tok) for t in range(n_tok)])]
    pallas_call x1, Pallas kernels: 8.77 us -> 7.44 us  [project_call(): pl.pallas_call(project_kernel, in_specs=[HBM] * 8, out_specs=[VM, VM, VM]...]
    unnamed x26 -> x24, local copies, waits for them, and re-layouts: 3.46 us -> 3.28 us
  transfers between devices with their start and end apart: 15 -> 15, of which waited for: 8 -> 9; matrix products, arithmetic and copies ran while one was open for 0% -> 0% of each run, Pallas kernels for 33% -> 29%
where the time goes in v3:
time: 99.3 us; the launch traced here: 98.7 us
  Pallas kernels  36.8 us (37%)
  waiting for transfers between devices  33.8 us (34%)
  starting transfers between devices  24 us (24%)
  local copies, waits for them, and re-layouts  3.28 us (3%)
    ppermute x6, waiting for transfers between devices, along_z(): lax.ppermute(v, 'tok', [(t, (t + n * n_y) % n_tok) for t in range(n_tok)])  12.3 us
    ppermute x6, starting transfers between devices, along_z(): lax.ppermute(v, 'tok', [(t, (t + n * n_y) % n_tok) for t in range(n_tok)])  12.2 us
    ppermute x3, waiting for transfers between devices, along_x(): lax.ppermute(v, 'mdl', [(m, (m + 2 * n) % n_mdl) for m in range(n_mdl)])  10.7 us
    ppermute x4, waiting for transfers between devices, along_y(): return lax.ppermute(v, 'tok', perm)  9.32 us
    pallas_call x1, Pallas kernels, project_call(): pl.pallas_call(project_kernel, in_specs=[HBM] * 8, out_specs=[VM, VM, VM]...  7.44 us
    pallas_call x1, Pallas kernels, home_call(): pl.pallas_call(home_kernel, in_specs=[SMEM, SMEM, SMEM] + [VM] * 8 + [HBM...  7.19 us
    ppermute x4, starting transfers between devices, along_y(): return lax.ppermute(v, 'tok', perm)  6.43 us
    ppermute x3, starting transfers between devices, along_x(): lax.ppermute(v, 'mdl', [(m, (m + 2 * n) % n_mdl) for m in range(n_mdl)])  5.2 us
  transfers between devices with their start and end apart: 15, of which 9 were waited for; matrix products, arithmetic and copies ran while one was open for 0% of the time, Pallas kernels for 29%

profile of v3, /device:TPU:0, one launch (start us, length us, event | category | flops | bytes accessed | tf_op | source)
XLA Modules:
  0.0 98.7 jit_solution(7531864825889416347)
XLA Ops:
  1.3 4.9 %out_columns.1 = (bf16[4,512,640]{2,1,0:T(8,128)(2,1)S(1)}, bf16[4,512,640]{2,1,0:T(8,128)(2,1)}, f32[8,8,640]{2,1,0:T(8,128)}) custom-call(s32[1]{0:T(128)} %bitcast.7.mdl_ref, s32[8,8]{1,0:T(8,128)S(1)} %copy-done.8, bf16[512,5120]{1,0:T(8,128)(2,1)} %w_hbm.1, bf16[256,5120]{1,0:T(8,128)(2,1)} %tok_hbm.3), custom_call_target="tpu_custom_call" | custom-call | tf_op jit(solution)/shard_map/out_columns/pallas_call | solution.py:462
  7.4 3.2 %collective-permute-start.1 = (bf16[12,256,128]{2,1,0:T(8,128)(2,1)S(1)}, bf16[12,256,128]{2,1,0:T(8,128)(2,1)S(1)}, u32[]{:S(2)}, u32[]{:S(2)}) collective-permute-start(bf16[12,256,128]{2,1,0:T(8,128)(2,1)S(1)} %join.1.kv.refs_2_), channel_id=1, source_target_pairs={{0,24},{8,0},{16,8},{24,16},{32,56},{40,32},{48,40},{56,48},{64,88... | collective-permute-start | bytes 2359304 | tf_op jit(solution)/shard_map/ppermute | solution.py:587
  10.6 7.4 %projections.1 = (bf16[1024,128]{1,0:T(8,128)(2,1)}, bf16[256,128]{1,0:T(8,128)(2,1)S(1)}, bf16[256,128]{1,0:T(8,128)(2,1)S(1)}) custom-call(s32[8]{0:T(128)} %len_ref.1, bf16[256,5120]{1,0:T(8,128)(2,1)} %tok_hbm.3, bf16[40,128]{1,0:T(8,128)(2,1)} %bitcast.14, bf16[5120,512]{1,0:T(8,128)(2,1)} %wq_hbm.1, bf16[5120,128]{1,0:T(8,128)(2,1)} %wk_hbm.1, ...), custom_call_target="tpu_custom_call" | custom-call | tf_op jit(solution)/shard_map/projections/pallas_call | solution.py:130
  18.1 4.1 %collective-permute-start.6 = (bf16[1024,128]{1,0:T(8,128)(2,1)}, bf16[1024,128]{1,0:T(8,128)(2,1)S(1)}, u32[]{:S(2)}, u32[]{:S(2)}) collective-permute-start(bf16[1024,128]{1,0:T(8,128)(2,1)} %get-tuple-element.19.q_ref), channel_id=1, source_target_pairs={{0,96},{8,104},{16,112},{24,120},{32,0},{40,8},{48,16},{56,24},{64... | collective-permute-start | bytes 786440 | tf_op jit(solution)/shard_map/ppermute | solution.py:590
  22.2 5.9 %collective-permute-done.1.left_hbm.kv_l.refs_4_ = bf16[12,256,128]{2,1,0:T(8,128)(2,1)S(1)} collective-permute-done((bf16[12,256,128]{2,1,0:T(8,128)(2,1)S(1)}, bf16[12,256,128]{2,1,0:T(8,128)(2,1)S(1)}, u32[]{:S(2)}, u32[]{:S(2)}) %collective-permute-start.1) | collective-permute-done | bytes 786464 | tf_op jit(solution)/shard_map/ppermute | solution.py:587
  28.1 3.4 %collective-permute-done.right_hbm.kv_r.refs_3_ = bf16[12,256,128]{2,1,0:T(8,128)(2,1)S(1)} collective-permute-done((bf16[12,256,128]{2,1,0:T(8,128)(2,1)S(1)}, bf16[12,256,128]{2,1,0:T(8,128)(2,1)S(1)}, u32[]{:S(2)}, u32[]{:S(2)}) %collective-permute-start) | collective-permute-done | bytes 786464 | tf_op jit(solution)/shard_map/ppermute | solution.py:587
  33.8 3.2 %collective-permute-start.3 = (bf16[6,256,128]{2,1,0:T(8,128)(2,1)}, bf16[6,256,128]{2,1,0:T(8,128)(2,1)}, u32[]{:S(2)}, u32[]{:S(2)}) collective-permute-start(bf16[6,256,128]{2,1,0:T(8,128)(2,1)} %get-tuple-element.21), channel_id=1, source_target_pairs={{0,24},{8,0},{16,8},{24,16},{32,56},{40,32},{48,40},{56,48},{64,88... | collective-permute-start | bytes 1179656 | tf_op jit(solution)/shard_map/ppermute | solution.py:587
  37.0 1.9 %collective-permute-start.5 = (bf16[1024,128]{1,0:T(8,128)(2,1)}, bf16[1024,128]{1,0:T(8,128)(2,1)}, u32[]{:S(2)}, u32[]{:S(2)}) collective-permute-start(bf16[1024,128]{1,0:T(8,128)(2,1)} %get-tuple-element.19.q_ref), channel_id=1, source_target_pairs={{0,32},{8,40},{16,48},{24,56},{32,64},{40,72},{48,80},{56,88},{64,... | collective-permute-start | bytes 786440 | tf_op jit(solution)/shard_map/ppermute | solution.py:590
  39.7 3.6 %collective-permute-start.4 = (bf16[1024,128]{1,0:T(8,128)(2,1)}, bf16[1024,128]{1,0:T(8,128)(2,1)}, u32[]{:S(2)}, u32[]{:S(2)}) collective-permute-start(bf16[1024,128]{1,0:T(8,128)(2,1)} %get-tuple-element.19.q_ref), channel_id=1, source_target_pairs={{0,64},{8,72},{16,80},{24,88},{32,96},{40,104},{48,112},{56,120},{... | collective-permute-start | bytes 786440 | tf_op jit(solution)/shard_map/ppermute | solution.py:590
  43.2 4.4 %collective-permute-done.5.refs_6_.refs_4_ = bf16[1024,128]{1,0:T(8,128)(2,1)} collective-permute-done((bf16[1024,128]{1,0:T(8,128)(2,1)}, bf16[1024,128]{1,0:T(8,128)(2,1)}, u32[]{:S(2)}, u32[]{:S(2)}) %collective-permute-start.5) | collective-permute-done | bytes 262176 | tf_op jit(solution)/shard_map/ppermute | solution.py:590
  47.6 5.8 %collective-permute-done.4.refs_5_.refs_4_ = bf16[1024,128]{1,0:T(8,128)(2,1)} collective-permute-done((bf16[1024,128]{1,0:T(8,128)(2,1)}, bf16[1024,128]{1,0:T(8,128)(2,1)}, u32[]{:S(2)}, u32[]{:S(2)}) %collective-permute-start.4) | collective-permute-done | bytes 262176 | tf_op jit(solution)/shard_map/ppermute | solution.py:590
  54.4 4.3 %prompt_near.1 = (f32[1024,256]{1,0:T(8,128)S(1)}, f32[1024,256]{1,0:T(8,128)S(1)}, f32[1024,256]{1,0:T(8,128)S(1)}) custom-call(s32[128]{0:T(128)S(1)} %copy-done.10, s32[1]{0:T(128)} %bitcast.at_ref.refs_1_, bf16[12,256,128]{2,1,0:T(8,128)(2,1)S(1)} %join.1.kv.refs_2_, bf16[12,256,128]{2,1,0:T(8,128)(2,1)} %copy-done.2, bf16[12,256,128]{2,1,0:T(8,128)(2,1)} %copy-done, ...), custom_call_target="tpu_custom_call" | custom-call | tf_op jit(solution)/shard_map/prompt_near/pallas_call | solution.py:235
  58.8 2.2 %prompt_far.3 = (bf16[1040,128]{1,0:T(8,128)(2,1)S(1)}, bf16[1040,128]{1,0:T(8,128)(2,1)S(1)}) custom-call(s32[128]{0:T(128)S(1)} %copy-done.10, s32[1]{0:T(128)} %bitcast.at_ref.refs_1_, bf16[6,256,128]{2,1,0:T(8,128)(2,1)} %collective-permute-done.2.k_o.refs_2_, bf16[6,256,128]{2,1,0:T(8,128)(2,1)} %collective-permute-done.3.v_o.refs_3_, ...), custom_call_target="tpu_custom_call" | custom-call | tf_op jit(solution)/shard_map/prompt_far/pallas_call | solution.py:272
  61.0 2.0 %collective-permute-start.9 = (bf16[1040,128]{1,0:T(8,128)(2,1)S(1)}, bf16[1040,128]{1,0:T(8,128)(2,1)S(1)}, u32[]{:S(2)}, u32[]{:S(2)}) collective-permute-start(bf16[1040,128]{1,0:T(8,128)(2,1)S(1)} %get-tuple-element.28), channel_id=1, source_target_pairs={{0,32},{8,40},{16,48},{24,56},{32,64},{40,72},{48,80},{56,88},{64,... | collective-permute-start | bytes 798728 | tf_op jit(solution)/shard_map/ppermute | solution.py:590
  63.0 1.8 %prompt_far.2 = bf16[1040,128]{1,0:T(8,128)(2,1)S(1)} custom-call(s32[128]{0:T(128)S(1)} %copy-done.10, s32[1]{0:T(128)} %bitcast.at_ref.refs_1_, bf16[6,256,128]{2,1,0:T(8,128)(2,1)} %collective-permute-done.2.k_o.refs_2_, bf16[6,256,128]{2,1,0:T(8,128)(2,1)} %collective-permute-done.3.v_o.refs_3_, ...), custom_call_target="tpu_custom_call" | custom-call | tf_op jit(solution)/shard_map/prompt_far/pallas_call | solution.py:272
  65.3 7.2 %home_attention.1.refs_0_ = f32[1024,256]{1,0:T(8,128)S(1)} custom-call(s32[128]{0:T(128)S(1)} %copy-done.10, s32[1]{0:T(128)} %bitcast.at_ref.refs_1_, s32[8]{0:T(128)S(1)} %copy-done.11, bf16[1024,128]{1,0:T(8,128)(2,1)} %get-tuple-element.19.q_ref, bf16[12,256,128]{2,1,0:T(8,128)(2,1)S(1)} %join.1.kv.refs_2_, bf16[12,256,128]{2,1,0:T(8,128)(2,1)S(1)} %copy-done.3, ...), custom_call_target="tpu_custom_call" | custom-call | tf_op jit(solution)/shard_map/home_attention/pallas_call | solution.py:362
  72.5 2.1 %collective-permute-done.9.refs_3_ = bf16[1040,128]{1,0:T(8,128)(2,1)S(1)} collective-permute-done((bf16[1040,128]{1,0:T(8,128)(2,1)S(1)}, bf16[1040,128]{1,0:T(8,128)(2,1)S(1)}, u32[]{:S(2)}, u32[]{:S(2)}) %collective-permute-start.9) | collective-permute-done | bytes 266272 | tf_op jit(solution)/shard_map/ppermute | solution.py:590
  76.5 2.3 %out_proj.3 = (bf16[256,640]{1,0:T(8,128)(2,1)S(1)}, bf16[256,640]{1,0:T(8,128)(2,1)S(1)}) custom-call(bf16[256,512]{1,0:T(8,128)(2,1)S(1)} %merge.1.mine_ref.refs_0_, bf16[256,512]{1,0:T(8,128)(2,1)S(1)} %collective-permute-done.10.other_ref, bf16[4,512,640]{2,1,0:T(8,128)(2,1)S(1)} %get-tuple-element.29.refs_0_.refs_1_, ...), custom_call_target="tpu_custom_call" | custom-call | tf_op jit(solution)/shard_map/out_proj/pallas_call | solution.py:536
  80.3 1.7 %collective-permute-start.14 = (bf16[256,640]{1,0:T(8,128)(2,1)S(1)}, bf16[256,640]{1,0:T(8,128)(2,1)S(1)}, u32[]{:S(2)}, u32[]{:S(2)}) collective-permute-start(bf16[256,640]{1,0:T(8,128)(2,1)S(1)} %get-tuple-element.34), channel_id=1, source_target_pairs={{0,6},{1,7},{2,0},{3,1},{4,2},{5,3},{6,4},{7,5},{8,14},{9,15},{10,... | collective-permute-start | bytes 983048 | tf_op jit(solution)/shard_map/ppermute | solution.py:593
  83.6 1.9 %collective-permute-start.12 = (bf16[256,640]{1,0:T(8,128)(2,1)S(1)}, bf16[256,640]{1,0:T(8,128)(2,1)S(1)}, u32[]{:S(2)}, u32[]{:S(2)}) collective-permute-start(bf16[256,640]{1,0:T(8,128)(2,1)S(1)} %out_second.1), channel_id=1, source_target_pairs={{0,4},{1,5},{2,6},{3,7},{4,0},{5,1},{6,2},{7,3},{8,12},{9,13},{10,... | collective-permute-start | bytes 983048 | tf_op jit(solution)/shard_map/ppermute | solution.py:593
  85.5 1.7 %out_proj.2.own_ref = f32[256,640]{1,0:T(8,128)S(1)} custom-call(bf16[256,512]{1,0:T(8,128)(2,1)S(1)} %merge.1.mine_ref.refs_0_, bf16[256,512]{1,0:T(8,128)(2,1)S(1)} %collective-permute-done.10.other_ref, bf16[4,512,640]{2,1,0:T(8,128)(2,1)S(1)} %get-tuple-element.29.refs_0_.refs_1_, bf16[4,512,640]{2,1,0:T(8,128)(2,1)} %collective-permute-done.11.refs_1_.refs_2_.refs_3_), custom_call_target="tpu_custom_call" | custom-call | tf_op jit(solution)/shard_map/out_proj/pallas_call | solution.py:536
  87.1 2.7 %collective-permute-done.13.b_ref = bf16[256,640]{1,0:T(8,128)(2,1)S(1)} collective-permute-done((bf16[256,640]{1,0:T(8,128)(2,1)S(1)}, bf16[256,640]{1,0:T(8,128)(2,1)S(1)}, u32[]{:S(2)}, u32[]{:S(2)}) %collective-permute-start.13) | collective-permute-done | bytes 327712 | tf_op jit(solution)/shard_map/ppermute | solution.py:593
  89.8 6.3 %collective-permute-done.14.c_ref = bf16[256,640]{1,0:T(8,128)(2,1)S(1)} collective-permute-done((bf16[256,640]{1,0:T(8,128)(2,1)S(1)}, bf16[256,640]{1,0:T(8,128)(2,1)S(1)}, u32[]{:S(2)}, u32[]{:S(2)}) %collective-permute-start.14) | collective-permute-done | bytes 327712 | tf_op jit(solution)/shard_map/ppermute | solution.py:593
  96.1 1.7 %collective-permute-done.12.a_ref = bf16[256,640]{1,0:T(8,128)(2,1)S(1)} collective-permute-done((bf16[256,640]{1,0:T(8,128)(2,1)S(1)}, bf16[256,640]{1,0:T(8,128)(2,1)S(1)}, u32[]{:S(2)}, u32[]{:S(2)}) %collective-permute-start.12) | collective-permute-done | bytes 327712 | tf_op jit(solution)/shard_map/ppermute | solution.py:593
  (44 shorter events, 12.3 us)
Async XLA Ops:
  6.2 70.3 %collective-permute-start.11 = (bf16[4,512,640]{2,1,0:T(8,128)(2,1)}, bf16[4,512,640]{2,1,0:T(8,128)(2,1)}, u32[]{:S(2)}, u32[]{:S(2)}) collective-permute-start(bf16[4,512,640]{2,1,0:T(8,128)(2,1)} %get-tuple-element.30), channel_id=1, source_target_pairs={{0,1},{1,0},{2,3},{3,2},{4,5},{5,4},{6,7},{7,6},{8,9},{9,8},{10,11... | collective-permute-start | bytes 7864328 | tf_op jit(solution)/shard_map/ppermute | solution.py:596
  7.4 20.7 %collective-permute-start.1 = (bf16[12,256,128]{2,1,0:T(8,128)(2,1)S(1)}, bf16[12,256,128]{2,1,0:T(8,128)(2,1)S(1)}, u32[]{:S(2)}, u32[]{:S(2)}) collective-permute-start(bf16[12,256,128]{2,1,0:T(8,128)(2,1)S(1)} %join.1.kv.refs_2_), channel_id=1, source_target_pairs={{0,24},{8,0},{16,8},{24,16},{32,56},{40,32},{48,40},{56,48},{64,88... | collective-permute-start | bytes 2359304 | tf_op jit(solution)/shard_map/ppermute | solution.py:587
  10.6 20.9 %collective-permute-start = (bf16[12,256,128]{2,1,0:T(8,128)(2,1)S(1)}, bf16[12,256,128]{2,1,0:T(8,128)(2,1)S(1)}, u32[]{:S(2)}, u32[]{:S(2)}) collective-permute-start(bf16[12,256,128]{2,1,0:T(8,128)(2,1)S(1)} %join.1.kv.refs_2_), channel_id=1, source_target_pairs={{0,8},{8,16},{16,24},{24,0},{32,40},{40,48},{48,56},{56,32},{64,72... | collective-permute-start | bytes 2359304 | tf_op jit(solution)/shard_map/ppermute | solution.py:587
  10.6 42.8 %copy-start.10 = (s32[128]{0:T(128)S(1)}, s32[128]{0:T(128)}, u32[]{:S(2)}) copy-start(s32[128]{0:T(128)} %refs_0_.5) | copy-start | bytes 1540
  18.1 20.9 %collective-permute-start.6 = (bf16[1024,128]{1,0:T(8,128)(2,1)}, bf16[1024,128]{1,0:T(8,128)(2,1)S(1)}, u32[]{:S(2)}, u32[]{:S(2)}) collective-permute-start(bf16[1024,128]{1,0:T(8,128)(2,1)} %get-tuple-element.19.q_ref), channel_id=1, source_target_pairs={{0,96},{8,104},{16,112},{24,120},{32,0},{40,8},{48,16},{56,24},{64... | collective-permute-start | bytes 786440 | tf_op jit(solution)/shard_map/ppermute | solution.py:590
  31.5 1.4 %copy-start.2 = (bf16[12,256,128]{2,1,0:T(8,128)(2,1)}, bf16[12,256,128]{2,1,0:T(8,128)(2,1)S(1)}, u32[]{:S(2)}) copy-start(bf16[12,256,128]{2,1,0:T(8,128)(2,1)S(1)} %collective-permute-done.right_hbm.kv_r.refs_3_) | copy-start | bytes 2359300
  33.8 24.9 %collective-permute-start.2 = (bf16[6,256,128]{2,1,0:T(8,128)(2,1)}, bf16[6,256,128]{2,1,0:T(8,128)(2,1)}, u32[]{:S(2)}, u32[]{:S(2)}) collective-permute-start(bf16[6,256,128]{2,1,0:T(8,128)(2,1)} %get-tuple-element.20), channel_id=1, source_target_pairs={{0,8},{8,16},{16,24},{24,0},{32,40},{40,48},{48,56},{56,32},{64,72... | collective-permute-start | bytes 1179656 | tf_op jit(solution)/shard_map/ppermute | solution.py:587
  33.8 24.9 %collective-permute-start.3 = (bf16[6,256,128]{2,1,0:T(8,128)(2,1)}, bf16[6,256,128]{2,1,0:T(8,128)(2,1)}, u32[]{:S(2)}, u32[]{:S(2)}) collective-permute-start(bf16[6,256,128]{2,1,0:T(8,128)(2,1)} %get-tuple-element.21), channel_id=1, source_target_pairs={{0,24},{8,0},{16,8},{24,16},{32,56},{40,32},{48,40},{56,48},{64,88... | collective-permute-start | bytes 1179656 | tf_op jit(solution)/shard_map/ppermute | solution.py:587
  37.0 10.6 %collective-permute-start.5 = (bf16[1024,128]{1,0:T(8,128)(2,1)}, bf16[1024,128]{1,0:T(8,128)(2,1)}, u32[]{:S(2)}, u32[]{:S(2)}) collective-permute-start(bf16[1024,128]{1,0:T(8,128)(2,1)} %get-tuple-element.19.q_ref), channel_id=1, source_target_pairs={{0,32},{8,40},{16,48},{24,56},{32,64},{40,72},{48,80},{56,88},{64,... | collective-permute-start | bytes 786440 | tf_op jit(solution)/shard_map/ppermute | solution.py:590
  39.7 13.8 %collective-permute-start.4 = (bf16[1024,128]{1,0:T(8,128)(2,1)}, bf16[1024,128]{1,0:T(8,128)(2,1)}, u32[]{:S(2)}, u32[]{:S(2)}) collective-permute-start(bf16[1024,128]{1,0:T(8,128)(2,1)} %get-tuple-element.19.q_ref), channel_id=1, source_target_pairs={{0,64},{8,72},{16,80},{24,88},{32,96},{40,104},{48,112},{56,120},{... | collective-permute-start | bytes 786440 | tf_op jit(solution)/shard_map/ppermute | solution.py:590
  53.4 1.0 copy-start.5
  54.4 4.3 %copy-start.6 = (bf16[1024,128]{1,0:T(8,128)(2,1)S(1)}, bf16[1024,128]{1,0:T(8,128)(2,1)}, u32[]{:S(2)}) copy-start(bf16[1024,128]{1,0:T(8,128)(2,1)} %copy-done.4) | copy-start | bytes 786436
  58.7 6.6 %copy-start.1 = (bf16[12,256,128]{2,1,0:T(8,128)(2,1)S(1)}, bf16[12,256,128]{2,1,0:T(8,128)(2,1)}, u32[]{:S(2)}) copy-start(bf16[12,256,128]{2,1,0:T(8,128)(2,1)} %copy-done) | copy-start | bytes 2359300
  58.7 6.6 %copy-start.3 = (bf16[12,256,128]{2,1,0:T(8,128)(2,1)S(1)}, bf16[12,256,128]{2,1,0:T(8,128)(2,1)}, u32[]{:S(2)}) copy-start(bf16[12,256,128]{2,1,0:T(8,128)(2,1)} %copy-done.2) | copy-start | bytes 2359300
  58.7 6.5 %copy-start.11 = (s32[8]{0:T(128)S(1)}, s32[8]{0:T(128)}, u32[]{:S(2)}) copy-start(s32[8]{0:T(128)} %len_ref.1) | copy-start | bytes 100
  60.9 11.6 %collective-permute-start.8 = (bf16[1040,128]{1,0:T(8,128)(2,1)S(1)}, bf16[1040,128]{1,0:T(8,128)(2,1)S(1)}, u32[]{:S(2)}, u32[]{:S(2)}) collective-permute-start(bf16[1040,128]{1,0:T(8,128)(2,1)S(1)} %get-tuple-element.27), channel_id=1, source_target_pairs={{0,96},{8,104},{16,112},{24,120},{32,0},{40,8},{48,16},{56,24},{64... | collective-permute-start | bytes 798728 | tf_op jit(solution)/shard_map/ppermute | solution.py:590
  61.0 13.6 %collective-permute-start.9 = (bf16[1040,128]{1,0:T(8,128)(2,1)S(1)}, bf16[1040,128]{1,0:T(8,128)(2,1)S(1)}, u32[]{:S(2)}, u32[]{:S(2)}) collective-permute-start(bf16[1040,128]{1,0:T(8,128)(2,1)S(1)} %get-tuple-element.28), channel_id=1, source_target_pairs={{0,32},{8,40},{16,48},{24,56},{32,64},{40,72},{48,80},{56,88},{64,... | collective-permute-start | bytes 798728 | tf_op jit(solution)/shard_map/ppermute | solution.py:590
  64.8 9.8 %collective-permute-start.7 = (bf16[1040,128]{1,0:T(8,128)(2,1)S(1)}, bf16[1040,128]{1,0:T(8,128)(2,1)S(1)}, u32[]{:S(2)}, u32[]{:S(2)}) collective-permute-start(bf16[1040,128]{1,0:T(8,128)(2,1)S(1)} %prompt_far.2), channel_id=1, source_target_pairs={{0,64},{8,72},{16,80},{24,88},{32,96},{40,104},{48,112},{56,120},{... | collective-permute-start | bytes 798728 | tf_op jit(solution)/shard_map/ppermute | solution.py:590
  74.9 1.6 %collective-permute-start.10 = (bf16[256,512]{1,0:T(8,128)(2,1)S(1)}, bf16[256,512]{1,0:T(8,128)(2,1)S(1)}, u32[]{:S(2)}, u32[]{:S(2)}) collective-permute-start(bf16[256,512]{1,0:T(8,128)(2,1)S(1)} %merge.1.mine_ref.refs_0_), channel_id=1, source_target_pairs={{0,1},{1,0},{2,3},{3,2},{4,5},{5,4},{6,7},{7,6},{8,9},{9,8},{10,11... | collective-permute-start | bytes 786440 | tf_op jit(solution)/shard_map/ppermute | solution.py:596
  78.8 11.0 %collective-permute-start.13 = (bf16[256,640]{1,0:T(8,128)(2,1)S(1)}, bf16[256,640]{1,0:T(8,128)(2,1)S(1)}, u32[]{:S(2)}, u32[]{:S(2)}) collective-permute-start(bf16[256,640]{1,0:T(8,128)(2,1)S(1)} %get-tuple-element.33), channel_id=1, source_target_pairs={{0,2},{1,3},{2,4},{3,5},{4,6},{5,7},{6,0},{7,1},{8,10},{9,11},{10,... | collective-permute-start | bytes 983048 | tf_op jit(solution)/shard_map/ppermute | solution.py:593
  80.3 15.8 %collective-permute-start.14 = (bf16[256,640]{1,0:T(8,128)(2,1)S(1)}, bf16[256,640]{1,0:T(8,128)(2,1)S(1)}, u32[]{:S(2)}, u32[]{:S(2)}) collective-permute-start(bf16[256,640]{1,0:T(8,128)(2,1)S(1)} %get-tuple-element.34), channel_id=1, source_target_pairs={{0,6},{1,7},{2,0},{3,1},{4,2},{5,3},{6,4},{7,5},{8,14},{9,15},{10,... | collective-permute-start | bytes 983048 | tf_op jit(solution)/shard_map/ppermute | solution.py:593
  83.6 14.2 %copy-start.7 = (f32[8,8,640]{2,1,0:T(8,128)S(1)}, f32[8,8,640]{2,1,0:T(8,128)}, u32[]{:S(2)}) copy-start(f32[8,8,640]{2,1,0:T(8,128)} %get-tuple-element.35.tok_ref) | copy-start | bytes 491524
  83.6 14.2 %copy-start.9 = (s32[8,8]{1,0:T(8,128)S(1)}, s32[8,8]{1,0:T(8,128)}, u32[]{:S(2)}) copy-start(s32[8,8]{1,0:T(8,128)} %acc_ref.3) | copy-start | bytes 772
  83.6 14.2 %collective-permute-start.12 = (bf16[256,640]{1,0:T(8,128)(2,1)S(1)}, bf16[256,640]{1,0:T(8,128)(2,1)S(1)}, u32[]{:S(2)}, u32[]{:S(2)}) collective-permute-start(bf16[256,640]{1,0:T(8,128)(2,1)S(1)} %out_second.1), channel_id=1, source_target_pairs={{0,4},{1,5},{2,6},{3,7},{4,0},{5,1},{6,2},{7,3},{8,12},{9,13},{10,... | collective-permute-start | bytes 983048 | tf_op jit(solution)/shard_map/ppermute | solution.py:593
  (3 other events, 2.3 us)

commit v4 on v3

--- a/solution.py
+++ b/solution.py
@@ -151,77 +151,23 @@
     )(lengths, tokens, gain, w_query, w_key, w_value, ancestors, inverse)
 
 
-def join_kernel(a_hbm, b_hbm, out_ref, sems):
-    n = a_hbm.shape[0]
-    copies = [
-        pltpu.make_async_copy(ref, out_ref.at[pl.ds(i * n, n)], sems.at[i])
-        for i, ref in enumerate((a_hbm, b_hbm))
-    ]
-    for c in copies:
-        c.start()
-    for c in copies:
-        c.wait()
-
-
-def join_call(a, b):
-    return pl.pallas_call(
-        join_kernel,
-        in_specs=[HBM, HBM],
-        out_specs=VM,
-        out_shape=jax.ShapeDtypeStruct((2 * a.shape[0],) + a.shape[1:], a.dtype),
-        scratch_shapes=[pltpu.SemaphoreType.DMA((2,))],
-        compiler_params=params(4),
-        name="join",
-    )(a, b)
-
-
-def halves_kernel(right_hbm, left_hbm, k_ref, v_ref, sems):
-    n = k_ref.shape[0]
-    copies = (
-        pltpu.make_async_copy(right_hbm.at[pl.ds(0, n)], k_ref, sems.at[0]),
-        pltpu.make_async_copy(left_hbm.at[pl.ds(n, n)], v_ref, sems.at[1]),
-    )
-    for c in copies:
-        c.start()
-    for c in copies:
-        c.wait()
-
-
-def halves_call(right, left):
-    half = jax.ShapeDtypeStruct((right.shape[0] // 2,) + right.shape[1:], right.dtype)
-    return pl.pallas_call(
-        halves_kernel,
-        in_specs=[pl.BlockSpec(memory_space=pl.ANY)] * 2,
-        out_specs=[VM, VM],
-        out_shape=[half, half],
-        scratch_shapes=[pltpu.SemaphoreType.DMA((2,))],
-        compiler_params=params(4),
-        name="halves",
-    )(right, left)
-
-
 def prompt_sum(q, g, pieces, ones):
     weights, values = [], []
-    for kref, koff, vref, voff in pieces:
-        weights.append(jnp.exp2(dot_nt(q, kref[koff + g])).astype(BF16))
-        values.append(jnp.concatenate([vref[voff + g], ones], axis=1))
+    for keys, vals in pieces:
+        weights.append(jnp.exp2(dot_nt(q, keys[g])).astype(BF16))
+        values.append(jnp.concatenate([vals[g], ones], axis=1))
     return dot(jnp.concatenate(weights, axis=1), jnp.concatenate(values, axis=0))
-
-
-def near_pieces(kv, kv_r, kv_l):
-    n = kv.shape[0] // 2
-    return [(kv, 0, kv, n), (kv_r, 0, kv_r, n), (kv_l, 0, kv_l, n)]
 
 
 def source_of(at_ref, requests, shift, n_tok):
     return lax.rem(at_ref[0] + n_tok - shift, n_tok) * requests
 
 
-def near_kernel(group_ref, at_ref, kv, kv_r, kv_l, *refs, requests, shifts, n_tok):
-    hd = kv.shape[2]
+def near_kernel(group_ref, at_ref, k, k_r, k_l, v, v_r, v_l, *refs, requests, shifts, n_tok):
+    hd = k.shape[2]
     qrows = refs[0].shape[0] // requests
-    pieces = near_pieces(kv, kv_r, kv_l)
-    ones = jnp.ones((kv.shape[1], hd), BF16)
+    pieces = [(k, v), (k_r, v_r), (k_l, v_l)]
+    ones = jnp.ones((k.shape[1], hd), BF16)
     for shift, q_ref, out_ref in zip(shifts, refs[: len(shifts)], refs[len(shifts) :]):
         base = source_of(at_ref, requests, shift, n_tok)
         for r in range(requests):
@@ -229,17 +175,17 @@
             out_ref[at, :] = prompt_sum(q_ref[at, :], group_ref[base + r], pieces, ones)
 
 
-def near_call(groups, at, qs, kv, kv_r, kv_l, requests, shifts, n_tok):
+def near_call(groups, at, qs, prompts, requests, shifts, n_tok):
     rows, hd = qs[0].shape
     n = len(shifts)
     return pl.pallas_call(
         lambda *refs: near_kernel(*refs, requests=requests, shifts=shifts, n_tok=n_tok),
-        in_specs=[SMEM, SMEM] + [VM] * (3 + n),
+        in_specs=[SMEM, SMEM] + [VM] * (6 + n),
         out_specs=[VM] * n,
         out_shape=[jax.ShapeDtypeStruct((rows, 2 * hd), F32)] * n,
         compiler_params=params(16),
         name="prompt_near",
-    )(groups, at, kv, kv_r, kv_l, *qs)
+    )(groups, at, *prompts, *qs)
 
 
 def far_kernel(group_ref, at_ref, k_o, v_o, *refs, requests, shifts, n_tok):
@@ -256,7 +202,7 @@
         for r in range(requests):
             at = pl.ds(r * qrows, qrows)
             acc = near_ref[at, :] + prompt_sum(
-                q_ref[at, :], group_ref[base + r], [(k_o, 0, v_o, 0)], ones
+                q_ref[at, :], group_ref[base + r], [(k_o, v_o)], ones
             )
             out_ref[at, :] = acc[:, :hd].astype(BF16)
             totals.append(jnp.sum(jnp.where(diagonal, acc[:, hd:], 0.0), axis=0, keepdims=True))
@@ -280,8 +226,8 @@
 
 
 def home_kernel(
-    group_ref, at_ref, len_ref, q_ref, kv, kv_r, kv_l, k_o, v_o, new_k, new_v, anc_hbm, ck_hbm,
-    cv_hbm, out_ref, anc_ref, keys, values, where_ref, sems, anc_sem,
+    group_ref, at_ref, len_ref, q_ref, k, k_r, k_l, v, v_r, v_l, k_o, v_o, new_k, new_v, anc_hbm,
+    ck_hbm, cv_hbm, out_ref, anc_ref, keys, values, where_ref, sems, anc_sem,
 ):
     requests, slots, hd = keys.shape
     qrows = q_ref.shape[0] // requests
@@ -323,7 +269,7 @@
     for j in range(LANES):
         where_ref[0, count + j] = requests - 1
         where_ref[1, count + j] = 0
-    pieces = near_pieces(kv, kv_r, kv_l) + [(k_o, 0, v_o, 0)]
+    pieces = [(k, v), (k_r, v_r), (k_l, v_l), (k_o, v_o)]
     ones = jnp.ones((KB, hd), BF16)
     get_anc.wait()
     for r in range(requests):
@@ -361,7 +307,7 @@
     requests, slots, hd = cache_keys.shape
     return pl.pallas_call(
         home_kernel,
-        in_specs=[SMEM, SMEM, SMEM] + [VM] * 8 + [HBM] * 3,
+        in_specs=[SMEM, SMEM, SMEM] + [VM] * 11 + [HBM] * 3,
         out_specs=VM,
         out_shape=jax.ShapeDtypeStruct((q.shape[0], 2 * hd), F32),
         scratch_shapes=[
@@ -602,9 +548,9 @@
     mdl_at = jnp.reshape(mdl, (1,)).astype(jnp.int32)
 
     squeeze = lambda v: v.reshape(v.shape[0], v.shape[1], v.shape[3])
-    kv = join_call(in_hbm(squeeze(prompt_keys)), in_hbm(squeeze(prompt_values)))
-    kv_r = along_y(kv, 1)
-    kv_l = along_y(kv, -1)
+    k, v = squeeze(prompt_keys), squeeze(prompt_values)
+    k_r, k_l = along_y(k, 1), along_y(k, -1)
+    v_r, v_l = along_y(v, 1), along_y(v, -1)
 
     exponent = np.arange(hd // 2, dtype=np.float64) * (2.0 / hd)
     inverse = jnp.asarray(np.tile(THETA**-exponent, 2)[None, :], dtype=F32)
@@ -624,24 +570,24 @@
     w_mine, w_send, picked = columns_call(mdl_at, accepted, in_hbm(w_out), in_hbm(tokens), n_x)
     w_other = other_core(w_send)
 
-    k_half, v_half = halves_call(kv_r, kv_l)
-    k_o = along_y(k_half, 1)
-    v_o = along_y(v_half, -1)
-    prompts = (kv, kv_r, kv_l, k_o, v_o)
+    k_o = along_y(k_r, 1)
+    v_o = along_y(v_l, -1)
+    near = tuple(map(in_hbm, (k, k_r, k_l, v, v_r, v_l)))
 
     turns = [n % n_z * n_y for n in shifts]
-    nears = near_call(
-        request_group, tok_at, q_far, kv, in_hbm(kv_r), in_hbm(kv_l), requests, turns, n_tok
-    )
-    parts = []
-    for some in (slice(0, 1), slice(1, 3)):
+    nears, parts = [], []
+    two = (slice(0, 1), slice(1, 3))
+    for some in two:
+        nears.append(
+            near_call(request_group, tok_at, q_far[some], near, requests, turns[some], n_tok)
+        )
+    for i, some in enumerate(two):
         parts += far_call(
-            request_group, tok_at, nears[some], q_far[some], k_o, v_o, requests, turns[some],
-            n_tok,
+            request_group, tok_at, nears[i], q_far[some], k_o, v_o, requests, turns[some], n_tok
         )
     back = [along_z(part, -n) for n, part in zip(shifts, parts)]
     home = home_call(
-        request_group, tok_at, cache_length, q, prompts, new_k, new_v, in_hbm(table),
+        request_group, tok_at, cache_length, q, (k, k_r, k_l, v, v_r, v_l, k_o, v_o), new_k, new_v, in_hbm(table),
         in_hbm(squeeze(cache_keys)), in_hbm(squeeze(cache_values)),
     )
     attended = merge_call(home, *back, requests, rows)

time: 99.3 us -> 92.5 us (0.932)
  waiting for transfers between devices: 33.8 us -> 27.5 us
  Pallas kernels: 36.8 us -> 35.6 us
    ppermute x6, waiting for transfers between devices: 12.3 us -> 6.02 us  [along_z(): lax.ppermute(v, 'tok', [(t, (t + n * n_y) % n_tok) for t in range(n_tok)])]
    ppermute x4 -> x6, starting transfers between devices: 6.43 us -> 9.86 us  [along_y(): return lax.ppermute(v, 'tok', perm)]
    ppermute x6, starting transfers between devices: 12.2 us -> 9.57 us  [along_z(): lax.ppermute(v, 'tok', [(t, (t + n * n_y) % n_tok) for t in range(n_tok)])]
    pallas_call x3 -> x1, Pallas kernels: 9.68 us -> 7.2 us  [home_call(): pl.pallas_call(home_kernel, in_specs=[SMEM, SMEM, SMEM] + [VM] * 11 + [HB...]
    pallas_call x1 -> x2, Pallas kernels: 4.29 us -> 6.39 us  [near_call(): pl.pallas_call(lambda *refs: near_kernel(*refs, requests=requests, shifts...]
    unnamed x24 -> x32, local copies, waits for them, and re-layouts: 3.28 us -> 3.17 us
    ppermute x4 -> x6, waiting for transfers between devices: 9.32 us -> 9.34 us  [along_y(): return lax.ppermute(v, 'tok', perm)]
  transfers between devices with their start and end apart: 15 -> 17, of which waited for: 9 -> 10; matrix products, arithmetic and copies ran while one was open for 0% -> 0% of each run, Pallas kernels for 29% -> 30%
where the time goes in v4:
time: 92.5 us; the launch traced here: 91.9 us
  Pallas kernels  35.6 us (38%)
  waiting for transfers between devices  27.5 us (30%)
  starting transfers between devices  24.8 us (27%)
  local copies, waits for them, and re-layouts  3.17 us (3%)
    ppermute x3, waiting for transfers between devices, along_x(): lax.ppermute(v, 'mdl', [(m, (m + 2 * n) % n_mdl) for m in range(n_mdl)])  10.7 us
    ppermute x6, starting transfers between devices, along_y(): return lax.ppermute(v, 'tok', perm)  9.86 us
    ppermute x6, starting transfers between devices, along_z(): lax.ppermute(v, 'tok', [(t, (t + n * n_y) % n_tok) for t in range(n_tok)])  9.57 us
    ppermute x6, waiting for transfers between devices, along_y(): return lax.ppermute(v, 'tok', perm)  9.34 us
    pallas_call x1, Pallas kernels, project_call(): pl.pallas_call(project_kernel, in_specs=[HBM] * 8, out_specs=[VM, VM, VM]...  7.49 us
    pallas_call x1, Pallas kernels, home_call(): pl.pallas_call(home_kernel, in_specs=[SMEM, SMEM, SMEM] + [VM] * 11 + [HB...  7.2 us
    pallas_call x2, Pallas kernels, near_call(): pl.pallas_call(lambda *refs: near_kernel(*refs, requests=requests, shifts...  6.39 us
    ppermute x6, waiting for transfers between devices, along_z(): lax.ppermute(v, 'tok', [(t, (t + n * n_y) % n_tok) for t in range(n_tok)])  6.02 us
  transfers between devices with their start and end apart: 17, of which 10 were waited for; matrix products, arithmetic and copies ran while one was open for 0% of the time, Pallas kernels for 30%

profile of v4, /device:TPU:0, one launch (start us, length us, event | category | flops | bytes accessed | tf_op | source)
XLA Modules:
  0.0 91.9 jit_solution(10451775636378752893)
XLA Ops:
  1.3 4.9 %out_columns.1 = (bf16[4,512,640]{2,1,0:T(8,128)(2,1)S(1)}, bf16[4,512,640]{2,1,0:T(8,128)(2,1)}, f32[8,8,640]{2,1,0:T(8,128)}) custom-call(s32[1]{0:T(128)} %bitcast.7.mdl_ref, s32[8,8]{1,0:T(8,128)S(1)} %copy-done.12, bf16[512,5120]{1,0:T(8,128)(2,1)} %w_hbm.1, bf16[256,5120]{1,0:T(8,128)(2,1)} %tok_hbm.3), custom_call_target="tpu_custom_call" | custom-call | tf_op jit(solution)/shard_map/out_columns/pallas_call | solution.py:408
  6.4 7.5 %projections.1 = (bf16[1024,128]{1,0:T(8,128)(2,1)}, bf16[256,128]{1,0:T(8,128)(2,1)S(1)}, bf16[256,128]{1,0:T(8,128)(2,1)S(1)}) custom-call(s32[8]{0:T(128)} %len_ref.1, bf16[256,5120]{1,0:T(8,128)(2,1)} %tok_hbm.3, bf16[40,128]{1,0:T(8,128)(2,1)} %bitcast.22, bf16[5120,512]{1,0:T(8,128)(2,1)} %wq_hbm.1, bf16[5120,128]{1,0:T(8,128)(2,1)} %wk_hbm.1, ...), custom_call_target="tpu_custom_call" | custom-call | tf_op jit(solution)/shard_map/projections/pallas_call | solution.py:130
  13.9 4.1 %collective-permute-start.6 = (bf16[1024,128]{1,0:T(8,128)(2,1)}, bf16[1024,128]{1,0:T(8,128)(2,1)S(1)}, u32[]{:S(2)}, u32[]{:S(2)}) collective-permute-start(bf16[1024,128]{1,0:T(8,128)(2,1)} %get-tuple-element.16.q_ref), channel_id=1, source_target_pairs={{0,64},{8,72},{16,80},{24,88},{32,96},{40,104},{48,112},{56,120},{... | collective-permute-start | bytes 786440 | tf_op jit(solution)/shard_map/ppermute | solution.py:536
  17.9 1.6 %collective-permute-start = (bf16[6,256,128]{2,1,0:T(8,128)(2,1)S(1)}, bf16[6,256,128]{2,1,0:T(8,128)(2,1)}, u32[]{:S(2)}, u32[]{:S(2)}) collective-permute-start(bf16[6,256,128]{2,1,0:T(8,128)(2,1)S(1)} %bitcast.10), channel_id=1, source_target_pairs={{0,8},{8,16},{16,24},{24,0},{32,40},{40,48},{48,56},{56,32},{64,72... | collective-permute-start | bytes 1179656 | tf_op jit(solution)/shard_map/ppermute | solution.py:533
  19.5 1.7 %collective-permute-start.3 = (bf16[6,256,128]{2,1,0:T(8,128)(2,1)S(1)}, bf16[6,256,128]{2,1,0:T(8,128)(2,1)}, u32[]{:S(2)}, u32[]{:S(2)}) collective-permute-start(bf16[6,256,128]{2,1,0:T(8,128)(2,1)S(1)} %bitcast.15), channel_id=1, source_target_pairs={{0,24},{8,0},{16,8},{24,16},{32,56},{40,32},{48,40},{56,48},{64,88... | collective-permute-start | bytes 1179656 | tf_op jit(solution)/shard_map/ppermute | solution.py:533
  21.2 1.8 %collective-permute-start.1 = (bf16[6,256,128]{2,1,0:T(8,128)(2,1)S(1)}, bf16[6,256,128]{2,1,0:T(8,128)(2,1)S(1)}, u32[]{:S(2)}, u32[]{:S(2)}) collective-permute-start(bf16[6,256,128]{2,1,0:T(8,128)(2,1)S(1)} %bitcast.11), channel_id=1, source_target_pairs={{0,24},{8,0},{16,8},{24,16},{32,56},{40,32},{48,40},{56,48},{64,88... | collective-permute-start | bytes 1179656 | tf_op jit(solution)/shard_map/ppermute | solution.py:533
  23.0 2.1 %collective-permute-done.6.refs_8_.refs_4_ = bf16[1024,128]{1,0:T(8,128)(2,1)S(1)} collective-permute-done((bf16[1024,128]{1,0:T(8,128)(2,1)}, bf16[1024,128]{1,0:T(8,128)(2,1)S(1)}, u32[]{:S(2)}, u32[]{:S(2)}) %collective-permute-start.6) | collective-permute-done | bytes 262176 | tf_op jit(solution)/shard_map/ppermute | solution.py:536
  25.8 1.6 %collective-permute-start.2 = (bf16[6,256,128]{2,1,0:T(8,128)(2,1)S(1)}, bf16[6,256,128]{2,1,0:T(8,128)(2,1)S(1)}, u32[]{:S(2)}, u32[]{:S(2)}) collective-permute-start(bf16[6,256,128]{2,1,0:T(8,128)(2,1)S(1)} %bitcast.16), channel_id=1, source_target_pairs={{0,8},{8,16},{16,24},{24,0},{32,40},{40,48},{48,56},{56,32},{64,72... | collective-permute-start | bytes 1179656 | tf_op jit(solution)/shard_map/ppermute | solution.py:533
  27.3 3.9 %collective-permute-done.k_r.refs_3_ = bf16[6,256,128]{2,1,0:T(8,128)(2,1)} collective-permute-done((bf16[6,256,128]{2,1,0:T(8,128)(2,1)S(1)}, bf16[6,256,128]{2,1,0:T(8,128)(2,1)}, u32[]{:S(2)}, u32[]{:S(2)}) %collective-permute-start) | collective-permute-done | bytes 393248 | tf_op jit(solution)/shard_map/ppermute | solution.py:533
  31.6 2.9 %collective-permute-start.5 = (bf16[6,256,128]{2,1,0:T(8,128)(2,1)}, bf16[6,256,128]{2,1,0:T(8,128)(2,1)S(1)}, u32[]{:S(2)}, u32[]{:S(2)}) collective-permute-start(bf16[6,256,128]{2,1,0:T(8,128)(2,1)} %collective-permute-done.3.v_l.refs_7_), channel_id=1, source_target_pairs={{0,24},{8,0},{16,8},{24,16},{32,56},{40,32},{48,40},{56,48},{64,88... | collective-permute-start | bytes 1179656 | tf_op jit(solution)/shard_map/ppermute | solution.py:533
  34.5 5.4 %collective-permute-done.1.k_l.refs_4_ = bf16[6,256,128]{2,1,0:T(8,128)(2,1)S(1)} collective-permute-done((bf16[6,256,128]{2,1,0:T(8,128)(2,1)S(1)}, bf16[6,256,128]{2,1,0:T(8,128)(2,1)S(1)}, u32[]{:S(2)}, u32[]{:S(2)}) %collective-permute-start.1) | collective-permute-done | bytes 393248 | tf_op jit(solution)/shard_map/ppermute | solution.py:533
  43.7 2.7 %prompt_near.2.refs_5_ = f32[1024,256]{1,0:T(8,128)S(1)} custom-call(s32[128]{0:T(128)S(1)} %copy-done.14, s32[1]{0:T(128)} %bitcast.at_ref.refs_1_, bf16[6,256,128]{2,1,0:T(8,128)(2,1)} %bitcast.8, bf16[6,256,128]{2,1,0:T(8,128)(2,1)} %collective-permute-done.k_r.refs_3_, bf16[6,256,128]{2,1,0:T(8,128)(2,1)} %copy-done.4, bf16[6,256,128]{2,1,0:T(8,128)(2,1)} %bitcast.13, ...), custom_call_target="tpu_custom_call" | custom-call | tf_op jit(solution)/shard_map/prompt_near/pallas_call | solution.py:181
  46.6 2.7 %collective-permute-done.8.refs_8_.refs_4_ = bf16[1024,128]{1,0:T(8,128)(2,1)} collective-permute-done((bf16[1024,128]{1,0:T(8,128)(2,1)}, bf16[1024,128]{1,0:T(8,128)(2,1)}, u32[]{:S(2)}, u32[]{:S(2)}) %collective-permute-start.8) | collective-permute-done | bytes 262176 | tf_op jit(solution)/shard_map/ppermute | solution.py:536
  49.3 3.7 %prompt_near.3 = (f32[1024,256]{1,0:T(8,128)S(1)}, f32[1024,256]{1,0:T(8,128)S(1)}) custom-call(s32[128]{0:T(128)S(1)} %copy-done.14, s32[1]{0:T(128)} %bitcast.at_ref.refs_1_, bf16[6,256,128]{2,1,0:T(8,128)(2,1)} %bitcast.9, bf16[6,256,128]{2,1,0:T(8,128)(2,1)} %collective-permute-done.k_r.refs_3_, bf16[6,256,128]{2,1,0:T(8,128)(2,1)} %copy-done.4, ...), custom_call_target="tpu_custom_call" | custom-call | tf_op jit(solution)/shard_map/prompt_near/pallas_call | solution.py:181
  55.6 1.9 %prompt_far.3 = (bf16[1040,128]{1,0:T(8,128)(2,1)S(1)}, bf16[1040,128]{1,0:T(8,128)(2,1)S(1)}) custom-call(s32[128]{0:T(128)S(1)} %copy-done.14, s32[1]{0:T(128)} %bitcast.at_ref.refs_1_, bf16[6,256,128]{2,1,0:T(8,128)(2,1)S(1)} %collective-permute-done.4.k_o.refs_2_, bf16[6,256,128]{2,1,0:T(8,128)(2,1)S(1)} %collective-permute-done.5.v_o.refs_3_, ...), custom_call_target="tpu_custom_call" | custom-call | tf_op jit(solution)/shard_map/prompt_far/pallas_call | solution.py:218
  57.5 1.7 %collective-permute-start.10 = (bf16[1040,128]{1,0:T(8,128)(2,1)S(1)}, bf16[1040,128]{1,0:T(8,128)(2,1)S(1)}, u32[]{:S(2)}, u32[]{:S(2)}) collective-permute-start(bf16[1040,128]{1,0:T(8,128)(2,1)S(1)} %get-tuple-element.21), channel_id=1, source_target_pairs={{0,96},{8,104},{16,112},{24,120},{32,0},{40,8},{48,16},{56,24},{64... | collective-permute-start | bytes 798728 | tf_op jit(solution)/shard_map/ppermute | solution.py:536
  59.6 7.2 %home_attention.1.refs_0_ = f32[1024,256]{1,0:T(8,128)S(1)} custom-call(s32[128]{0:T(128)S(1)} %copy-done.14, s32[1]{0:T(128)} %bitcast.at_ref.refs_1_, s32[8]{0:T(128)S(1)} %copy-done.15, bf16[1024,128]{1,0:T(8,128)(2,1)} %get-tuple-element.16.q_ref, bf16[6,256,128]{2,1,0:T(8,128)(2,1)S(1)} %bitcast.12, ...), custom_call_target="tpu_custom_call" | custom-call | tf_op jit(solution)/shard_map/home_attention/pallas_call | solution.py:308
  69.7 2.3 %out_proj.3 = (bf16[256,640]{1,0:T(8,128)(2,1)S(1)}, bf16[256,640]{1,0:T(8,128)(2,1)S(1)}) custom-call(bf16[256,512]{1,0:T(8,128)(2,1)S(1)} %merge.1.mine_ref.refs_0_, bf16[256,512]{1,0:T(8,128)(2,1)S(1)} %collective-permute-done.12.other_ref, bf16[4,512,640]{2,1,0:T(8,128)(2,1)S(1)} %get-tuple-element.23.refs_0_.refs_1_, ...), custom_call_target="tpu_custom_call" | custom-call | tf_op jit(solution)/shard_map/out_proj/pallas_call | solution.py:482
  73.5 1.7 %collective-permute-start.16 = (bf16[256,640]{1,0:T(8,128)(2,1)S(1)}, bf16[256,640]{1,0:T(8,128)(2,1)S(1)}, u32[]{:S(2)}, u32[]{:S(2)}) collective-permute-start(bf16[256,640]{1,0:T(8,128)(2,1)S(1)} %get-tuple-element.28), channel_id=1, source_target_pairs={{0,6},{1,7},{2,0},{3,1},{4,2},{5,3},{6,4},{7,5},{8,14},{9,15},{10,... | collective-permute-start | bytes 983048 | tf_op jit(solution)/shard_map/ppermute | solution.py:539
  76.8 1.9 %collective-permute-start.14 = (bf16[256,640]{1,0:T(8,128)(2,1)S(1)}, bf16[256,640]{1,0:T(8,128)(2,1)S(1)}, u32[]{:S(2)}, u32[]{:S(2)}) collective-permute-start(bf16[256,640]{1,0:T(8,128)(2,1)S(1)} %out_second.1), channel_id=1, source_target_pairs={{0,4},{1,5},{2,6},{3,7},{4,0},{5,1},{6,2},{7,3},{8,12},{9,13},{10,... | collective-permute-start | bytes 983048 | tf_op jit(solution)/shard_map/ppermute | solution.py:539
  78.7 1.7 %out_proj.2.own_ref = f32[256,640]{1,0:T(8,128)S(1)} custom-call(bf16[256,512]{1,0:T(8,128)(2,1)S(1)} %merge.1.mine_ref.refs_0_, bf16[256,512]{1,0:T(8,128)(2,1)S(1)} %collective-permute-done.12.other_ref, bf16[4,512,640]{2,1,0:T(8,128)(2,1)S(1)} %get-tuple-element.23.refs_0_.refs_1_, bf16[4,512,640]{2,1,0:T(8,128)(2,1)} %collective-permute-done.13.refs_1_.refs_2_.refs_3_), custom_call_target="tpu_custom_call" | custom-call | tf_op jit(solution)/shard_map/out_proj/pallas_call | solution.py:482
  80.4 2.6 %collective-permute-done.15.b_ref = bf16[256,640]{1,0:T(8,128)(2,1)S(1)} collective-permute-done((bf16[256,640]{1,0:T(8,128)(2,1)S(1)}, bf16[256,640]{1,0:T(8,128)(2,1)S(1)}, u32[]{:S(2)}, u32[]{:S(2)}) %collective-permute-start.15) | collective-permute-done | bytes 327712 | tf_op jit(solution)/shard_map/ppermute | solution.py:539
  83.0 6.3 %collective-permute-done.16.c_ref = bf16[256,640]{1,0:T(8,128)(2,1)S(1)} collective-permute-done((bf16[256,640]{1,0:T(8,128)(2,1)S(1)}, bf16[256,640]{1,0:T(8,128)(2,1)S(1)}, u32[]{:S(2)}, u32[]{:S(2)}) %collective-permute-start.16) | collective-permute-done | bytes 327712 | tf_op jit(solution)/shard_map/ppermute | solution.py:539
  89.3 1.7 %collective-permute-done.14.a_ref = bf16[256,640]{1,0:T(8,128)(2,1)S(1)} collective-permute-done((bf16[256,640]{1,0:T(8,128)(2,1)S(1)}, bf16[256,640]{1,0:T(8,128)(2,1)S(1)}, u32[]{:S(2)}, u32[]{:S(2)}) %collective-permute-start.14) | collective-permute-done | bytes 327712 | tf_op jit(solution)/shard_map/ppermute | solution.py:539
  (55 shorter events, 15.6 us)
Async XLA Ops:
  6.2 63.5 %collective-permute-start.13 = (bf16[4,512,640]{2,1,0:T(8,128)(2,1)}, bf16[4,512,640]{2,1,0:T(8,128)(2,1)}, u32[]{:S(2)}, u32[]{:S(2)}) collective-permute-start(bf16[4,512,640]{2,1,0:T(8,128)(2,1)} %get-tuple-element.24), channel_id=1, source_target_pairs={{0,1},{1,0},{2,3},{3,2},{4,5},{5,4},{6,7},{7,6},{8,9},{9,8},{10,11... | collective-permute-start | bytes 7864328 | tf_op jit(solution)/shard_map/ppermute | solution.py:542
  6.3 11.6 %copy-start = (bf16[6,256,1,128]{3,1,2,0:T(8,128)(2,1)S(1)}, bf16[6,256,1,128]{3,1,2,0:T(8,128)(2,1)}, u32[]{:S(2)}) copy-start(bf16[6,256,1,128]{3,1,2,0:T(8,128)(2,1)} %param.21) | copy-start | bytes 1179652
  6.3 13.2 %copy-start.2 = (bf16[6,256,1,128]{3,1,2,0:T(8,128)(2,1)S(1)}, bf16[6,256,1,128]{3,1,2,0:T(8,128)(2,1)}, u32[]{:S(2)}) copy-start(bf16[6,256,1,128]{3,1,2,0:T(8,128)(2,1)} %param.22) | copy-start | bytes 1179652
  6.3 36.4 %copy-start.14 = (s32[128]{0:T(128)S(1)}, s32[128]{0:T(128)}, u32[]{:S(2)}) copy-start(s32[128]{0:T(128)} %refs_0_.7) | copy-start | bytes 1540
  13.9 11.2 %collective-permute-start.6 = (bf16[1024,128]{1,0:T(8,128)(2,1)}, bf16[1024,128]{1,0:T(8,128)(2,1)S(1)}, u32[]{:S(2)}, u32[]{:S(2)}) collective-permute-start(bf16[1024,128]{1,0:T(8,128)(2,1)} %get-tuple-element.16.q_ref), channel_id=1, source_target_pairs={{0,64},{8,72},{16,80},{24,88},{32,96},{40,104},{48,112},{56,120},{... | collective-permute-start | bytes 786440 | tf_op jit(solution)/shard_map/ppermute | solution.py:536
  17.9 13.3 %collective-permute-start = (bf16[6,256,128]{2,1,0:T(8,128)(2,1)S(1)}, bf16[6,256,128]{2,1,0:T(8,128)(2,1)}, u32[]{:S(2)}, u32[]{:S(2)}) collective-permute-start(bf16[6,256,128]{2,1,0:T(8,128)(2,1)S(1)} %bitcast.10), channel_id=1, source_target_pairs={{0,8},{8,16},{16,24},{24,0},{32,40},{40,48},{48,56},{56,32},{64,72... | collective-permute-start | bytes 1179656 | tf_op jit(solution)/shard_map/ppermute | solution.py:533
  19.5 12.1 %collective-permute-start.3 = (bf16[6,256,128]{2,1,0:T(8,128)(2,1)S(1)}, bf16[6,256,128]{2,1,0:T(8,128)(2,1)}, u32[]{:S(2)}, u32[]{:S(2)}) collective-permute-start(bf16[6,256,128]{2,1,0:T(8,128)(2,1)S(1)} %bitcast.15), channel_id=1, source_target_pairs={{0,24},{8,0},{16,8},{24,16},{32,56},{40,32},{48,40},{56,48},{64,88... | collective-permute-start | bytes 1179656 | tf_op jit(solution)/shard_map/ppermute | solution.py:533
  21.2 18.7 %collective-permute-start.1 = (bf16[6,256,128]{2,1,0:T(8,128)(2,1)S(1)}, bf16[6,256,128]{2,1,0:T(8,128)(2,1)S(1)}, u32[]{:S(2)}, u32[]{:S(2)}) collective-permute-start(bf16[6,256,128]{2,1,0:T(8,128)(2,1)S(1)} %bitcast.11), channel_id=1, source_target_pairs={{0,24},{8,0},{16,8},{24,16},{32,56},{40,32},{48,40},{56,48},{64,88... | collective-permute-start | bytes 1179656 | tf_op jit(solution)/shard_map/ppermute | solution.py:533
  25.8 14.9 %collective-permute-start.2 = (bf16[6,256,128]{2,1,0:T(8,128)(2,1)S(1)}, bf16[6,256,128]{2,1,0:T(8,128)(2,1)S(1)}, u32[]{:S(2)}, u32[]{:S(2)}) collective-permute-start(bf16[6,256,128]{2,1,0:T(8,128)(2,1)S(1)} %bitcast.16), channel_id=1, source_target_pairs={{0,8},{8,16},{16,24},{24,0},{32,40},{40,48},{48,56},{56,32},{64,72... | collective-permute-start | bytes 1179656 | tf_op jit(solution)/shard_map/ppermute | solution.py:533
  31.2 21.8 %collective-permute-start.4 = (bf16[6,256,128]{2,1,0:T(8,128)(2,1)}, bf16[6,256,128]{2,1,0:T(8,128)(2,1)S(1)}, u32[]{:S(2)}, u32[]{:S(2)}) collective-permute-start(bf16[6,256,128]{2,1,0:T(8,128)(2,1)} %collective-permute-done.k_r.refs_3_), channel_id=1, source_target_pairs={{0,8},{8,16},{16,24},{24,0},{32,40},{40,48},{48,56},{56,32},{64,72... | collective-permute-start | bytes 1179656 | tf_op jit(solution)/shard_map/ppermute | solution.py:533
  31.6 21.5 %collective-permute-start.5 = (bf16[6,256,128]{2,1,0:T(8,128)(2,1)}, bf16[6,256,128]{2,1,0:T(8,128)(2,1)S(1)}, u32[]{:S(2)}, u32[]{:S(2)}) collective-permute-start(bf16[6,256,128]{2,1,0:T(8,128)(2,1)} %collective-permute-done.3.v_l.refs_7_), channel_id=1, source_target_pairs={{0,24},{8,0},{16,8},{24,16},{32,56},{40,32},{48,40},{56,48},{64,88... | collective-permute-start | bytes 1179656 | tf_op jit(solution)/shard_map/ppermute | solution.py:533
  39.9 6.7 %collective-permute-start.9 = (bf16[1024,128]{1,0:T(8,128)(2,1)}, bf16[1024,128]{1,0:T(8,128)(2,1)}, u32[]{:S(2)}, u32[]{:S(2)}) collective-permute-start(bf16[1024,128]{1,0:T(8,128)(2,1)} %get-tuple-element.16.q_ref), channel_id=1, source_target_pairs={{0,96},{8,104},{16,112},{24,120},{32,0},{40,8},{48,16},{56,24},{64... | collective-permute-start | bytes 786440 | tf_op jit(solution)/shard_map/ppermute | solution.py:536
  41.4 7.9 %collective-permute-start.8 = (bf16[1024,128]{1,0:T(8,128)(2,1)}, bf16[1024,128]{1,0:T(8,128)(2,1)}, u32[]{:S(2)}, u32[]{:S(2)}) collective-permute-start(bf16[1024,128]{1,0:T(8,128)(2,1)} %get-tuple-element.16.q_ref), channel_id=1, source_target_pairs={{0,32},{8,40},{16,48},{24,56},{32,64},{40,72},{48,80},{56,88},{64,... | collective-permute-start | bytes 786440 | tf_op jit(solution)/shard_map/ppermute | solution.py:536
  43.7 9.4 %copy-start.10 = (bf16[1024,128]{1,0:T(8,128)(2,1)S(1)}, bf16[1024,128]{1,0:T(8,128)(2,1)}, u32[]{:S(2)}) copy-start(bf16[1024,128]{1,0:T(8,128)(2,1)} %copy-done.8) | copy-start | bytes 786436
  53.0 6.6 %copy-start.1 = (bf16[6,256,1,128]{3,1,2,0:T(8,128)(2,1)S(1)}, bf16[6,256,1,128]{3,1,2,0:T(8,128)(2,1)}, u32[]{:S(2)}) copy-start(bf16[6,256,1,128]{3,1,2,0:T(8,128)(2,1)} %param.21) | copy-start | bytes 1179652
  54.2 12.6 %collective-permute-start.7 = (bf16[1040,128]{1,0:T(8,128)(2,1)S(1)}, bf16[1040,128]{1,0:T(8,128)(2,1)S(1)}, u32[]{:S(2)}, u32[]{:S(2)}) collective-permute-start(bf16[1040,128]{1,0:T(8,128)(2,1)S(1)} %prompt_far.2), channel_id=1, source_target_pairs={{0,64},{8,72},{16,80},{24,88},{32,96},{40,104},{48,112},{56,120},{... | collective-permute-start | bytes 798728 | tf_op jit(solution)/shard_map/ppermute | solution.py:536
  57.5 9.3 %collective-permute-start.10 = (bf16[1040,128]{1,0:T(8,128)(2,1)S(1)}, bf16[1040,128]{1,0:T(8,128)(2,1)S(1)}, u32[]{:S(2)}, u32[]{:S(2)}) collective-permute-start(bf16[1040,128]{1,0:T(8,128)(2,1)S(1)} %get-tuple-element.21), channel_id=1, source_target_pairs={{0,96},{8,104},{16,112},{24,120},{32,0},{40,8},{48,16},{56,24},{64... | collective-permute-start | bytes 798728 | tf_op jit(solution)/shard_map/ppermute | solution.py:536
  59.2 8.7 %collective-permute-start.11 = (bf16[1040,128]{1,0:T(8,128)(2,1)S(1)}, bf16[1040,128]{1,0:T(8,128)(2,1)S(1)}, u32[]{:S(2)}, u32[]{:S(2)}) collective-permute-start(bf16[1040,128]{1,0:T(8,128)(2,1)S(1)} %get-tuple-element.22), channel_id=1, source_target_pairs={{0,32},{8,40},{16,48},{24,56},{32,64},{40,72},{48,80},{56,88},{64,... | collective-permute-start | bytes 798728 | tf_op jit(solution)/shard_map/ppermute | solution.py:536
  68.1 1.6 %collective-permute-start.12 = (bf16[256,512]{1,0:T(8,128)(2,1)S(1)}, bf16[256,512]{1,0:T(8,128)(2,1)S(1)}, u32[]{:S(2)}, u32[]{:S(2)}) collective-permute-start(bf16[256,512]{1,0:T(8,128)(2,1)S(1)} %merge.1.mine_ref.refs_0_), channel_id=1, source_target_pairs={{0,1},{1,0},{2,3},{3,2},{4,5},{5,4},{6,7},{7,6},{8,9},{9,8},{10,11... | collective-permute-start | bytes 786440 | tf_op jit(solution)/shard_map/ppermute | solution.py:542
  72.0 11.0 %collective-permute-start.15 = (bf16[256,640]{1,0:T(8,128)(2,1)S(1)}, bf16[256,640]{1,0:T(8,128)(2,1)S(1)}, u32[]{:S(2)}, u32[]{:S(2)}) collective-permute-start(bf16[256,640]{1,0:T(8,128)(2,1)S(1)} %get-tuple-element.27), channel_id=1, source_target_pairs={{0,2},{1,3},{2,4},{3,5},{4,6},{5,7},{6,0},{7,1},{8,10},{9,11},{10,... | collective-permute-start | bytes 983048 | tf_op jit(solution)/shard_map/ppermute | solution.py:539
  73.5 15.8 %collective-permute-start.16 = (bf16[256,640]{1,0:T(8,128)(2,1)S(1)}, bf16[256,640]{1,0:T(8,128)(2,1)S(1)}, u32[]{:S(2)}, u32[]{:S(2)}) collective-permute-start(bf16[256,640]{1,0:T(8,128)(2,1)S(1)} %get-tuple-element.28), channel_id=1, source_target_pairs={{0,6},{1,7},{2,0},{3,1},{4,2},{5,3},{6,4},{7,5},{8,14},{9,15},{10,... | collective-permute-start | bytes 983048 | tf_op jit(solution)/shard_map/ppermute | solution.py:539
  76.8 14.2 %copy-start.11 = (f32[8,8,640]{2,1,0:T(8,128)S(1)}, f32[8,8,640]{2,1,0:T(8,128)}, u32[]{:S(2)}) copy-start(f32[8,8,640]{2,1,0:T(8,128)} %get-tuple-element.29.tok_ref) | copy-start | bytes 491524
  76.8 14.2 %copy-start.13 = (s32[8,8]{1,0:T(8,128)S(1)}, s32[8,8]{1,0:T(8,128)}, u32[]{:S(2)}) copy-start(s32[8,8]{1,0:T(8,128)} %acc_ref.3) | copy-start | bytes 772
  76.8 14.2 %collective-permute-start.14 = (bf16[256,640]{1,0:T(8,128)(2,1)S(1)}, bf16[256,640]{1,0:T(8,128)(2,1)S(1)}, u32[]{:S(2)}, u32[]{:S(2)}) collective-permute-start(bf16[256,640]{1,0:T(8,128)(2,1)S(1)} %out_second.1), channel_id=1, source_target_pairs={{0,4},{1,5},{2,6},{3,7},{4,0},{5,1},{6,2},{7,3},{8,12},{9,13},{10,... | collective-permute-start | bytes 983048 | tf_op jit(solution)/shard_map/ppermute | solution.py:539
  (9 other events, 30.2 us)

commit v5 on v4

--- a/solution.py
+++ b/solution.py
@@ -376,81 +376,88 @@
     return rows
 
 
-def columns_kernel(
-    mdl_ref, acc_ref, w_hbm, tok_hbm, mine_ref, send_ref, tok_out, tok, rows_ref, sems, sem, put_sem
-):
-    count, _, cols = mine_ref.shape
+def pick_kernel(mdl_ref, acc_ref, tok_hbm, out_ref, tok, sem):
+    cols = tok.shape[1]
     get = pltpu.make_async_copy(
         tok_hbm.at[:, pl.ds(pl.multiple_of(mdl_ref[0] * cols, 128), cols)], tok, sem
     )
     get.start()
-    copies = []
-    for i in range(count):
-        there = lax.rem(mdl_ref[0] // 2 + i, count)
-        for j, ref in enumerate((mine_ref, send_ref)):
-            side = lax.rem(mdl_ref[0] + j, 2)
-            start = pl.multiple_of((2 * there + side) * cols, 128)
-            c = pltpu.make_async_copy(w_hbm.at[:, pl.ds(start, cols)], ref.at[i], sems.at[j, i])
-            c.start()
-            copies.append(c)
     get.wait()
     for r, row in enumerate(pick(acc_ref, tok[...], tok.shape[0] // acc_ref.shape[0])):
-        rows_ref[r] = row
-    put = pltpu.make_async_copy(rows_ref, tok_out, put_sem)
-    put.start()
+        out_ref[r] = row
+
+
+def pick_call(mdl, accepted, tokens, cols):
+    return pl.pallas_call(
+        pick_kernel,
+        in_specs=[SMEM, VM, HBM],
+        out_specs=VM,
+        out_shape=jax.ShapeDtypeStruct(accepted.shape + (cols,), F32),
+        scratch_shapes=[pltpu.VMEM((tokens.shape[0], cols), BF16), pltpu.SemaphoreType.DMA],
+        compiler_params=params(4),
+        name="pick_tokens",
+    )(mdl, accepted, tokens)
+
+
+def columns_of(mdl_ref, w_hbm, shift, side, count, cols):
+    there = lax.rem(mdl_ref[0] // 2 + shift, count)
+    start = (2 * there + lax.rem(mdl_ref[0] + side, 2)) * cols
+    return w_hbm.at[:, pl.ds(pl.multiple_of(start, 128), cols)]
+
+
+def columns_kernel(mdl_ref, w_hbm, send_ref, sems):
+    count, _, cols = send_ref.shape
+    copies = [
+        pltpu.make_async_copy(
+            columns_of(mdl_ref, w_hbm, i, 1, count, cols), send_ref.at[i], sems.at[i]
+        )
+        for i in range(count)
+    ]
+    for c in copies:
+        c.start()
     for c in copies:
         c.wait()
-    put.wait()
-
-
-def columns_call(mdl, accepted, w_out, tokens, count):
+
+
+def columns_call(mdl, w_out, count):
     cols = w_out.shape[1] // (2 * count)
     return pl.pallas_call(
         columns_kernel,
+        in_specs=[SMEM, HBM],
+        out_specs=VM,
+        out_shape=jax.ShapeDtypeStruct((count, w_out.shape[0], cols), BF16),
+        scratch_shapes=[pltpu.SemaphoreType.DMA((count,))],
+        compiler_params=params(6),
+        name="out_columns",
+    )(mdl, w_out)
+
+
+def first_kernel(mdl_ref, mine_ref, w_hbm, other_hbm, out_ref, other_ref, w, sems, *, shift):
+    count, _, cols = other_hbm.shape
+    get = pltpu.make_async_copy(columns_of(mdl_ref, w_hbm, shift, 0, count, cols), w, sems.at[0])
+    get_other = pltpu.make_async_copy(other_hbm.at[shift], other_ref, sems.at[1])
+    get.start()
+    get_other.start()
+    get.wait()
+    out_ref[...] = dot(mine_ref[...], w[...])
+    get_other.wait()
+
+
+def out_first(mdl, mine, w_out, w_other, shift):
+    rows, inner = mine.shape
+    cols = w_other.shape[2]
+    return pl.pallas_call(
+        lambda *refs: first_kernel(*refs, shift=shift),
         in_specs=[SMEM, VM, HBM, HBM],
-        out_specs=[VM, VM, HBM],
-        out_shape=[jax.ShapeDtypeStruct((count, w_out.shape[0], cols), BF16)] * 2
-        + [pltpu.HBM(accepted.shape + (cols,), F32)],
-        scratch_shapes=[
-            pltpu.VMEM((tokens.shape[0], cols), BF16),
-            pltpu.VMEM(accepted.shape + (cols,), F32),
-            pltpu.SemaphoreType.DMA((2, count)),
-            pltpu.SemaphoreType.DMA,
-            pltpu.SemaphoreType.DMA,
-        ],
-        compiler_params=params(12),
-        name="out_columns",
-    )(mdl, accepted, w_out, tokens)
-
-
-def first_kernel(mine_ref, w_ref, other_hbm, out_ref, other_ref, sem, *, shift):
-    get = pltpu.make_async_copy(other_hbm.at[shift], other_ref, sem)
-    get.start()
-    out_ref[...] = dot(mine_ref[...], w_ref[0])
-    get.wait()
-
-
-def out_first(mine, w_mine, w_other, shift):
-    rows, inner = mine.shape
-    cols = w_mine.shape[2]
-    flat = lambda i: (0, 0)
-    return pl.pallas_call(
-        lambda *refs: first_kernel(*refs, shift=shift),
-        grid=(1,),
-        in_specs=[
-            pl.BlockSpec((rows, inner), flat),
-            pl.BlockSpec((1, inner, cols), lambda i: (shift, 0, 0)),
-            HBM,
-        ],
-        out_specs=[pl.BlockSpec((rows, cols), flat), pl.BlockSpec((inner, cols), flat)],
+        out_specs=[VM, VM],
         out_shape=[
             jax.ShapeDtypeStruct((rows, cols), F32),
             jax.ShapeDtypeStruct((inner, cols), BF16),
         ],
-        scratch_shapes=[pltpu.SemaphoreType.DMA],
+        scratch_shapes=[pltpu.VMEM((inner, cols), BF16), pltpu.SemaphoreType.DMA((2,))],
         compiler_params=params(12),
         name="out_first",
-    )(mine, w_mine, w_other)
+    )(mdl, mine, w_out, w_other)
 
 
 def second_kernel(first_ref, other_ref, w_ref, out_ref):
@@ -468,26 +475,45 @@
     )(first, other, w)
 
 
-def out_kernel(mine_ref, other_ref, *refs):
-    n = len(refs) // 3
-    for wa, wb, out in zip(refs[:n], refs[n : 2 * n], refs[2 * n :]):
-        out[...] = (dot(mine_ref[...], wa[0]) + dot(other_ref[...], wb[0])).astype(out.dtype)
-
-
-def out_call(mine, other, w_mine, w_other, shifts, dtype):
+def out_kernel(mdl_ref, mine_ref, other_ref, w_hbm, wo_hbm, *refs, shifts):
+    outs = refs[: len(shifts)]
+    wa, wb, sems = refs[len(shifts) :]
+    count, _, cols = wo_hbm.shape
+    copies = []
+    for i, shift in enumerate(shifts):
+        two = (
+            pltpu.make_async_copy(
+                columns_of(mdl_ref, w_hbm, shift, 0, count, cols), wa.at[i], sems.at[0, i]
+            ),
+            pltpu.make_async_copy(wo_hbm.at[shift], wb.at[i], sems.at[1, i]),
+        )
+        for c in two:
+            c.start()
+        copies.append(two)
+    for i, out in enumerate(outs):
+        for c in copies[i]:
+            c.wait()
+        d = dot(mine_ref[...], wa[i]) + dot(other_ref[...], wb[i])
+        out[...] = d.astype(out.dtype)
+
+
+def out_call(mdl, mine, other, w_out, w_other, shifts, dtype):
     rows, inner = mine.shape
     cols = w_other.shape[2]
-    whole = pl.BlockSpec((rows, inner), lambda i: (0, 0))
-    chunks = [pl.BlockSpec((1, inner, cols), lambda i, n=n: (n, 0, 0)) for n in shifts]
-    return pl.pallas_call(
-        out_kernel,
-        grid=(1,),
-        in_specs=[whole, whole] + chunks * 2,
-        out_specs=[pl.BlockSpec((rows, cols), lambda i: (0, 0))] * len(shifts),
-        out_shape=[jax.ShapeDtypeStruct((rows, cols), dtype)] * len(shifts),
-        compiler_params=params(16),
+    n = len(shifts)
+    return pl.pallas_call(
+        lambda *refs: out_kernel(*refs, shifts=shifts),
+        in_specs=[SMEM, VM, VM, HBM, HBM],
+        out_specs=[VM] * n,
+        out_shape=[jax.ShapeDtypeStruct((rows, cols), dtype)] * n,
+        scratch_shapes=[
+            pltpu.VMEM((n, inner, cols), BF16),
+            pltpu.VMEM((n, inner, cols), BF16),
+            pltpu.SemaphoreType.DMA((2, n)),
+        ],
+        compiler_params=params(12),
         name="out_proj",
-    )(mine, other, *([w_mine] * len(shifts)), *([w_other] * len(shifts)))
+    )(mdl, mine, other, w_out, w_other)
 
 
 def last_kernel(acc_ref, own_ref, a_ref, b_ref, c_ref, tok_ref, out_ref, rows_ref):
@@ -567,23 +593,20 @@
     shifts = (2, 1, -1)
     q_far = [along_z(q, n) for n in shifts]
 
-    w_mine, w_send, picked = columns_call(mdl_at, accepted, in_hbm(w_out), in_hbm(tokens), n_x)
-    w_other = other_core(w_send)
+    w_send = columns_call(mdl_at, in_hbm(w_out), n_x)
+    w_other = in_hbm(other_core(w_send))
 
     k_o = along_y(k_r, 1)
     v_o = along_y(v_l, -1)
     near = tuple(map(in_hbm, (k, k_r, k_l, v, v_r, v_l)))
 
     turns = [n % n_z * n_y for n in shifts]
-    nears, parts = [], []
-    two = (slice(0, 1), slice(1, 3))
-    for some in two:
-        nears.append(
-            near_call(request_group, tok_at, q_far[some], near, requests, turns[some], n_tok)
-        )
-    for i, some in enumerate(two):
+    nears = near_call(request_group, tok_at, q_far, near, requests, turns, n_tok)
+    parts = []
+    for some in (slice(0, 1), slice(1, 3)):
         parts += far_call(
-            request_group, tok_at, nears[i], q_far[some], k_o, v_o, requests, turns[some], n_tok
+            request_group, tok_at, nears[some], q_far[some], k_o, v_o, requests, turns[some],
+            n_tok,
         )
     back = [along_z(part, -n) for n, part in zip(shifts, parts)]
     home = home_call(
@@ -593,12 +616,15 @@
     attended = merge_call(home, *back, requests, rows)
 
     attended_other = other_core(attended)
-    first, w_second = out_first(attended, w_mine, in_hbm(w_other), 2)
+    weights = (in_hbm(w_out), w_other)
+    first, w_second = out_first(mdl_at, attended, *weights, 2)
     far = along_x(out_second(first, attended_other, w_second), 2)
-    up, down = out_call(attended, attended_other, w_mine, w_other, (1, n_x - 1), BF16)
+    both = (mdl_at, attended, attended_other, *weights)
+    up, down = out_call(*both, (1, n_x - 1), BF16)
     up = along_x(up, 1)
     down = along_x(down, -1)
-    (own_sum,) = out_call(attended, attended_other, w_mine, w_other, (0,), F32)
+    (own_sum,) = out_call(*both, (0,), F32)
+    picked = pick_call(mdl_at, accepted, in_hbm(tokens), w_other.shape[2])
     return tuple(last_call(accepted, own_sum, far, up, down, picked))
 
 

time: 92.5 us -> 94.2 us (1.018)
  starting transfers between devices: 24.8 us -> 30.3 us
  Pallas kernels: 35.6 us -> 31.8 us
  local copies, waits for them, and re-layouts: 3.17 us -> 5.71 us
  waiting for transfers between devices: 27.5 us -> 25 us
    ppermute x6, starting transfers between devices: 9.57 us -> 13.9 us  [along_z(): lax.ppermute(v, 'tok', [(t, (t + n * n_y) % n_tok) for t in range(n_tok)])]
    unnamed x32 -> x22, local copies, waits for them, and re-layouts: 3.17 us -> 5.71 us
    pallas_call x2 -> x1, Pallas kernels: 6.39 us -> 4.33 us  [near_call(): pl.pallas_call(lambda *refs: near_kernel(*refs, requests=requests, shifts...]
    ppermute x3, waiting for transfers between devices: 10.7 us -> 8.84 us  [along_x(): lax.ppermute(v, 'mdl', [(m, (m + 2 * n) % n_mdl) for m in range(n_mdl)])]
    ppermute x6, starting transfers between devices: 9.86 us -> 11.1 us  [along_y(): return lax.ppermute(v, 'tok', perm)]
    pallas_call x4 -> x5, Pallas kernels: 9.93 us -> 8.82 us  [the longest x2 4.38 us: out_call(): pl.pallas_call(lambda *refs: out_kernel(*refs, shifts=shifts), in_specs=[...]
  transfers between devices with their start and end apart: 17 -> 17, of which waited for: 10 -> 10; matrix products, arithmetic and copies ran while one was open for 0% -> 0% of each run, Pallas kernels for 30% -> 28%
where the time goes in v5:
time: 94.2 us; the launch traced here: 93.6 us
  Pallas kernels  31.8 us (34%)
  starting transfers between devices  30.3 us (32%)
  waiting for transfers between devices  25 us (27%)
  local copies, waits for them, and re-layouts  5.71 us (6%)
    ppermute x6, starting transfers between devices, along_z(): lax.ppermute(v, 'tok', [(t, (t + n * n_y) % n_tok) for t in range(n_tok)])  13.9 us
    ppermute x6, starting transfers between devices, along_y(): return lax.ppermute(v, 'tok', perm)  11.1 us
    ppermute x3, waiting for transfers between devices, along_x(): lax.ppermute(v, 'mdl', [(m, (m + 2 * n) % n_mdl) for m in range(n_mdl)])  8.84 us
    ppermute x6, waiting for transfers between devices, along_y(): return lax.ppermute(v, 'tok', perm)  8.7 us
    pallas_call x1, Pallas kernels, home_call(): pl.pallas_call(home_kernel, in_specs=[SMEM, SMEM, SMEM] + [VM] * 11 + [HB...  7.62 us
    pallas_call x1, Pallas kernels, project_call(): pl.pallas_call(project_kernel, in_specs=[HBM] * 8, out_specs=[VM, VM, VM]...  7 us
    ppermute x6, waiting for transfers between devices, along_z(): lax.ppermute(v, 'tok', [(t, (t + n * n_y) % n_tok) for t in range(n_tok)])  5.93 us
    unnamed x22, local copies, waits for them, and re-layouts  5.71 us
  transfers between devices with their start and end apart: 17, of which 10 were waited for; matrix products, arithmetic and copies ran while one was open for 0% of the time, Pallas kernels for 28%

profile of v5, /device:TPU:0, one launch (start us, length us, event | category | flops | bytes accessed | tf_op | source)
XLA Modules:
  0.0 93.6 jit_solution(7389176036225527001)
XLA Ops:
  0.6 1.7 %out_columns.1 = bf16[4,512,640]{2,1,0:T(8,128)(2,1)S(1)} custom-call(s32[1]{0:T(128)} %bitcast.mdl_ref.refs_0_, bf16[512,5120]{1,0:T(8,128)(2,1)} %refs_3_.3), custom_call_target="tpu_custom_call" | custom-call | tf_op jit(solution)/shard_map/out_columns/pallas_call | solution.py:424
  2.5 7.0 %projections.1 = (bf16[1024,128]{1,0:T(8,128)(2,1)S(1)}, bf16[256,128]{1,0:T(8,128)(2,1)S(1)}, bf16[256,128]{1,0:T(8,128)(2,1)S(1)}) custom-call(s32[8]{0:T(128)} %len_ref.1, bf16[256,5120]{1,0:T(8,128)(2,1)} %tok_hbm.3, bf16[40,128]{1,0:T(8,128)(2,1)} %bitcast.12, bf16[5120,512]{1,0:T(8,128)(2,1)} %wq_hbm.1, bf16[5120,128]{1,0:T(8,128)(2,1)} %wk_hbm.1, ...), custom_call_target="tpu_custom_call" | custom-call | tf_op jit(solution)/shard_map/projections/pallas_call | solution.py:130
  9.5 4.1 %collective-permute-start.6 = (bf16[1024,128]{1,0:T(8,128)(2,1)S(1)}, bf16[1024,128]{1,0:T(8,128)(2,1)S(1)}, u32[]{:S(2)}, u32[]{:S(2)}) collective-permute-start(bf16[1024,128]{1,0:T(8,128)(2,1)S(1)} %get-tuple-element.14.q_ref), channel_id=1, source_target_pairs={{0,64},{8,72},{16,80},{24,88},{32,96},{40,104},{48,112},{56,120},{... | collective-permute-start | bytes 786440 | tf_op jit(solution)/shard_map/ppermute | solution.py:562
  13.6 1.6 %collective-permute-start = (bf16[6,256,128]{2,1,0:T(8,128)(2,1)}, bf16[6,256,128]{2,1,0:T(8,128)(2,1)}, u32[]{:S(2)}, u32[]{:S(2)}) collective-permute-start(bf16[6,256,128]{2,1,0:T(8,128)(2,1)} %bitcast.4.k.refs_2_), channel_id=1, source_target_pairs={{0,8},{8,16},{16,24},{24,0},{32,40},{40,48},{48,56},{56,32},{64,72... | collective-permute-start | bytes 1179656 | tf_op jit(solution)/shard_map/ppermute | solution.py:559
  15.1 1.7 %collective-permute-start.3 = (bf16[6,256,128]{2,1,0:T(8,128)(2,1)}, bf16[6,256,128]{2,1,0:T(8,128)(2,1)}, u32[]{:S(2)}, u32[]{:S(2)}) collective-permute-start(bf16[6,256,128]{2,1,0:T(8,128)(2,1)} %bitcast.5.v.refs_5_), channel_id=1, source_target_pairs={{0,24},{8,0},{16,8},{24,16},{32,56},{40,32},{48,40},{56,48},{64,88... | collective-permute-start | bytes 1179656 | tf_op jit(solution)/shard_map/ppermute | solution.py:559
  17.8 2.9 %collective-permute-done.6.refs_8_.refs_4_ = bf16[1024,128]{1,0:T(8,128)(2,1)S(1)} collective-permute-done((bf16[1024,128]{1,0:T(8,128)(2,1)S(1)}, bf16[1024,128]{1,0:T(8,128)(2,1)S(1)}, u32[]{:S(2)}, u32[]{:S(2)}) %collective-permute-start.6) | collective-permute-done | bytes 262176 | tf_op jit(solution)/shard_map/ppermute | solution.py:562
  21.4 3.2 %collective-permute-start.8 = (bf16[1024,128]{1,0:T(8,128)(2,1)S(1)}, bf16[1024,128]{1,0:T(8,128)(2,1)S(1)}, u32[]{:S(2)}, u32[]{:S(2)}) collective-permute-start(bf16[1024,128]{1,0:T(8,128)(2,1)S(1)} %get-tuple-element.14.q_ref), channel_id=1, source_target_pairs={{0,96},{8,104},{16,112},{24,120},{32,0},{40,8},{48,16},{56,24},{64... | collective-permute-start | bytes 786440 | tf_op jit(solution)/shard_map/ppermute | solution.py:562
  26.9 3.0 %collective-permute-start.1 = (bf16[6,256,128]{2,1,0:T(8,128)(2,1)}, bf16[6,256,128]{2,1,0:T(8,128)(2,1)}, u32[]{:S(2)}, u32[]{:S(2)}) collective-permute-start(bf16[6,256,128]{2,1,0:T(8,128)(2,1)} %bitcast.4.k.refs_2_), channel_id=1, source_target_pairs={{0,24},{8,0},{16,8},{24,16},{32,56},{40,32},{48,40},{56,48},{64,88... | collective-permute-start | bytes 1179656 | tf_op jit(solution)/shard_map/ppermute | solution.py:559
  30.7 1.6 %collective-permute-start.2 = (bf16[6,256,128]{2,1,0:T(8,128)(2,1)}, bf16[6,256,128]{2,1,0:T(8,128)(2,1)}, u32[]{:S(2)}, u32[]{:S(2)}) collective-permute-start(bf16[6,256,128]{2,1,0:T(8,128)(2,1)} %bitcast.5.v.refs_5_), channel_id=1, source_target_pairs={{0,8},{8,16},{16,24},{24,0},{32,40},{40,48},{48,56},{56,32},{64,72... | collective-permute-start | bytes 1179656 | tf_op jit(solution)/shard_map/ppermute | solution.py:559
  32.3 1.6 %collective-permute-start.4 = (bf16[6,256,128]{2,1,0:T(8,128)(2,1)}, bf16[6,256,128]{2,1,0:T(8,128)(2,1)S(1)}, u32[]{:S(2)}, u32[]{:S(2)}) collective-permute-start(bf16[6,256,128]{2,1,0:T(8,128)(2,1)} %collective-permute-done.k_r.refs_3_), channel_id=1, source_target_pairs={{0,8},{8,16},{16,24},{24,0},{32,40},{40,48},{48,56},{56,32},{64,72... | collective-permute-start | bytes 1179656 | tf_op jit(solution)/shard_map/ppermute | solution.py:559
  33.9 1.7 %collective-permute-start.5 = (bf16[6,256,128]{2,1,0:T(8,128)(2,1)}, bf16[6,256,128]{2,1,0:T(8,128)(2,1)S(1)}, u32[]{:S(2)}, u32[]{:S(2)}) collective-permute-start(bf16[6,256,128]{2,1,0:T(8,128)(2,1)} %collective-permute-done.3.v_l.refs_7_), channel_id=1, source_target_pairs={{0,24},{8,0},{16,8},{24,16},{32,56},{40,32},{48,40},{56,48},{64,88... | collective-permute-start | bytes 1179656 | tf_op jit(solution)/shard_map/ppermute | solution.py:559
  35.5 4.1 %collective-permute-done.1.k_l.refs_4_ = bf16[6,256,128]{2,1,0:T(8,128)(2,1)} collective-permute-done((bf16[6,256,128]{2,1,0:T(8,128)(2,1)}, bf16[6,256,128]{2,1,0:T(8,128)(2,1)}, u32[]{:S(2)}, u32[]{:S(2)}) %collective-permute-start.1) | collective-permute-done | bytes 393248 | tf_op jit(solution)/shard_map/ppermute | solution.py:559
  39.7 4.5 %collective-permute-done.2.v_r.refs_6_ = bf16[6,256,128]{2,1,0:T(8,128)(2,1)} collective-permute-done((bf16[6,256,128]{2,1,0:T(8,128)(2,1)}, bf16[6,256,128]{2,1,0:T(8,128)(2,1)}, u32[]{:S(2)}, u32[]{:S(2)}) %collective-permute-start.2) | collective-permute-done | bytes 393248 | tf_op jit(solution)/shard_map/ppermute | solution.py:559
  47.1 4.3 %prompt_near.1 = (f32[1024,256]{1,0:T(8,128)S(1)}, f32[1024,256]{1,0:T(8,128)S(1)}, f32[1024,256]{1,0:T(8,128)S(1)}) custom-call(s32[128]{0:T(128)S(1)} %copy-done.9, s32[1]{0:T(128)} %bitcast.1.at_ref.refs_1_, bf16[6,256,128]{2,1,0:T(8,128)(2,1)} %bitcast.4.k.refs_2_, bf16[6,256,128]{2,1,0:T(8,128)(2,1)} %collective-permute-done.k_r.refs_3_, ...), custom_call_target="tpu_custom_call" | custom-call | tf_op jit(solution)/shard_map/prompt_near/pallas_call | solution.py:181
  52.9 3.8 %collective-permute-start.10 = (bf16[1040,128]{1,0:T(8,128)(2,1)S(1)}, bf16[1040,128]{1,0:T(8,128)(2,1)S(1)}, u32[]{:S(2)}, u32[]{:S(2)}) collective-permute-start(bf16[1040,128]{1,0:T(8,128)(2,1)S(1)} %get-tuple-element.20), channel_id=1, source_target_pairs={{0,96},{8,104},{16,112},{24,120},{32,0},{40,8},{48,16},{56,24},{64... | collective-permute-start | bytes 798728 | tf_op jit(solution)/shard_map/ppermute | solution.py:562
  57.7 1.8 %collective-permute-start.9 = (bf16[1040,128]{1,0:T(8,128)(2,1)S(1)}, bf16[1040,128]{1,0:T(8,128)(2,1)S(1)}, u32[]{:S(2)}, u32[]{:S(2)}) collective-permute-start(bf16[1040,128]{1,0:T(8,128)(2,1)S(1)} %prompt_far.2), channel_id=1, source_target_pairs={{0,64},{8,72},{16,80},{24,88},{32,96},{40,104},{48,112},{56,120},{... | collective-permute-start | bytes 798728 | tf_op jit(solution)/shard_map/ppermute | solution.py:562
  59.6 7.6 %home_attention.1.refs_0_ = f32[1024,256]{1,0:T(8,128)S(1)} custom-call(s32[128]{0:T(128)S(1)} %copy-done.9, s32[1]{0:T(128)} %bitcast.1.at_ref.refs_1_, s32[8]{0:T(128)S(1)} %copy-done.10, bf16[1024,128]{1,0:T(8,128)(2,1)S(1)} %copy-done.7, bf16[6,256,128]{2,1,0:T(8,128)(2,1)} %bitcast.4.k.refs_2_, bf16[6,256,128]{2,1,0:T(8,128)(2,1)} %collective-permute-done.k_r.refs_3_, ...), custom_call_target="tpu_custom_call" | custom-call | tf_op jit(solution)/shard_map/home_attention/pallas_call | solution.py:308
  67.2 2.1 %collective-permute-done.11.refs_3_ = bf16[1040,128]{1,0:T(8,128)(2,1)S(1)} collective-permute-done((bf16[1040,128]{1,0:T(8,128)(2,1)S(1)}, bf16[1040,128]{1,0:T(8,128)(2,1)S(1)}, u32[]{:S(2)}, u32[]{:S(2)}) %collective-permute-start.11) | collective-permute-done | bytes 266272 | tf_op jit(solution)/shard_map/ppermute | solution.py:562
  71.2 2.5 %out_proj.3 = (bf16[256,640]{1,0:T(8,128)(2,1)S(1)}, bf16[256,640]{1,0:T(8,128)(2,1)S(1)}) custom-call(s32[1]{0:T(128)} %bitcast.mdl_ref.refs_0_, bf16[256,512]{1,0:T(8,128)(2,1)S(1)} %merge.1.refs_1_, bf16[256,512]{1,0:T(8,128)(2,1)S(1)} %collective-permute-done.12.refs_2_.other_ref, bf16[512,5120]{1,0:T(8,128)(2,1)} %refs_3_.3, ...), custom_call_target="tpu_custom_call" | custom-call | tf_op jit(solution)/shard_map/out_proj/pallas_call | solution.py:504
  75.2 1.7 %collective-permute-start.16 = (bf16[256,640]{1,0:T(8,128)(2,1)S(1)}, bf16[256,640]{1,0:T(8,128)(2,1)S(1)}, u32[]{:S(2)}, u32[]{:S(2)}) collective-permute-start(bf16[256,640]{1,0:T(8,128)(2,1)S(1)} %get-tuple-element.25), channel_id=1, source_target_pairs={{0,6},{1,7},{2,0},{3,1},{4,2},{5,3},{6,4},{7,5},{8,14},{9,15},{10,... | collective-permute-start | bytes 983048 | tf_op jit(solution)/shard_map/ppermute | solution.py:565
  78.8 1.9 %collective-permute-start.14 = (bf16[256,640]{1,0:T(8,128)(2,1)S(1)}, bf16[256,640]{1,0:T(8,128)(2,1)S(1)}, u32[]{:S(2)}, u32[]{:S(2)}) collective-permute-start(bf16[256,640]{1,0:T(8,128)(2,1)S(1)} %out_second.1), channel_id=1, source_target_pairs={{0,4},{1,5},{2,6},{3,7},{4,0},{5,1},{6,2},{7,3},{8,12},{9,13},{10,... | collective-permute-start | bytes 983048 | tf_op jit(solution)/shard_map/ppermute | solution.py:565
  81.9 1.9 %out_proj.2.own_ref = f32[256,640]{1,0:T(8,128)S(1)} custom-call(s32[1]{0:T(128)} %bitcast.mdl_ref.refs_0_, bf16[256,512]{1,0:T(8,128)(2,1)S(1)} %merge.1.refs_1_, bf16[256,512]{1,0:T(8,128)(2,1)S(1)} %collective-permute-done.12.refs_2_.other_ref, bf16[512,5120]{1,0:T(8,128)(2,1)} %refs_3_.3, bf16[4,512,640]{2,1,0:T(8,128)(2,1)} %collective-permute-done.13.refs_4_.refs_3_), custom_call_target="tpu_custom_call" | custom-call | tf_op jit(solution)/shard_map/out_proj/pallas_call | solution.py:504
  84.7 6.3 %collective-permute-done.16.c_ref = bf16[256,640]{1,0:T(8,128)(2,1)S(1)} collective-permute-done((bf16[256,640]{1,0:T(8,128)(2,1)S(1)}, bf16[256,640]{1,0:T(8,128)(2,1)S(1)}, u32[]{:S(2)}, u32[]{:S(2)}) %collective-permute-start.16) | collective-permute-done | bytes 327712 | tf_op jit(solution)/shard_map/ppermute | solution.py:565
  91.0 1.7 %collective-permute-done.14.a_ref = bf16[256,640]{1,0:T(8,128)(2,1)S(1)} collective-permute-done((bf16[256,640]{1,0:T(8,128)(2,1)S(1)}, bf16[256,640]{1,0:T(8,128)(2,1)S(1)}, u32[]{:S(2)}, u32[]{:S(2)}) %collective-permute-start.14) | collective-permute-done | bytes 327712 | tf_op jit(solution)/shard_map/ppermute | solution.py:565
  (45 shorter events, 18.5 us)
Async XLA Ops:
  2.4 68.8 %collective-permute-start.13 = (bf16[4,512,640]{2,1,0:T(8,128)(2,1)S(1)}, bf16[4,512,640]{2,1,0:T(8,128)(2,1)}, u32[]{:S(2)}, u32[]{:S(2)}) collective-permute-start(bf16[4,512,640]{2,1,0:T(8,128)(2,1)S(1)} %out_columns.1), channel_id=1, source_target_pairs={{0,1},{1,0},{2,3},{3,2},{4,5},{5,4},{6,7},{7,6},{8,9},{9,8},{10,11... | collective-permute-start | bytes 7864328 | tf_op jit(solution)/shard_map/ppermute | solution.py:568
  2.5 41.8 %copy-start.9 = (s32[128]{0:T(128)S(1)}, s32[128]{0:T(128)}, u32[]{:S(2)}) copy-start(s32[128]{0:T(128)} %refs_0_.5) | copy-start | bytes 1540
  9.5 11.2 %collective-permute-start.6 = (bf16[1024,128]{1,0:T(8,128)(2,1)S(1)}, bf16[1024,128]{1,0:T(8,128)(2,1)S(1)}, u32[]{:S(2)}, u32[]{:S(2)}) collective-permute-start(bf16[1024,128]{1,0:T(8,128)(2,1)S(1)} %get-tuple-element.14.q_ref), channel_id=1, source_target_pairs={{0,64},{8,72},{16,80},{24,88},{32,96},{40,104},{48,112},{56,120},{... | collective-permute-start | bytes 786440 | tf_op jit(solution)/shard_map/ppermute | solution.py:562
  13.6 18.7 %collective-permute-start = (bf16[6,256,128]{2,1,0:T(8,128)(2,1)}, bf16[6,256,128]{2,1,0:T(8,128)(2,1)}, u32[]{:S(2)}, u32[]{:S(2)}) collective-permute-start(bf16[6,256,128]{2,1,0:T(8,128)(2,1)} %bitcast.4.k.refs_2_), channel_id=1, source_target_pairs={{0,8},{8,16},{16,24},{24,0},{32,40},{40,48},{48,56},{56,32},{64,72... | collective-permute-start | bytes 1179656 | tf_op jit(solution)/shard_map/ppermute | solution.py:559
  15.1 18.7 %collective-permute-start.3 = (bf16[6,256,128]{2,1,0:T(8,128)(2,1)}, bf16[6,256,128]{2,1,0:T(8,128)(2,1)}, u32[]{:S(2)}, u32[]{:S(2)}) collective-permute-start(bf16[6,256,128]{2,1,0:T(8,128)(2,1)} %bitcast.5.v.refs_5_), channel_id=1, source_target_pairs={{0,24},{8,0},{16,8},{24,16},{32,56},{40,32},{48,40},{56,48},{64,88... | collective-permute-start | bytes 1179656 | tf_op jit(solution)/shard_map/ppermute | solution.py:559
  16.8 9.3 %collective-permute-start.7 = (bf16[1024,128]{1,0:T(8,128)(2,1)S(1)}, bf16[1024,128]{1,0:T(8,128)(2,1)S(1)}, u32[]{:S(2)}, u32[]{:S(2)}) collective-permute-start(bf16[1024,128]{1,0:T(8,128)(2,1)S(1)} %get-tuple-element.14.q_ref), channel_id=1, source_target_pairs={{0,32},{8,40},{16,48},{24,56},{32,64},{40,72},{48,80},{56,88},{64,... | collective-permute-start | bytes 786440 | tf_op jit(solution)/shard_map/ppermute | solution.py:562
  21.4 8.6 %collective-permute-start.8 = (bf16[1024,128]{1,0:T(8,128)(2,1)S(1)}, bf16[1024,128]{1,0:T(8,128)(2,1)S(1)}, u32[]{:S(2)}, u32[]{:S(2)}) collective-permute-start(bf16[1024,128]{1,0:T(8,128)(2,1)S(1)} %get-tuple-element.14.q_ref), channel_id=1, source_target_pairs={{0,96},{8,104},{16,112},{24,120},{32,0},{40,8},{48,16},{56,24},{64... | collective-permute-start | bytes 786440 | tf_op jit(solution)/shard_map/ppermute | solution.py:562
  26.9 12.8 %collective-permute-start.1 = (bf16[6,256,128]{2,1,0:T(8,128)(2,1)}, bf16[6,256,128]{2,1,0:T(8,128)(2,1)}, u32[]{:S(2)}, u32[]{:S(2)}) collective-permute-start(bf16[6,256,128]{2,1,0:T(8,128)(2,1)} %bitcast.4.k.refs_2_), channel_id=1, source_target_pairs={{0,24},{8,0},{16,8},{24,16},{32,56},{40,32},{48,40},{56,48},{64,88... | collective-permute-start | bytes 1179656 | tf_op jit(solution)/shard_map/ppermute | solution.py:559
  30.7 13.5 %collective-permute-start.2 = (bf16[6,256,128]{2,1,0:T(8,128)(2,1)}, bf16[6,256,128]{2,1,0:T(8,128)(2,1)}, u32[]{:S(2)}, u32[]{:S(2)}) collective-permute-start(bf16[6,256,128]{2,1,0:T(8,128)(2,1)} %bitcast.5.v.refs_5_), channel_id=1, source_target_pairs={{0,8},{8,16},{16,24},{24,0},{32,40},{40,48},{48,56},{56,32},{64,72... | collective-permute-start | bytes 1179656 | tf_op jit(solution)/shard_map/ppermute | solution.py:559
  32.3 19.1 %collective-permute-start.4 = (bf16[6,256,128]{2,1,0:T(8,128)(2,1)}, bf16[6,256,128]{2,1,0:T(8,128)(2,1)S(1)}, u32[]{:S(2)}, u32[]{:S(2)}) collective-permute-start(bf16[6,256,128]{2,1,0:T(8,128)(2,1)} %collective-permute-done.k_r.refs_3_), channel_id=1, source_target_pairs={{0,8},{8,16},{16,24},{24,0},{32,40},{40,48},{48,56},{56,32},{64,72... | collective-permute-start | bytes 1179656 | tf_op jit(solution)/shard_map/ppermute | solution.py:559
  33.9 17.5 %collective-permute-start.5 = (bf16[6,256,128]{2,1,0:T(8,128)(2,1)}, bf16[6,256,128]{2,1,0:T(8,128)(2,1)S(1)}, u32[]{:S(2)}, u32[]{:S(2)}) collective-permute-start(bf16[6,256,128]{2,1,0:T(8,128)(2,1)} %collective-permute-done.3.v_l.refs_7_), channel_id=1, source_target_pairs={{0,24},{8,0},{16,8},{24,16},{32,56},{40,32},{48,40},{56,48},{64,88... | collective-permute-start | bytes 1179656 | tf_op jit(solution)/shard_map/ppermute | solution.py:559
  44.2 1.0 %copy-start.1 = (bf16[1024,128]{1,0:T(8,128)(2,1)S(1)}, bf16[1024,128]{1,0:T(8,128)(2,1)}, u32[]{:S(2)}) copy-start(bf16[1024,128]{1,0:T(8,128)(2,1)} %copy-done) | copy-start | bytes 786436
  45.2 0.9 %copy-start.3 = (bf16[1024,128]{1,0:T(8,128)(2,1)S(1)}, bf16[1024,128]{1,0:T(8,128)(2,1)}, u32[]{:S(2)}) copy-start(bf16[1024,128]{1,0:T(8,128)(2,1)} %copy-done.2) | copy-start | bytes 786436
  46.1 0.9 %copy-start.5 = (bf16[1024,128]{1,0:T(8,128)(2,1)S(1)}, bf16[1024,128]{1,0:T(8,128)(2,1)}, u32[]{:S(2)}) copy-start(bf16[1024,128]{1,0:T(8,128)(2,1)} %copy-done.4) | copy-start | bytes 786436
  51.4 8.1 %copy-start.7 = (bf16[1024,128]{1,0:T(8,128)(2,1)S(1)}, bf16[1024,128]{1,0:T(8,128)(2,1)}, u32[]{:S(2)}) copy-start(bf16[1024,128]{1,0:T(8,128)(2,1)} %copy-done.6) | copy-start | bytes 786436
  51.5 8.1 %copy-start.10 = (s32[8]{0:T(128)S(1)}, s32[8]{0:T(128)}, u32[]{:S(2)}) copy-start(s32[8]{0:T(128)} %len_ref.1) | copy-start | bytes 100
  52.9 14.3 %collective-permute-start.10 = (bf16[1040,128]{1,0:T(8,128)(2,1)S(1)}, bf16[1040,128]{1,0:T(8,128)(2,1)S(1)}, u32[]{:S(2)}, u32[]{:S(2)}) collective-permute-start(bf16[1040,128]{1,0:T(8,128)(2,1)S(1)} %get-tuple-element.20), channel_id=1, source_target_pairs={{0,96},{8,104},{16,112},{24,120},{32,0},{40,8},{48,16},{56,24},{64... | collective-permute-start | bytes 798728 | tf_op jit(solution)/shard_map/ppermute | solution.py:562
  56.6 12.7 %collective-permute-start.11 = (bf16[1040,128]{1,0:T(8,128)(2,1)S(1)}, bf16[1040,128]{1,0:T(8,128)(2,1)S(1)}, u32[]{:S(2)}, u32[]{:S(2)}) collective-permute-start(bf16[1040,128]{1,0:T(8,128)(2,1)S(1)} %get-tuple-element.21), channel_id=1, source_target_pairs={{0,32},{8,40},{16,48},{24,56},{32,64},{40,72},{48,80},{56,88},{64,... | collective-permute-start | bytes 798728 | tf_op jit(solution)/shard_map/ppermute | solution.py:562
  57.7 11.5 %collective-permute-start.9 = (bf16[1040,128]{1,0:T(8,128)(2,1)S(1)}, bf16[1040,128]{1,0:T(8,128)(2,1)S(1)}, u32[]{:S(2)}, u32[]{:S(2)}) collective-permute-start(bf16[1040,128]{1,0:T(8,128)(2,1)S(1)} %prompt_far.2), channel_id=1, source_target_pairs={{0,64},{8,72},{16,80},{24,88},{32,96},{40,104},{48,112},{56,120},{... | collective-permute-start | bytes 798728 | tf_op jit(solution)/shard_map/ppermute | solution.py:562
  69.5 1.6 %collective-permute-start.12 = (bf16[256,512]{1,0:T(8,128)(2,1)S(1)}, bf16[256,512]{1,0:T(8,128)(2,1)S(1)}, u32[]{:S(2)}, u32[]{:S(2)}) collective-permute-start(bf16[256,512]{1,0:T(8,128)(2,1)S(1)} %merge.1.refs_1_), channel_id=1, source_target_pairs={{0,1},{1,0},{2,3},{3,2},{4,5},{5,4},{6,7},{7,6},{8,9},{9,8},{10,11... | collective-permute-start | bytes 786440 | tf_op jit(solution)/shard_map/ppermute | solution.py:568
  73.6 11.0 %collective-permute-start.15 = (bf16[256,640]{1,0:T(8,128)(2,1)S(1)}, bf16[256,640]{1,0:T(8,128)(2,1)S(1)}, u32[]{:S(2)}, u32[]{:S(2)}) collective-permute-start(bf16[256,640]{1,0:T(8,128)(2,1)S(1)} %get-tuple-element.24), channel_id=1, source_target_pairs={{0,2},{1,3},{2,4},{3,5},{4,6},{5,7},{6,0},{7,1},{8,10},{9,11},{10,... | collective-permute-start | bytes 983048 | tf_op jit(solution)/shard_map/ppermute | solution.py:565
  75.2 5.5 %copy-start.8 = (s32[8,8]{1,0:T(8,128)S(1)}, s32[8,8]{1,0:T(8,128)}, u32[]{:S(2)}) copy-start(s32[8,8]{1,0:T(8,128)} %acc_ref.3) | copy-start | bytes 772
  75.2 15.8 %collective-permute-start.16 = (bf16[256,640]{1,0:T(8,128)(2,1)S(1)}, bf16[256,640]{1,0:T(8,128)(2,1)S(1)}, u32[]{:S(2)}, u32[]{:S(2)}) collective-permute-start(bf16[256,640]{1,0:T(8,128)(2,1)S(1)} %get-tuple-element.25), channel_id=1, source_target_pairs={{0,6},{1,7},{2,0},{3,1},{4,2},{5,3},{6,4},{7,5},{8,14},{9,15},{10,... | collective-permute-start | bytes 983048 | tf_op jit(solution)/shard_map/ppermute | solution.py:565
  78.8 13.9 %collective-permute-start.14 = (bf16[256,640]{1,0:T(8,128)(2,1)S(1)}, bf16[256,640]{1,0:T(8,128)(2,1)S(1)}, u32[]{:S(2)}, u32[]{:S(2)}) collective-permute-start(bf16[256,640]{1,0:T(8,128)(2,1)S(1)} %out_second.1), channel_id=1, source_target_pairs={{0,4},{1,5},{2,6},{3,7},{4,0},{5,1},{6,2},{7,3},{8,12},{9,13},{10,... | collective-permute-start | bytes 983048 | tf_op jit(solution)/shard_map/ppermute | solution.py:565
  (4 other events, 2.8 us)

commit v6 on v5

--- a/solution.py
+++ b/solution.py
@@ -225,9 +225,41 @@
     )(groups, at, k_o, v_o, *qs, *nears)
 
 
+def own_kernel(group_ref, at_ref, q_ref, k, k_r, k_l, v, v_r, v_l, out_hbm, acc_ref, sems):
+    hd = k.shape[2]
+    requests = sems.shape[0]
+    qrows = q_ref.shape[0] // requests
+    pieces = [(k, v), (k_r, v_r), (k_l, v_l)]
+    ones = jnp.ones((k.shape[1], hd), BF16)
+    puts = []
+    for r in range(requests):
+        at = pl.ds(r * qrows, qrows)
+        acc_ref[at, :] = prompt_sum(
+            q_ref[at, :], group_ref[at_ref[0] * requests + r], pieces, ones
+        )
+        put = pltpu.make_async_copy(acc_ref.at[at], out_hbm.at[at], sems.at[r])
+        put.start()
+        puts.append(put)
+    for put in puts:
+        put.wait()
+
+
+def own_call(groups, at, q, prompts, requests):
+    shape = (q.shape[0], 2 * q.shape[1])
+    return pl.pallas_call(
+        own_kernel,
+        in_specs=[SMEM, SMEM] + [VM] * 7,
+        out_specs=HBM,
+        out_shape=pltpu.HBM(shape, F32),
+        scratch_shapes=[pltpu.VMEM(shape, F32), pltpu.SemaphoreType.DMA((requests,))],
+        compiler_params=params(12),
+        name="own_near",
+    )(groups, at, q, *prompts)
+
+
 def home_kernel(
-    group_ref, at_ref, len_ref, q_ref, k, k_r, k_l, v, v_r, v_l, k_o, v_o, new_k, new_v, anc_hbm,
-    ck_hbm, cv_hbm, out_ref, anc_ref, keys, values, where_ref, sems, anc_sem,
+    group_ref, at_ref, len_ref, q_ref, k_o, v_o, new_k, new_v, anc_hbm, own_hbm, ck_hbm, cv_hbm,
+    out_ref, anc_ref, own_ref, keys, values, where_ref, sems, anc_sem, own_sem,
 ):
     requests, slots, hd = keys.shape
     qrows = q_ref.shape[0] // requests
@@ -255,6 +287,8 @@
 
     get_anc = pltpu.make_async_copy(anc_hbm, anc_ref, anc_sem)
     get_anc.start()
+    get_own = pltpu.make_async_copy(own_hbm, own_ref, own_sem)
+    get_own.start()
     tree = anc_ref.shape[1]
     each_copy(lambda c: c.start())
     count = 0
@@ -269,16 +303,17 @@
     for j in range(LANES):
         where_ref[0, count + j] = requests - 1
         where_ref[1, count + j] = 0
-    pieces = [(k, v), (k_r, v_r), (k_l, v_l), (k_o, v_o)]
+    pieces = [(k_o, v_o)]
     ones = jnp.ones((KB, hd), BF16)
     get_anc.wait()
+    get_own.wait()
     for r in range(requests):
         at = pl.ds(r * qrows, qrows)
         mine = pl.ds(r * tree, tree)
         q = q_ref[at, :]
         seen = jnp.concatenate([anc_ref[mine, :]] * (qrows // tree), axis=0)
         p = jnp.where(seen > 0, jnp.exp2(dot_nt(q, new_k[mine, :])), 0.0).astype(BF16)
-        out_ref[at, :] = prompt_sum(
+        out_ref[at, :] = own_ref[at, :] + prompt_sum(
             q, group_ref[at_ref[0] * requests + r], pieces, ones
         ) + dot(p, jnp.concatenate([new_v[mine, :], ones[:tree]], axis=1))
     column = lax.broadcasted_iota(jnp.int32, (qrows, KB), 1)
@@ -303,24 +338,26 @@
     lax.fori_loop(0, (count + LANES - 1) // LANES, step, 0)
 
 
-def home_call(groups, at, lengths, q, prompts, new_k, new_v, ancestors, cache_keys, cache_values):
+def home_call(groups, at, lengths, q, far, new_k, new_v, ancestors, own, cache_keys, cache_values):
     requests, slots, hd = cache_keys.shape
     return pl.pallas_call(
         home_kernel,
-        in_specs=[SMEM, SMEM, SMEM] + [VM] * 11 + [HBM] * 3,
+        in_specs=[SMEM, SMEM, SMEM] + [VM] * 5 + [HBM] * 4,
         out_specs=VM,
         out_shape=jax.ShapeDtypeStruct((q.shape[0], 2 * hd), F32),
         scratch_shapes=[
             pltpu.VMEM(ancestors.shape, jnp.int32),
+            pltpu.VMEM(own.shape, F32),
             pltpu.VMEM(cache_keys.shape, BF16),
             pltpu.VMEM(cache_values.shape, BF16),
             pltpu.SMEM((2, requests * slots // KB + LANES), jnp.int32),
             pltpu.SemaphoreType.DMA((2, requests, PIECES)),
             pltpu.SemaphoreType.DMA,
+            pltpu.SemaphoreType.DMA,
         ],
         compiler_params=params(20),
         name="home_attention",
-    )(groups, at, lengths, q, *prompts, new_k, new_v, ancestors, cache_keys, cache_values)
+    )(groups, at, lengths, q, *far, new_k, new_v, ancestors, own, cache_keys, cache_values)
 
 
 def merge_kernel(home_ref, a_ref, b_ref, c_ref, out_ref, *, requests):
@@ -600,6 +637,8 @@
     v_o = along_y(v_l, -1)
     near = tuple(map(in_hbm, (k, k_r, k_l, v, v_r, v_l)))
 
+    own = own_call(request_group, tok_at, q, near, requests)
+
     turns = [n % n_z * n_y for n in shifts]
     nears = near_call(request_group, tok_at, q_far, near, requests, turns, n_tok)
     parts = []
@@ -610,8 +649,8 @@
         )
     back = [along_z(part, -n) for n, part in zip(shifts, parts)]
     home = home_call(
-        request_group, tok_at, cache_length, q, (k, k_r, k_l, v, v_r, v_l, k_o, v_o), new_k, new_v, in_hbm(table),
-        in_hbm(squeeze(cache_keys)), in_hbm(squeeze(cache_values)),
+        request_group, tok_at, cache_length, q, (k_o, v_o), new_k, new_v, in_hbm(table),
+        in_hbm(own), in_hbm(squeeze(cache_keys)), in_hbm(squeeze(cache_values)),
     )
     attended = merge_call(home, *back, requests, rows)
 

time: 94.2 us -> 94.4 us (level)
  waiting for transfers between devices: 25 us -> 22.9 us
  Pallas kernels: 31.8 us -> 33.9 us
    ppermute x6, waiting for transfers between devices: 5.93 us -> 3.85 us  [along_z(): lax.ppermute(v, 'tok', [(t, (t + n * n_y) % n_tok) for t in range(n_tok)])]
    pallas_call x1 -> x2, Pallas kernels: 7.62 us -> 9.7 us  [the longest x1 6.28 us: home_call(): pl.pallas_call(home_kernel, in_specs=[SMEM, SMEM, SMEM] + [VM] * 5 + [HBM...]
  transfers between devices with their start and end apart: 17 -> 17, of which waited for: 10 -> 9; matrix products, arithmetic and copies ran while one was open for 0% -> 0% of each run, Pallas kernels for 28% -> 31%
where the time goes in v6:
time: 94.4 us; the launch traced here: 93.6 us
  Pallas kernels  33.9 us (36%)
  starting transfers between devices  30.3 us (32%)
  waiting for transfers between devices  22.9 us (24%)
  local copies, waits for them, and re-layouts  5.68 us (6%)
    ppermute x6, starting transfers between devices, along_z(): lax.ppermute(v, 'tok', [(t, (t + n * n_y) % n_tok) for t in range(n_tok)])  13.9 us
    ppermute x6, starting transfers between devices, along_y(): return lax.ppermute(v, 'tok', perm)  11.1 us
    ppermute x3, waiting for transfers between devices, along_x(): lax.ppermute(v, 'mdl', [(m, (m + 2 * n) % n_mdl) for m in range(n_mdl)])  8.83 us
    ppermute x6, waiting for transfers between devices, along_y(): return lax.ppermute(v, 'tok', perm)  8.7 us
    pallas_call x1, Pallas kernels, project_call(): pl.pallas_call(project_kernel, in_specs=[HBM] * 8, out_specs=[VM, VM, VM]...  7 us
    pallas_call x1, Pallas kernels, home_call(): pl.pallas_call(home_kernel, in_specs=[SMEM, SMEM, SMEM] + [VM] * 5 + [HBM...  6.28 us
    unnamed x22, local copies, waits for them, and re-layouts  5.68 us
    ppermute x3, starting transfers between devices, along_x(): lax.ppermute(v, 'mdl', [(m, (m + 2 * n) % n_mdl) for m in range(n_mdl)])  5.21 us
  transfers between devices with their start and end apart: 17, of which 9 were waited for; matrix products, arithmetic and copies ran while one was open for 0% of the time, Pallas kernels for 31%

profile of v6, /device:TPU:0, one launch (start us, length us, event | category | flops | bytes accessed | tf_op | source)
XLA Modules:
  0.0 93.6 jit_solution(381195113909444350)
XLA Ops:
  0.6 1.7 %out_columns.1 = bf16[4,512,640]{2,1,0:T(8,128)(2,1)S(1)} custom-call(s32[1]{0:T(128)} %bitcast.mdl_ref.refs_0_, bf16[512,5120]{1,0:T(8,128)(2,1)} %refs_3_.3), custom_call_target="tpu_custom_call" | custom-call | tf_op jit(solution)/shard_map/out_columns/pallas_call | solution.py:461
  2.5 7.0 %projections.1 = (bf16[1024,128]{1,0:T(8,128)(2,1)S(1)}, bf16[256,128]{1,0:T(8,128)(2,1)S(1)}, bf16[256,128]{1,0:T(8,128)(2,1)S(1)}) custom-call(s32[8]{0:T(128)} %len_ref.1, bf16[256,5120]{1,0:T(8,128)(2,1)} %tok_hbm.3, bf16[40,128]{1,0:T(8,128)(2,1)} %bitcast.12, bf16[5120,512]{1,0:T(8,128)(2,1)} %wq_hbm.1, bf16[5120,128]{1,0:T(8,128)(2,1)} %wk_hbm.1, ...), custom_call_target="tpu_custom_call" | custom-call | tf_op jit(solution)/shard_map/projections/pallas_call | solution.py:130
  9.5 4.1 %collective-permute-start.6 = (bf16[1024,128]{1,0:T(8,128)(2,1)S(1)}, bf16[1024,128]{1,0:T(8,128)(2,1)S(1)}, u32[]{:S(2)}, u32[]{:S(2)}) collective-permute-start(bf16[1024,128]{1,0:T(8,128)(2,1)S(1)} %get-tuple-element.14.q_ref), channel_id=1, source_target_pairs={{0,64},{8,72},{16,80},{24,88},{32,96},{40,104},{48,112},{56,120},{... | collective-permute-start | bytes 786440 | tf_op jit(solution)/shard_map/ppermute | solution.py:599
  13.6 1.6 %collective-permute-start = (bf16[6,256,128]{2,1,0:T(8,128)(2,1)}, bf16[6,256,128]{2,1,0:T(8,128)(2,1)}, u32[]{:S(2)}, u32[]{:S(2)}) collective-permute-start(bf16[6,256,128]{2,1,0:T(8,128)(2,1)} %bitcast.4.k.refs_2_), channel_id=1, source_target_pairs={{0,8},{8,16},{16,24},{24,0},{32,40},{40,48},{48,56},{56,32},{64,72... | collective-permute-start | bytes 1179656 | tf_op jit(solution)/shard_map/ppermute | solution.py:596
  15.1 1.7 %collective-permute-start.2 = (bf16[6,256,128]{2,1,0:T(8,128)(2,1)}, bf16[6,256,128]{2,1,0:T(8,128)(2,1)}, u32[]{:S(2)}, u32[]{:S(2)}) collective-permute-start(bf16[6,256,128]{2,1,0:T(8,128)(2,1)} %bitcast.5.v.refs_5_), channel_id=1, source_target_pairs={{0,24},{8,0},{16,8},{24,16},{32,56},{40,32},{48,40},{56,48},{64,88... | collective-permute-start | bytes 1179656 | tf_op jit(solution)/shard_map/ppermute | solution.py:596
  17.8 2.9 %collective-permute-done.6.refs_8_.refs_4_ = bf16[1024,128]{1,0:T(8,128)(2,1)S(1)} collective-permute-done((bf16[1024,128]{1,0:T(8,128)(2,1)S(1)}, bf16[1024,128]{1,0:T(8,128)(2,1)S(1)}, u32[]{:S(2)}, u32[]{:S(2)}) %collective-permute-start.6) | collective-permute-done | bytes 262176 | tf_op jit(solution)/shard_map/ppermute | solution.py:599
  21.4 3.2 %collective-permute-start.8 = (bf16[1024,128]{1,0:T(8,128)(2,1)S(1)}, bf16[1024,128]{1,0:T(8,128)(2,1)S(1)}, u32[]{:S(2)}, u32[]{:S(2)}) collective-permute-start(bf16[1024,128]{1,0:T(8,128)(2,1)S(1)} %get-tuple-element.14.q_ref), channel_id=1, source_target_pairs={{0,96},{8,104},{16,112},{24,120},{32,0},{40,8},{48,16},{56,24},{64... | collective-permute-start | bytes 786440 | tf_op jit(solution)/shard_map/ppermute | solution.py:599
  26.9 3.0 %collective-permute-start.4 = (bf16[6,256,128]{2,1,0:T(8,128)(2,1)}, bf16[6,256,128]{2,1,0:T(8,128)(2,1)}, u32[]{:S(2)}, u32[]{:S(2)}) collective-permute-start(bf16[6,256,128]{2,1,0:T(8,128)(2,1)} %bitcast.4.k.refs_2_), channel_id=1, source_target_pairs={{0,24},{8,0},{16,8},{24,16},{32,56},{40,32},{48,40},{56,48},{64,88... | collective-permute-start | bytes 1179656 | tf_op jit(solution)/shard_map/ppermute | solution.py:596
  30.7 1.6 %collective-permute-start.5 = (bf16[6,256,128]{2,1,0:T(8,128)(2,1)}, bf16[6,256,128]{2,1,0:T(8,128)(2,1)}, u32[]{:S(2)}, u32[]{:S(2)}) collective-permute-start(bf16[6,256,128]{2,1,0:T(8,128)(2,1)} %bitcast.5.v.refs_5_), channel_id=1, source_target_pairs={{0,8},{8,16},{16,24},{24,0},{32,40},{40,48},{48,56},{56,32},{64,72... | collective-permute-start | bytes 1179656 | tf_op jit(solution)/shard_map/ppermute | solution.py:596
  32.3 1.6 %collective-permute-start.1 = (bf16[6,256,128]{2,1,0:T(8,128)(2,1)}, bf16[6,256,128]{2,1,0:T(8,128)(2,1)S(1)}, u32[]{:S(2)}, u32[]{:S(2)}) collective-permute-start(bf16[6,256,128]{2,1,0:T(8,128)(2,1)} %collective-permute-done.k_r.refs_3_), channel_id=1, source_target_pairs={{0,8},{8,16},{16,24},{24,0},{32,40},{40,48},{48,56},{56,32},{64,72... | collective-permute-start | bytes 1179656 | tf_op jit(solution)/shard_map/ppermute | solution.py:596
  33.9 1.7 %collective-permute-start.3 = (bf16[6,256,128]{2,1,0:T(8,128)(2,1)}, bf16[6,256,128]{2,1,0:T(8,128)(2,1)S(1)}, u32[]{:S(2)}, u32[]{:S(2)}) collective-permute-start(bf16[6,256,128]{2,1,0:T(8,128)(2,1)} %collective-permute-done.2.v_l.refs_7_), channel_id=1, source_target_pairs={{0,24},{8,0},{16,8},{24,16},{32,56},{40,32},{48,40},{56,48},{64,88... | collective-permute-start | bytes 1179656 | tf_op jit(solution)/shard_map/ppermute | solution.py:596
  35.5 4.2 %collective-permute-done.4.k_l.refs_4_ = bf16[6,256,128]{2,1,0:T(8,128)(2,1)} collective-permute-done((bf16[6,256,128]{2,1,0:T(8,128)(2,1)}, bf16[6,256,128]{2,1,0:T(8,128)(2,1)}, u32[]{:S(2)}, u32[]{:S(2)}) %collective-permute-start.4) | collective-permute-done | bytes 393248 | tf_op jit(solution)/shard_map/ppermute | solution.py:596
  39.7 4.5 %collective-permute-done.5.v_r.refs_6_ = bf16[6,256,128]{2,1,0:T(8,128)(2,1)} collective-permute-done((bf16[6,256,128]{2,1,0:T(8,128)(2,1)}, bf16[6,256,128]{2,1,0:T(8,128)(2,1)}, u32[]{:S(2)}, u32[]{:S(2)}) %collective-permute-start.5) | collective-permute-done | bytes 393248 | tf_op jit(solution)/shard_map/ppermute | solution.py:596
  47.1 4.3 %prompt_near.1 = (f32[1024,256]{1,0:T(8,128)S(1)}, f32[1024,256]{1,0:T(8,128)S(1)}, f32[1024,256]{1,0:T(8,128)S(1)}) custom-call(s32[128]{0:T(128)S(1)} %copy-done.9, s32[1]{0:T(128)} %bitcast.1.at_ref.refs_1_, bf16[6,256,128]{2,1,0:T(8,128)(2,1)} %bitcast.4.k.refs_2_, bf16[6,256,128]{2,1,0:T(8,128)(2,1)} %collective-permute-done.k_r.refs_3_, ...), custom_call_target="tpu_custom_call" | custom-call | tf_op jit(solution)/shard_map/prompt_near/pallas_call | solution.py:181
  52.8 3.8 %collective-permute-start.10 = (bf16[1040,128]{1,0:T(8,128)(2,1)S(1)}, bf16[1040,128]{1,0:T(8,128)(2,1)S(1)}, u32[]{:S(2)}, u32[]{:S(2)}) collective-permute-start(bf16[1040,128]{1,0:T(8,128)(2,1)S(1)} %get-tuple-element.20), channel_id=1, source_target_pairs={{0,96},{8,104},{16,112},{24,120},{32,0},{40,8},{48,16},{56,24},{64... | collective-permute-start | bytes 798728 | tf_op jit(solution)/shard_map/ppermute | solution.py:599
  57.7 1.8 %collective-permute-start.9 = (bf16[1040,128]{1,0:T(8,128)(2,1)S(1)}, bf16[1040,128]{1,0:T(8,128)(2,1)S(1)}, u32[]{:S(2)}, u32[]{:S(2)}) collective-permute-start(bf16[1040,128]{1,0:T(8,128)(2,1)S(1)} %prompt_far.2), channel_id=1, source_target_pairs={{0,64},{8,72},{16,80},{24,88},{32,96},{40,104},{48,112},{56,120},{... | collective-permute-start | bytes 798728 | tf_op jit(solution)/shard_map/ppermute | solution.py:599
  59.5 3.4 %own_near.1.own_hbm = f32[1024,256]{1,0:T(8,128)} custom-call(s32[128]{0:T(128)S(1)} %copy-done.9, s32[1]{0:T(128)} %bitcast.1.at_ref.refs_1_, bf16[1024,128]{1,0:T(8,128)(2,1)S(1)} %copy-done.7, bf16[6,256,128]{2,1,0:T(8,128)(2,1)} %bitcast.4.k.refs_2_, bf16[6,256,128]{2,1,0:T(8,128)(2,1)} %collective-permute-done.k_r.refs_3_, ...), custom_call_target="tpu_custom_call" | custom-call | tf_op jit(solution)/shard_map/own_near/pallas_call | solution.py:249
  63.0 6.3 %home_attention.1.refs_0_ = f32[1024,256]{1,0:T(8,128)S(1)} custom-call(s32[128]{0:T(128)S(1)} %copy-done.9, s32[1]{0:T(128)} %bitcast.1.at_ref.refs_1_, s32[8]{0:T(128)S(1)} %copy-done.10, bf16[1024,128]{1,0:T(8,128)(2,1)S(1)} %copy-done.7, bf16[6,256,128]{2,1,0:T(8,128)(2,1)S(1)} %collective-permute-done.1.k_o.refs_2_, ...), custom_call_target="tpu_custom_call" | custom-call | tf_op jit(solution)/shard_map/home_attention/pallas_call | solution.py:343
  71.2 2.5 %out_proj.3 = (bf16[256,640]{1,0:T(8,128)(2,1)S(1)}, bf16[256,640]{1,0:T(8,128)(2,1)S(1)}) custom-call(s32[1]{0:T(128)} %bitcast.mdl_ref.refs_0_, bf16[256,512]{1,0:T(8,128)(2,1)S(1)} %merge.1.refs_1_, bf16[256,512]{1,0:T(8,128)(2,1)S(1)} %collective-permute-done.12.refs_2_.other_ref, bf16[512,5120]{1,0:T(8,128)(2,1)} %refs_3_.3, ...), custom_call_target="tpu_custom_call" | custom-call | tf_op jit(solution)/shard_map/out_proj/pallas_call | solution.py:541
  73.6 1.6 %collective-permute-start.15 = (bf16[256,640]{1,0:T(8,128)(2,1)S(1)}, bf16[256,640]{1,0:T(8,128)(2,1)S(1)}, u32[]{:S(2)}, u32[]{:S(2)}) collective-permute-start(bf16[256,640]{1,0:T(8,128)(2,1)S(1)} %get-tuple-element.24), channel_id=1, source_target_pairs={{0,2},{1,3},{2,4},{3,5},{4,6},{5,7},{6,0},{7,1},{8,10},{9,11},{10,... | collective-permute-start | bytes 983048 | tf_op jit(solution)/shard_map/ppermute | solution.py:602
  75.2 1.7 %collective-permute-start.16 = (bf16[256,640]{1,0:T(8,128)(2,1)S(1)}, bf16[256,640]{1,0:T(8,128)(2,1)S(1)}, u32[]{:S(2)}, u32[]{:S(2)}) collective-permute-start(bf16[256,640]{1,0:T(8,128)(2,1)S(1)} %get-tuple-element.25), channel_id=1, source_target_pairs={{0,6},{1,7},{2,0},{3,1},{4,2},{5,3},{6,4},{7,5},{8,14},{9,15},{10,... | collective-permute-start | bytes 983048 | tf_op jit(solution)/shard_map/ppermute | solution.py:602
  78.8 1.9 %collective-permute-start.14 = (bf16[256,640]{1,0:T(8,128)(2,1)S(1)}, bf16[256,640]{1,0:T(8,128)(2,1)S(1)}, u32[]{:S(2)}, u32[]{:S(2)}) collective-permute-start(bf16[256,640]{1,0:T(8,128)(2,1)S(1)} %out_second.1), channel_id=1, source_target_pairs={{0,4},{1,5},{2,6},{3,7},{4,0},{5,1},{6,2},{7,3},{8,12},{9,13},{10,... | collective-permute-start | bytes 983048 | tf_op jit(solution)/shard_map/ppermute | solution.py:602
  81.9 1.9 %out_proj.2.own_ref = f32[256,640]{1,0:T(8,128)S(1)} custom-call(s32[1]{0:T(128)} %bitcast.mdl_ref.refs_0_, bf16[256,512]{1,0:T(8,128)(2,1)S(1)} %merge.1.refs_1_, bf16[256,512]{1,0:T(8,128)(2,1)S(1)} %collective-permute-done.12.refs_2_.other_ref, bf16[512,5120]{1,0:T(8,128)(2,1)} %refs_3_.3, bf16[4,512,640]{2,1,0:T(8,128)(2,1)} %collective-permute-done.13.refs_4_.refs_3_), custom_call_target="tpu_custom_call" | custom-call | tf_op jit(solution)/shard_map/out_proj/pallas_call | solution.py:541
  85.8 6.9 %collective-permute-done.14.a_ref = bf16[256,640]{1,0:T(8,128)(2,1)S(1)} collective-permute-done((bf16[256,640]{1,0:T(8,128)(2,1)S(1)}, bf16[256,640]{1,0:T(8,128)(2,1)S(1)}, u32[]{:S(2)}, u32[]{:S(2)}) %collective-permute-start.14) | collective-permute-done | bytes 327712 | tf_op jit(solution)/shard_map/ppermute | solution.py:602
  (46 shorter events, 18.1 us)
Async XLA Ops:
  2.4 68.8 %collective-permute-start.13 = (bf16[4,512,640]{2,1,0:T(8,128)(2,1)S(1)}, bf16[4,512,640]{2,1,0:T(8,128)(2,1)}, u32[]{:S(2)}, u32[]{:S(2)}) collective-permute-start(bf16[4,512,640]{2,1,0:T(8,128)(2,1)S(1)} %out_columns.1), channel_id=1, source_target_pairs={{0,1},{1,0},{2,3},{3,2},{4,5},{5,4},{6,7},{7,6},{8,9},{9,8},{10,11... | collective-permute-start | bytes 7864328 | tf_op jit(solution)/shard_map/ppermute | solution.py:605
  2.5 41.7 %copy-start.9 = (s32[128]{0:T(128)S(1)}, s32[128]{0:T(128)}, u32[]{:S(2)}) copy-start(s32[128]{0:T(128)} %refs_0_.5) | copy-start | bytes 1540
  9.5 11.2 %collective-permute-start.6 = (bf16[1024,128]{1,0:T(8,128)(2,1)S(1)}, bf16[1024,128]{1,0:T(8,128)(2,1)S(1)}, u32[]{:S(2)}, u32[]{:S(2)}) collective-permute-start(bf16[1024,128]{1,0:T(8,128)(2,1)S(1)} %get-tuple-element.14.q_ref), channel_id=1, source_target_pairs={{0,64},{8,72},{16,80},{24,88},{32,96},{40,104},{48,112},{56,120},{... | collective-permute-start | bytes 786440 | tf_op jit(solution)/shard_map/ppermute | solution.py:599
  13.6 18.7 %collective-permute-start = (bf16[6,256,128]{2,1,0:T(8,128)(2,1)}, bf16[6,256,128]{2,1,0:T(8,128)(2,1)}, u32[]{:S(2)}, u32[]{:S(2)}) collective-permute-start(bf16[6,256,128]{2,1,0:T(8,128)(2,1)} %bitcast.4.k.refs_2_), channel_id=1, source_target_pairs={{0,8},{8,16},{16,24},{24,0},{32,40},{40,48},{48,56},{56,32},{64,72... | collective-permute-start | bytes 1179656 | tf_op jit(solution)/shard_map/ppermute | solution.py:596
  15.1 18.7 %collective-permute-start.2 = (bf16[6,256,128]{2,1,0:T(8,128)(2,1)}, bf16[6,256,128]{2,1,0:T(8,128)(2,1)}, u32[]{:S(2)}, u32[]{:S(2)}) collective-permute-start(bf16[6,256,128]{2,1,0:T(8,128)(2,1)} %bitcast.5.v.refs_5_), channel_id=1, source_target_pairs={{0,24},{8,0},{16,8},{24,16},{32,56},{40,32},{48,40},{56,48},{64,88... | collective-permute-start | bytes 1179656 | tf_op jit(solution)/shard_map/ppermute | solution.py:596
  16.8 9.3 %collective-permute-start.7 = (bf16[1024,128]{1,0:T(8,128)(2,1)S(1)}, bf16[1024,128]{1,0:T(8,128)(2,1)S(1)}, u32[]{:S(2)}, u32[]{:S(2)}) collective-permute-start(bf16[1024,128]{1,0:T(8,128)(2,1)S(1)} %get-tuple-element.14.q_ref), channel_id=1, source_target_pairs={{0,32},{8,40},{16,48},{24,56},{32,64},{40,72},{48,80},{56,88},{64,... | collective-permute-start | bytes 786440 | tf_op jit(solution)/shard_map/ppermute | solution.py:599
  21.4 8.6 %collective-permute-start.8 = (bf16[1024,128]{1,0:T(8,128)(2,1)S(1)}, bf16[1024,128]{1,0:T(8,128)(2,1)S(1)}, u32[]{:S(2)}, u32[]{:S(2)}) collective-permute-start(bf16[1024,128]{1,0:T(8,128)(2,1)S(1)} %get-tuple-element.14.q_ref), channel_id=1, source_target_pairs={{0,96},{8,104},{16,112},{24,120},{32,0},{40,8},{48,16},{56,24},{64... | collective-permute-start | bytes 786440 | tf_op jit(solution)/shard_map/ppermute | solution.py:599
  26.9 12.8 %collective-permute-start.4 = (bf16[6,256,128]{2,1,0:T(8,128)(2,1)}, bf16[6,256,128]{2,1,0:T(8,128)(2,1)}, u32[]{:S(2)}, u32[]{:S(2)}) collective-permute-start(bf16[6,256,128]{2,1,0:T(8,128)(2,1)} %bitcast.4.k.refs_2_), channel_id=1, source_target_pairs={{0,24},{8,0},{16,8},{24,16},{32,56},{40,32},{48,40},{56,48},{64,88... | collective-permute-start | bytes 1179656 | tf_op jit(solution)/shard_map/ppermute | solution.py:596
  30.7 13.5 %collective-permute-start.5 = (bf16[6,256,128]{2,1,0:T(8,128)(2,1)}, bf16[6,256,128]{2,1,0:T(8,128)(2,1)}, u32[]{:S(2)}, u32[]{:S(2)}) collective-permute-start(bf16[6,256,128]{2,1,0:T(8,128)(2,1)} %bitcast.5.v.refs_5_), channel_id=1, source_target_pairs={{0,8},{8,16},{16,24},{24,0},{32,40},{40,48},{48,56},{56,32},{64,72... | collective-permute-start | bytes 1179656 | tf_op jit(solution)/shard_map/ppermute | solution.py:596
  32.3 19.1 %collective-permute-start.1 = (bf16[6,256,128]{2,1,0:T(8,128)(2,1)}, bf16[6,256,128]{2,1,0:T(8,128)(2,1)S(1)}, u32[]{:S(2)}, u32[]{:S(2)}) collective-permute-start(bf16[6,256,128]{2,1,0:T(8,128)(2,1)} %collective-permute-done.k_r.refs_3_), channel_id=1, source_target_pairs={{0,8},{8,16},{16,24},{24,0},{32,40},{40,48},{48,56},{56,32},{64,72... | collective-permute-start | bytes 1179656 | tf_op jit(solution)/shard_map/ppermute | solution.py:596
  33.9 17.5 %collective-permute-start.3 = (bf16[6,256,128]{2,1,0:T(8,128)(2,1)}, bf16[6,256,128]{2,1,0:T(8,128)(2,1)S(1)}, u32[]{:S(2)}, u32[]{:S(2)}) collective-permute-start(bf16[6,256,128]{2,1,0:T(8,128)(2,1)} %collective-permute-done.2.v_l.refs_7_), channel_id=1, source_target_pairs={{0,24},{8,0},{16,8},{24,16},{32,56},{40,32},{48,40},{56,48},{64,88... | collective-permute-start | bytes 1179656 | tf_op jit(solution)/shard_map/ppermute | solution.py:596
  44.2 1.0 %copy-start.1 = (bf16[1024,128]{1,0:T(8,128)(2,1)S(1)}, bf16[1024,128]{1,0:T(8,128)(2,1)}, u32[]{:S(2)}) copy-start(bf16[1024,128]{1,0:T(8,128)(2,1)} %copy-done) | copy-start | bytes 786436
  45.2 0.9 %copy-start.3 = (bf16[1024,128]{1,0:T(8,128)(2,1)S(1)}, bf16[1024,128]{1,0:T(8,128)(2,1)}, u32[]{:S(2)}) copy-start(bf16[1024,128]{1,0:T(8,128)(2,1)} %copy-done.2) | copy-start | bytes 786436
  46.1 0.9 %copy-start.5 = (bf16[1024,128]{1,0:T(8,128)(2,1)S(1)}, bf16[1024,128]{1,0:T(8,128)(2,1)}, u32[]{:S(2)}) copy-start(bf16[1024,128]{1,0:T(8,128)(2,1)} %copy-done.4) | copy-start | bytes 786436
  51.4 8.1 %copy-start.7 = (bf16[1024,128]{1,0:T(8,128)(2,1)S(1)}, bf16[1024,128]{1,0:T(8,128)(2,1)}, u32[]{:S(2)}) copy-start(bf16[1024,128]{1,0:T(8,128)(2,1)} %copy-done.6) | copy-start | bytes 786436
  52.8 16.4 %collective-permute-start.10 = (bf16[1040,128]{1,0:T(8,128)(2,1)S(1)}, bf16[1040,128]{1,0:T(8,128)(2,1)S(1)}, u32[]{:S(2)}, u32[]{:S(2)}) collective-permute-start(bf16[1040,128]{1,0:T(8,128)(2,1)S(1)} %get-tuple-element.20), channel_id=1, source_target_pairs={{0,96},{8,104},{16,112},{24,120},{32,0},{40,8},{48,16},{56,24},{64... | collective-permute-start | bytes 798728 | tf_op jit(solution)/shard_map/ppermute | solution.py:599
  56.6 12.7 %collective-permute-start.11 = (bf16[1040,128]{1,0:T(8,128)(2,1)S(1)}, bf16[1040,128]{1,0:T(8,128)(2,1)S(1)}, u32[]{:S(2)}, u32[]{:S(2)}) collective-permute-start(bf16[1040,128]{1,0:T(8,128)(2,1)S(1)} %get-tuple-element.21), channel_id=1, source_target_pairs={{0,32},{8,40},{16,48},{24,56},{32,64},{40,72},{48,80},{56,88},{64,... | collective-permute-start | bytes 798728 | tf_op jit(solution)/shard_map/ppermute | solution.py:599
  56.6 6.3 %copy-start.10 = (s32[8]{0:T(128)S(1)}, s32[8]{0:T(128)}, u32[]{:S(2)}) copy-start(s32[8]{0:T(128)} %len_ref.1) | copy-start | bytes 100
  57.7 11.6 %collective-permute-start.9 = (bf16[1040,128]{1,0:T(8,128)(2,1)S(1)}, bf16[1040,128]{1,0:T(8,128)(2,1)S(1)}, u32[]{:S(2)}, u32[]{:S(2)}) collective-permute-start(bf16[1040,128]{1,0:T(8,128)(2,1)S(1)} %prompt_far.2), channel_id=1, source_target_pairs={{0,64},{8,72},{16,80},{24,88},{32,96},{40,104},{48,112},{56,120},{... | collective-permute-start | bytes 798728 | tf_op jit(solution)/shard_map/ppermute | solution.py:599
  69.5 1.6 %collective-permute-start.12 = (bf16[256,512]{1,0:T(8,128)(2,1)S(1)}, bf16[256,512]{1,0:T(8,128)(2,1)S(1)}, u32[]{:S(2)}, u32[]{:S(2)}) collective-permute-start(bf16[256,512]{1,0:T(8,128)(2,1)S(1)} %merge.1.refs_1_), channel_id=1, source_target_pairs={{0,1},{1,0},{2,3},{3,2},{4,5},{5,4},{6,7},{7,6},{8,9},{9,8},{10,11... | collective-permute-start | bytes 786440 | tf_op jit(solution)/shard_map/ppermute | solution.py:605
  73.6 11.0 %collective-permute-start.15 = (bf16[256,640]{1,0:T(8,128)(2,1)S(1)}, bf16[256,640]{1,0:T(8,128)(2,1)S(1)}, u32[]{:S(2)}, u32[]{:S(2)}) collective-permute-start(bf16[256,640]{1,0:T(8,128)(2,1)S(1)} %get-tuple-element.24), channel_id=1, source_target_pairs={{0,2},{1,3},{2,4},{3,5},{4,6},{5,7},{6,0},{7,1},{8,10},{9,11},{10,... | collective-permute-start | bytes 983048 | tf_op jit(solution)/shard_map/ppermute | solution.py:602
  75.2 5.5 %copy-start.8 = (s32[8,8]{1,0:T(8,128)S(1)}, s32[8,8]{1,0:T(8,128)}, u32[]{:S(2)}) copy-start(s32[8,8]{1,0:T(8,128)} %acc_ref.3) | copy-start | bytes 772
  75.2 10.6 %collective-permute-start.16 = (bf16[256,640]{1,0:T(8,128)(2,1)S(1)}, bf16[256,640]{1,0:T(8,128)(2,1)S(1)}, u32[]{:S(2)}, u32[]{:S(2)}) collective-permute-start(bf16[256,640]{1,0:T(8,128)(2,1)S(1)} %get-tuple-element.25), channel_id=1, source_target_pairs={{0,6},{1,7},{2,0},{3,1},{4,2},{5,3},{6,4},{7,5},{8,14},{9,15},{10,... | collective-permute-start | bytes 983048 | tf_op jit(solution)/shard_map/ppermute | solution.py:602
  78.8 13.9 %collective-permute-start.14 = (bf16[256,640]{1,0:T(8,128)(2,1)S(1)}, bf16[256,640]{1,0:T(8,128)(2,1)S(1)}, u32[]{:S(2)}, u32[]{:S(2)}) collective-permute-start(bf16[256,640]{1,0:T(8,128)(2,1)S(1)} %out_second.1), channel_id=1, source_target_pairs={{0,4},{1,5},{2,6},{3,7},{4,0},{5,1},{6,2},{7,3},{8,12},{9,13},{10,... | collective-permute-start | bytes 983048 | tf_op jit(solution)/shard_map/ppermute | solution.py:602
  (4 other events, 2.8 us)

commit v7 on v5

--- a/solution.py
+++ b/solution.py
@@ -601,8 +601,9 @@
     near = tuple(map(in_hbm, (k, k_r, k_l, v, v_r, v_l)))
 
     turns = [n % n_z * n_y for n in shifts]
-    nears = near_call(request_group, tok_at, q_far, near, requests, turns, n_tok)
-    parts = []
+    nears, parts = [], []
+    for some in (slice(0, 1), slice(1, 3)):
+        nears += near_call(request_group, tok_at, q_far[some], near, requests, turns[some], n_tok)
     for some in (slice(0, 1), slice(1, 3)):
         parts += far_call(
             request_group, tok_at, nears[some], q_far[some], k_o, v_o, requests, turns[some],

time: 94.2 us -> 90.4 us (0.960)
  local copies, waits for them, and re-layouts: 5.71 us -> 0.07 us
  Pallas kernels: 31.8 us -> 35.1 us
  starting transfers between devices: 30.3 us -> 27.6 us
  waiting for transfers between devices: 25 us -> 26.2 us
    unnamed x22 -> x30, local copies, waits for them, and re-layouts: 5.71 us -> 0.07 us
    pallas_call x1 -> x2, Pallas kernels: 4.33 us -> 6.21 us  [near_call(): pl.pallas_call(lambda *refs: near_kernel(*refs, requests=requests, shifts...]
    pallas_call x1, Pallas kernels: 1.74 us -> 3.22 us  [columns_call(): pl.pallas_call(columns_kernel, in_specs=[SMEM, HBM], out_specs=VM, out_sh...]
    ppermute x6, starting transfers between devices: 13.9 us -> 12.4 us  [along_z(): lax.ppermute(v, 'tok', [(t, (t + n * n_y) % n_tok) for t in range(n_tok)])]
    ppermute x6, waiting for transfers between devices: 8.7 us -> 10 us  [along_y(): return lax.ppermute(v, 'tok', perm)]
    ppermute x6, starting transfers between devices: 11.1 us -> 9.86 us  [along_y(): return lax.ppermute(v, 'tok', perm)]
  transfers between devices with their start and end apart: 17 -> 17, of which waited for: 10 -> 9; matrix products, arithmetic and copies ran while one was open for 0% -> 0% of each run, Pallas kernels for 28% -> 32%
where the time goes in v7:
time: 90.4 us; the launch traced here: 89.8 us
  Pallas kernels  35.1 us (39%)
  starting transfers between devices  27.6 us (31%)
  waiting for transfers between devices  26.2 us (29%)
    ppermute x6, starting transfers between devices, along_z(): lax.ppermute(v, 'tok', [(t, (t + n * n_y) % n_tok) for t in range(n_tok)])  12.4 us
    ppermute x6, waiting for transfers between devices, along_y(): return lax.ppermute(v, 'tok', perm)  10 us
    ppermute x6, starting transfers between devices, along_y(): return lax.ppermute(v, 'tok', perm)  9.86 us
    ppermute x3, waiting for transfers between devices, along_x(): lax.ppermute(v, 'mdl', [(m, (m + 2 * n) % n_mdl) for m in range(n_mdl)])  8.85 us
    pallas_call x1, Pallas kernels, project_call(): pl.pallas_call(project_kernel, in_specs=[HBM] * 8, out_specs=[VM, VM, VM]...  7.49 us
    pallas_call x1, Pallas kernels, home_call(): pl.pallas_call(home_kernel, in_specs=[SMEM, SMEM, SMEM] + [VM] * 11 + [HB...  6.99 us
    pallas_call x2, Pallas kernels, near_call(): pl.pallas_call(lambda *refs: near_kernel(*refs, requests=requests, shifts...  6.21 us
    ppermute x6, waiting for transfers between devices, along_z(): lax.ppermute(v, 'tok', [(t, (t + n * n_y) % n_tok) for t in range(n_tok)])  5.76 us
  transfers between devices with their start and end apart: 17, of which 9 were waited for; matrix products, arithmetic and copies ran while one was open for 0% of the time, Pallas kernels for 32%

profile of v7, /device:TPU:0, one launch (start us, length us, event | category | flops | bytes accessed | tf_op | source)
XLA Modules:
  0.0 89.8 jit_solution(13999737543875968112)
XLA Ops:
  0.6 3.2 %out_columns.1 = bf16[4,512,640]{2,1,0:T(8,128)(2,1)} custom-call(s32[1]{0:T(128)} %bitcast.mdl_ref.refs_0_, bf16[512,5120]{1,0:T(8,128)(2,1)} %refs_3_.3), custom_call_target="tpu_custom_call" | custom-call | tf_op jit(solution)/shard_map/out_columns/pallas_call | solution.py:424
  4.0 7.5 %projections.1 = (bf16[1024,128]{1,0:T(8,128)(2,1)}, bf16[256,128]{1,0:T(8,128)(2,1)S(1)}, bf16[256,128]{1,0:T(8,128)(2,1)S(1)}) custom-call(s32[8]{0:T(128)} %len_ref.1, bf16[256,5120]{1,0:T(8,128)(2,1)} %tok_hbm.3, bf16[40,128]{1,0:T(8,128)(2,1)} %bitcast.22, bf16[5120,512]{1,0:T(8,128)(2,1)} %wq_hbm.1, bf16[5120,128]{1,0:T(8,128)(2,1)} %wk_hbm.1, ...), custom_call_target="tpu_custom_call" | custom-call | tf_op jit(solution)/shard_map/projections/pallas_call | solution.py:130
  11.5 4.1 %collective-permute-start.6 = (bf16[1024,128]{1,0:T(8,128)(2,1)}, bf16[1024,128]{1,0:T(8,128)(2,1)S(1)}, u32[]{:S(2)}, u32[]{:S(2)}) collective-permute-start(bf16[1024,128]{1,0:T(8,128)(2,1)} %get-tuple-element.13.q_ref), channel_id=1, source_target_pairs={{0,64},{8,72},{16,80},{24,88},{32,96},{40,104},{48,112},{56,120},{... | collective-permute-start | bytes 786440 | tf_op jit(solution)/shard_map/ppermute | solution.py:562
  15.6 1.6 %collective-permute-start = (bf16[6,256,128]{2,1,0:T(8,128)(2,1)S(1)}, bf16[6,256,128]{2,1,0:T(8,128)(2,1)S(1)}, u32[]{:S(2)}, u32[]{:S(2)}) collective-permute-start(bf16[6,256,128]{2,1,0:T(8,128)(2,1)S(1)} %bitcast.10), channel_id=1, source_target_pairs={{0,8},{8,16},{16,24},{24,0},{32,40},{40,48},{48,56},{56,32},{64,72... | collective-permute-start | bytes 1179656 | tf_op jit(solution)/shard_map/ppermute | solution.py:559
  17.1 1.7 %collective-permute-start.3 = (bf16[6,256,128]{2,1,0:T(8,128)(2,1)S(1)}, bf16[6,256,128]{2,1,0:T(8,128)(2,1)S(1)}, u32[]{:S(2)}, u32[]{:S(2)}) collective-permute-start(bf16[6,256,128]{2,1,0:T(8,128)(2,1)S(1)} %bitcast.15), channel_id=1, source_target_pairs={{0,24},{8,0},{16,8},{24,16},{32,56},{40,32},{48,40},{56,48},{64,88... | collective-permute-start | bytes 1179656 | tf_op jit(solution)/shard_map/ppermute | solution.py:559
  18.8 1.8 %collective-permute-start.1 = (bf16[6,256,128]{2,1,0:T(8,128)(2,1)S(1)}, bf16[6,256,128]{2,1,0:T(8,128)(2,1)S(1)}, u32[]{:S(2)}, u32[]{:S(2)}) collective-permute-start(bf16[6,256,128]{2,1,0:T(8,128)(2,1)S(1)} %bitcast.11), channel_id=1, source_target_pairs={{0,24},{8,0},{16,8},{24,16},{32,56},{40,32},{48,40},{56,48},{64,88... | collective-permute-start | bytes 1179656 | tf_op jit(solution)/shard_map/ppermute | solution.py:559
  20.6 2.1 %collective-permute-done.6.refs_8_.refs_4_ = bf16[1024,128]{1,0:T(8,128)(2,1)S(1)} collective-permute-done((bf16[1024,128]{1,0:T(8,128)(2,1)}, bf16[1024,128]{1,0:T(8,128)(2,1)S(1)}, u32[]{:S(2)}, u32[]{:S(2)}) %collective-permute-start.6) | collective-permute-done | bytes 262176 | tf_op jit(solution)/shard_map/ppermute | solution.py:562
  24.3 4.5 %collective-permute-done.k_r.refs_3_ = bf16[6,256,128]{2,1,0:T(8,128)(2,1)S(1)} collective-permute-done((bf16[6,256,128]{2,1,0:T(8,128)(2,1)S(1)}, bf16[6,256,128]{2,1,0:T(8,128)(2,1)S(1)}, u32[]{:S(2)}, u32[]{:S(2)}) %collective-permute-start) | collective-permute-done | bytes 393248 | tf_op jit(solution)/shard_map/ppermute | solution.py:559
  29.1 2.9 %collective-permute-start.5 = (bf16[6,256,128]{2,1,0:T(8,128)(2,1)S(1)}, bf16[6,256,128]{2,1,0:T(8,128)(2,1)S(1)}, u32[]{:S(2)}, u32[]{:S(2)}) collective-permute-start(bf16[6,256,128]{2,1,0:T(8,128)(2,1)S(1)} %collective-permute-done.3.v_l.refs_7_), channel_id=1, source_target_pairs={{0,24},{8,0},{16,8},{24,16},{32,56},{40,32},{48,40},{56,48},{64,88... | collective-permute-start | bytes 1179656 | tf_op jit(solution)/shard_map/ppermute | solution.py:559
  32.0 5.5 %collective-permute-done.1.k_l.refs_4_ = bf16[6,256,128]{2,1,0:T(8,128)(2,1)S(1)} collective-permute-done((bf16[6,256,128]{2,1,0:T(8,128)(2,1)S(1)}, bf16[6,256,128]{2,1,0:T(8,128)(2,1)S(1)}, u32[]{:S(2)}, u32[]{:S(2)}) %collective-permute-start.1) | collective-permute-done | bytes 393248 | tf_op jit(solution)/shard_map/ppermute | solution.py:559
  38.6 2.2 %collective-permute-start.9 = (bf16[1024,128]{1,0:T(8,128)(2,1)}, bf16[1024,128]{1,0:T(8,128)(2,1)S(1)}, u32[]{:S(2)}, u32[]{:S(2)}) collective-permute-start(bf16[1024,128]{1,0:T(8,128)(2,1)} %get-tuple-element.13.q_ref), channel_id=1, source_target_pairs={{0,96},{8,104},{16,112},{24,120},{32,0},{40,8},{48,16},{56,24},{64... | collective-permute-start | bytes 786440 | tf_op jit(solution)/shard_map/ppermute | solution.py:562
  40.8 2.7 %prompt_near.2.refs_5_ = f32[1024,256]{1,0:T(8,128)S(1)} custom-call(s32[128]{0:T(128)S(1)} %copy-done.13, s32[1]{0:T(128)} %bitcast.1.at_ref.refs_1_, bf16[6,256,128]{2,1,0:T(8,128)(2,1)} %bitcast.8, bf16[6,256,128]{2,1,0:T(8,128)(2,1)} %copy-done.4, bf16[6,256,128]{2,1,0:T(8,128)(2,1)} %copy-done.8, bf16[6,256,128]{2,1,0:T(8,128)(2,1)} %bitcast.13, ...), custom_call_target="tpu_custom_call" | custom-call | tf_op jit(solution)/shard_map/prompt_near/pallas_call | solution.py:181
  43.5 1.8 %collective-permute-done.8.refs_8_.refs_4_ = bf16[1024,128]{1,0:T(8,128)(2,1)S(1)} collective-permute-done((bf16[1024,128]{1,0:T(8,128)(2,1)}, bf16[1024,128]{1,0:T(8,128)(2,1)S(1)}, u32[]{:S(2)}, u32[]{:S(2)}) %collective-permute-start.8) | collective-permute-done | bytes 262176 | tf_op jit(solution)/shard_map/ppermute | solution.py:562
  45.4 3.5 %prompt_near.3 = (f32[1024,256]{1,0:T(8,128)S(1)}, f32[1024,256]{1,0:T(8,128)S(1)}) custom-call(s32[128]{0:T(128)S(1)} %copy-done.13, s32[1]{0:T(128)} %bitcast.1.at_ref.refs_1_, bf16[6,256,128]{2,1,0:T(8,128)(2,1)} %bitcast.9, bf16[6,256,128]{2,1,0:T(8,128)(2,1)} %copy-done.4, bf16[6,256,128]{2,1,0:T(8,128)(2,1)} %copy-done.8, ...), custom_call_target="tpu_custom_call" | custom-call | tf_op jit(solution)/shard_map/prompt_near/pallas_call | solution.py:181
  50.4 3.3 %collective-permute-start.10 = (bf16[1040,128]{1,0:T(8,128)(2,1)S(1)}, bf16[1040,128]{1,0:T(8,128)(2,1)S(1)}, u32[]{:S(2)}, u32[]{:S(2)}) collective-permute-start(bf16[1040,128]{1,0:T(8,128)(2,1)S(1)} %get-tuple-element.18), channel_id=1, source_target_pairs={{0,96},{8,104},{16,112},{24,120},{32,0},{40,8},{48,16},{56,24},{64... | collective-permute-start | bytes 798728 | tf_op jit(solution)/shard_map/ppermute | solution.py:562
  54.8 1.8 %collective-permute-start.7 = (bf16[1040,128]{1,0:T(8,128)(2,1)S(1)}, bf16[1040,128]{1,0:T(8,128)(2,1)S(1)}, u32[]{:S(2)}, u32[]{:S(2)}) collective-permute-start(bf16[1040,128]{1,0:T(8,128)(2,1)S(1)} %prompt_far.2), channel_id=1, source_target_pairs={{0,64},{8,72},{16,80},{24,88},{32,96},{40,104},{48,112},{56,120},{... | collective-permute-start | bytes 798728 | tf_op jit(solution)/shard_map/ppermute | solution.py:562
  56.6 7.0 %home_attention.1.refs_0_ = f32[1024,256]{1,0:T(8,128)S(1)} custom-call(s32[128]{0:T(128)S(1)} %copy-done.13, s32[1]{0:T(128)} %bitcast.1.at_ref.refs_1_, s32[8]{0:T(128)S(1)} %copy-done.14, bf16[1024,128]{1,0:T(8,128)(2,1)} %get-tuple-element.13.q_ref, bf16[6,256,128]{2,1,0:T(8,128)(2,1)S(1)} %bitcast.12, bf16[6,256,128]{2,1,0:T(8,128)(2,1)S(1)} %copy-done.5, ...), custom_call_target="tpu_custom_call" | custom-call | tf_op jit(solution)/shard_map/home_attention/pallas_call | solution.py:308
  63.6 1.8 %collective-permute-done.11.refs_3_ = bf16[1040,128]{1,0:T(8,128)(2,1)S(1)} collective-permute-done((bf16[1040,128]{1,0:T(8,128)(2,1)S(1)}, bf16[1040,128]{1,0:T(8,128)(2,1)S(1)}, u32[]{:S(2)}, u32[]{:S(2)}) %collective-permute-start.11) | collective-permute-done | bytes 266272 | tf_op jit(solution)/shard_map/ppermute | solution.py:562
  67.4 2.5 %out_proj.3 = (bf16[256,640]{1,0:T(8,128)(2,1)S(1)}, bf16[256,640]{1,0:T(8,128)(2,1)S(1)}) custom-call(s32[1]{0:T(128)} %bitcast.mdl_ref.refs_0_, bf16[256,512]{1,0:T(8,128)(2,1)S(1)} %merge.1.refs_1_, bf16[256,512]{1,0:T(8,128)(2,1)S(1)} %collective-permute-done.12.refs_2_.other_ref, bf16[512,5120]{1,0:T(8,128)(2,1)} %refs_3_.3, ...), custom_call_target="tpu_custom_call" | custom-call | tf_op jit(solution)/shard_map/out_proj/pallas_call | solution.py:504
  71.4 1.8 %collective-permute-start.16 = (bf16[256,640]{1,0:T(8,128)(2,1)S(1)}, bf16[256,640]{1,0:T(8,128)(2,1)S(1)}, u32[]{:S(2)}, u32[]{:S(2)}) collective-permute-start(bf16[256,640]{1,0:T(8,128)(2,1)S(1)} %get-tuple-element.23), channel_id=1, source_target_pairs={{0,6},{1,7},{2,0},{3,1},{4,2},{5,3},{6,4},{7,5},{8,14},{9,15},{10,... | collective-permute-start | bytes 983048 | tf_op jit(solution)/shard_map/ppermute | solution.py:565
  75.0 1.9 %collective-permute-start.14 = (bf16[256,640]{1,0:T(8,128)(2,1)S(1)}, bf16[256,640]{1,0:T(8,128)(2,1)S(1)}, u32[]{:S(2)}, u32[]{:S(2)}) collective-permute-start(bf16[256,640]{1,0:T(8,128)(2,1)S(1)} %out_second.1), channel_id=1, source_target_pairs={{0,4},{1,5},{2,6},{3,7},{4,0},{5,1},{6,2},{7,3},{8,12},{9,13},{10,... | collective-permute-start | bytes 983048 | tf_op jit(solution)/shard_map/ppermute | solution.py:565
  78.1 1.9 %out_proj.2.own_ref = f32[256,640]{1,0:T(8,128)S(1)} custom-call(s32[1]{0:T(128)} %bitcast.mdl_ref.refs_0_, bf16[256,512]{1,0:T(8,128)(2,1)S(1)} %merge.1.refs_1_, bf16[256,512]{1,0:T(8,128)(2,1)S(1)} %collective-permute-done.12.refs_2_.other_ref, bf16[512,5120]{1,0:T(8,128)(2,1)} %refs_3_.3, bf16[4,512,640]{2,1,0:T(8,128)(2,1)} %collective-permute-done.13.refs_4_.refs_3_), custom_call_target="tpu_custom_call" | custom-call | tf_op jit(solution)/shard_map/out_proj/pallas_call | solution.py:504
  80.9 6.3 %collective-permute-done.16.c_ref = bf16[256,640]{1,0:T(8,128)(2,1)S(1)} collective-permute-done((bf16[256,640]{1,0:T(8,128)(2,1)S(1)}, bf16[256,640]{1,0:T(8,128)(2,1)S(1)}, u32[]{:S(2)}, u32[]{:S(2)}) %collective-permute-start.16) | collective-permute-done | bytes 327712 | tf_op jit(solution)/shard_map/ppermute | solution.py:565
  87.3 1.6 %collective-permute-done.14.a_ref = bf16[256,640]{1,0:T(8,128)(2,1)S(1)} collective-permute-done((bf16[256,640]{1,0:T(8,128)(2,1)S(1)}, bf16[256,640]{1,0:T(8,128)(2,1)S(1)}, u32[]{:S(2)}, u32[]{:S(2)}) %collective-permute-start.14) | collective-permute-done | bytes 327712 | tf_op jit(solution)/shard_map/ppermute | solution.py:565
  (54 shorter events, 14.0 us)
Async XLA Ops:
  3.9 63.5 %collective-permute-start.13 = (bf16[4,512,640]{2,1,0:T(8,128)(2,1)}, bf16[4,512,640]{2,1,0:T(8,128)(2,1)}, u32[]{:S(2)}, u32[]{:S(2)}) collective-permute-start(bf16[4,512,640]{2,1,0:T(8,128)(2,1)} %out_columns.1), channel_id=1, source_target_pairs={{0,1},{1,0},{2,3},{3,2},{4,5},{5,4},{6,7},{7,6},{8,9},{9,8},{10,11... | collective-permute-start | bytes 7864328 | tf_op jit(solution)/shard_map/ppermute | solution.py:568
  4.0 11.6 %copy-start = (bf16[6,256,1,128]{3,1,2,0:T(8,128)(2,1)S(1)}, bf16[6,256,1,128]{3,1,2,0:T(8,128)(2,1)}, u32[]{:S(2)}) copy-start(bf16[6,256,1,128]{3,1,2,0:T(8,128)(2,1)} %param.21) | copy-start | bytes 1179652
  4.0 13.2 %copy-start.2 = (bf16[6,256,1,128]{3,1,2,0:T(8,128)(2,1)S(1)}, bf16[6,256,1,128]{3,1,2,0:T(8,128)(2,1)}, u32[]{:S(2)}) copy-start(bf16[6,256,1,128]{3,1,2,0:T(8,128)(2,1)} %param.22) | copy-start | bytes 1179652
  4.0 36.8 %copy-start.13 = (s32[128]{0:T(128)S(1)}, s32[128]{0:T(128)}, u32[]{:S(2)}) copy-start(s32[128]{0:T(128)} %refs_0_.7) | copy-start | bytes 1540
  11.5 11.2 %collective-permute-start.6 = (bf16[1024,128]{1,0:T(8,128)(2,1)}, bf16[1024,128]{1,0:T(8,128)(2,1)S(1)}, u32[]{:S(2)}, u32[]{:S(2)}) collective-permute-start(bf16[1024,128]{1,0:T(8,128)(2,1)} %get-tuple-element.13.q_ref), channel_id=1, source_target_pairs={{0,64},{8,72},{16,80},{24,88},{32,96},{40,104},{48,112},{56,120},{... | collective-permute-start | bytes 786440 | tf_op jit(solution)/shard_map/ppermute | solution.py:562
  15.6 13.2 %collective-permute-start = (bf16[6,256,128]{2,1,0:T(8,128)(2,1)S(1)}, bf16[6,256,128]{2,1,0:T(8,128)(2,1)S(1)}, u32[]{:S(2)}, u32[]{:S(2)}) collective-permute-start(bf16[6,256,128]{2,1,0:T(8,128)(2,1)S(1)} %bitcast.10), channel_id=1, source_target_pairs={{0,8},{8,16},{16,24},{24,0},{32,40},{40,48},{48,56},{56,32},{64,72... | collective-permute-start | bytes 1179656 | tf_op jit(solution)/shard_map/ppermute | solution.py:559
  17.1 12.0 %collective-permute-start.3 = (bf16[6,256,128]{2,1,0:T(8,128)(2,1)S(1)}, bf16[6,256,128]{2,1,0:T(8,128)(2,1)S(1)}, u32[]{:S(2)}, u32[]{:S(2)}) collective-permute-start(bf16[6,256,128]{2,1,0:T(8,128)(2,1)S(1)} %bitcast.15), channel_id=1, source_target_pairs={{0,24},{8,0},{16,8},{24,16},{32,56},{40,32},{48,40},{56,48},{64,88... | collective-permute-start | bytes 1179656 | tf_op jit(solution)/shard_map/ppermute | solution.py:559
  18.8 18.8 %collective-permute-start.1 = (bf16[6,256,128]{2,1,0:T(8,128)(2,1)S(1)}, bf16[6,256,128]{2,1,0:T(8,128)(2,1)S(1)}, u32[]{:S(2)}, u32[]{:S(2)}) collective-permute-start(bf16[6,256,128]{2,1,0:T(8,128)(2,1)S(1)} %bitcast.11), channel_id=1, source_target_pairs={{0,24},{8,0},{16,8},{24,16},{32,56},{40,32},{48,40},{56,48},{64,88... | collective-permute-start | bytes 1179656 | tf_op jit(solution)/shard_map/ppermute | solution.py:559
  22.7 15.9 %collective-permute-start.2 = (bf16[6,256,128]{2,1,0:T(8,128)(2,1)S(1)}, bf16[6,256,128]{2,1,0:T(8,128)(2,1)S(1)}, u32[]{:S(2)}, u32[]{:S(2)}) collective-permute-start(bf16[6,256,128]{2,1,0:T(8,128)(2,1)S(1)} %bitcast.16), channel_id=1, source_target_pairs={{0,8},{8,16},{16,24},{24,0},{32,40},{40,48},{48,56},{56,32},{64,72... | collective-permute-start | bytes 1179656 | tf_op jit(solution)/shard_map/ppermute | solution.py:559
  28.8 12.0 %copy-start.4 = (bf16[6,256,128]{2,1,0:T(8,128)(2,1)}, bf16[6,256,128]{2,1,0:T(8,128)(2,1)S(1)}, u32[]{:S(2)}) copy-start(bf16[6,256,128]{2,1,0:T(8,128)(2,1)S(1)} %collective-permute-done.k_r.refs_3_) | copy-start | bytes 1179652
  28.8 20.1 %collective-permute-start.4 = (bf16[6,256,128]{2,1,0:T(8,128)(2,1)S(1)}, bf16[6,256,128]{2,1,0:T(8,128)(2,1)S(1)}, u32[]{:S(2)}, u32[]{:S(2)}) collective-permute-start(bf16[6,256,128]{2,1,0:T(8,128)(2,1)S(1)} %collective-permute-done.k_r.refs_3_), channel_id=1, source_target_pairs={{0,8},{8,16},{16,24},{24,0},{32,40},{40,48},{48,56},{56,32},{64,72... | collective-permute-start | bytes 1179656 | tf_op jit(solution)/shard_map/ppermute | solution.py:559
  29.1 11.7 %copy-start.6 = (bf16[6,256,128]{2,1,0:T(8,128)(2,1)}, bf16[6,256,128]{2,1,0:T(8,128)(2,1)S(1)}, u32[]{:S(2)}) copy-start(bf16[6,256,128]{2,1,0:T(8,128)(2,1)S(1)} %collective-permute-done.3.v_l.refs_7_) | copy-start | bytes 1179652
  29.1 19.7 %collective-permute-start.5 = (bf16[6,256,128]{2,1,0:T(8,128)(2,1)S(1)}, bf16[6,256,128]{2,1,0:T(8,128)(2,1)S(1)}, u32[]{:S(2)}, u32[]{:S(2)}) collective-permute-start(bf16[6,256,128]{2,1,0:T(8,128)(2,1)S(1)} %collective-permute-done.3.v_l.refs_7_), channel_id=1, source_target_pairs={{0,24},{8,0},{16,8},{24,16},{32,56},{40,32},{48,40},{56,48},{64,88... | collective-permute-start | bytes 1179656 | tf_op jit(solution)/shard_map/ppermute | solution.py:559
  37.6 7.8 %collective-permute-start.8 = (bf16[1024,128]{1,0:T(8,128)(2,1)}, bf16[1024,128]{1,0:T(8,128)(2,1)S(1)}, u32[]{:S(2)}, u32[]{:S(2)}) collective-permute-start(bf16[1024,128]{1,0:T(8,128)(2,1)} %get-tuple-element.13.q_ref), channel_id=1, source_target_pairs={{0,32},{8,40},{16,48},{24,56},{32,64},{40,72},{48,80},{56,88},{64,... | collective-permute-start | bytes 786440 | tf_op jit(solution)/shard_map/ppermute | solution.py:562
  38.6 6.8 %collective-permute-start.9 = (bf16[1024,128]{1,0:T(8,128)(2,1)}, bf16[1024,128]{1,0:T(8,128)(2,1)S(1)}, u32[]{:S(2)}, u32[]{:S(2)}) collective-permute-start(bf16[1024,128]{1,0:T(8,128)(2,1)} %get-tuple-element.13.q_ref), channel_id=1, source_target_pairs={{0,96},{8,104},{16,112},{24,120},{32,0},{40,8},{48,16},{56,24},{64... | collective-permute-start | bytes 786440 | tf_op jit(solution)/shard_map/ppermute | solution.py:562
  48.9 7.7 %copy-start.1 = (bf16[6,256,1,128]{3,1,2,0:T(8,128)(2,1)S(1)}, bf16[6,256,1,128]{3,1,2,0:T(8,128)(2,1)}, u32[]{:S(2)}) copy-start(bf16[6,256,1,128]{3,1,2,0:T(8,128)(2,1)} %param.21) | copy-start | bytes 1179652
  48.9 7.7 %copy-start.3 = (bf16[6,256,1,128]{3,1,2,0:T(8,128)(2,1)S(1)}, bf16[6,256,1,128]{3,1,2,0:T(8,128)(2,1)}, u32[]{:S(2)}) copy-start(bf16[6,256,1,128]{3,1,2,0:T(8,128)(2,1)} %param.22) | copy-start | bytes 1179652
  50.4 13.3 %collective-permute-start.10 = (bf16[1040,128]{1,0:T(8,128)(2,1)S(1)}, bf16[1040,128]{1,0:T(8,128)(2,1)S(1)}, u32[]{:S(2)}, u32[]{:S(2)}) collective-permute-start(bf16[1040,128]{1,0:T(8,128)(2,1)S(1)} %get-tuple-element.18), channel_id=1, source_target_pairs={{0,96},{8,104},{16,112},{24,120},{32,0},{40,8},{48,16},{56,24},{64... | collective-permute-start | bytes 798728 | tf_op jit(solution)/shard_map/ppermute | solution.py:562
  53.7 11.8 %collective-permute-start.11 = (bf16[1040,128]{1,0:T(8,128)(2,1)S(1)}, bf16[1040,128]{1,0:T(8,128)(2,1)S(1)}, u32[]{:S(2)}, u32[]{:S(2)}) collective-permute-start(bf16[1040,128]{1,0:T(8,128)(2,1)S(1)} %get-tuple-element.19), channel_id=1, source_target_pairs={{0,32},{8,40},{16,48},{24,56},{32,64},{40,72},{48,80},{56,88},{64,... | collective-permute-start | bytes 798728 | tf_op jit(solution)/shard_map/ppermute | solution.py:562
  54.8 10.7 %collective-permute-start.7 = (bf16[1040,128]{1,0:T(8,128)(2,1)S(1)}, bf16[1040,128]{1,0:T(8,128)(2,1)S(1)}, u32[]{:S(2)}, u32[]{:S(2)}) collective-permute-start(bf16[1040,128]{1,0:T(8,128)(2,1)S(1)} %prompt_far.2), channel_id=1, source_target_pairs={{0,64},{8,72},{16,80},{24,88},{32,96},{40,104},{48,112},{56,120},{... | collective-permute-start | bytes 798728 | tf_op jit(solution)/shard_map/ppermute | solution.py:562
  65.7 1.6 %collective-permute-start.12 = (bf16[256,512]{1,0:T(8,128)(2,1)S(1)}, bf16[256,512]{1,0:T(8,128)(2,1)S(1)}, u32[]{:S(2)}, u32[]{:S(2)}) collective-permute-start(bf16[256,512]{1,0:T(8,128)(2,1)S(1)} %merge.1.refs_1_), channel_id=1, source_target_pairs={{0,1},{1,0},{2,3},{3,2},{4,5},{5,4},{6,7},{7,6},{8,9},{9,8},{10,11... | collective-permute-start | bytes 786440 | tf_op jit(solution)/shard_map/ppermute | solution.py:568
  69.9 11.1 %collective-permute-start.15 = (bf16[256,640]{1,0:T(8,128)(2,1)S(1)}, bf16[256,640]{1,0:T(8,128)(2,1)S(1)}, u32[]{:S(2)}, u32[]{:S(2)}) collective-permute-start(bf16[256,640]{1,0:T(8,128)(2,1)S(1)} %get-tuple-element.22), channel_id=1, source_target_pairs={{0,2},{1,3},{2,4},{3,5},{4,6},{5,7},{6,0},{7,1},{8,10},{9,11},{10,... | collective-permute-start | bytes 983048 | tf_op jit(solution)/shard_map/ppermute | solution.py:565
  71.4 15.9 %collective-permute-start.16 = (bf16[256,640]{1,0:T(8,128)(2,1)S(1)}, bf16[256,640]{1,0:T(8,128)(2,1)S(1)}, u32[]{:S(2)}, u32[]{:S(2)}) collective-permute-start(bf16[256,640]{1,0:T(8,128)(2,1)S(1)} %get-tuple-element.23), channel_id=1, source_target_pairs={{0,6},{1,7},{2,0},{3,1},{4,2},{5,3},{6,4},{7,5},{8,14},{9,15},{10,... | collective-permute-start | bytes 983048 | tf_op jit(solution)/shard_map/ppermute | solution.py:565
  75.0 13.9 %collective-permute-start.14 = (bf16[256,640]{1,0:T(8,128)(2,1)S(1)}, bf16[256,640]{1,0:T(8,128)(2,1)S(1)}, u32[]{:S(2)}, u32[]{:S(2)}) collective-permute-start(bf16[256,640]{1,0:T(8,128)(2,1)S(1)} %out_second.1), channel_id=1, source_target_pairs={{0,4},{1,5},{2,6},{3,7},{4,0},{5,1},{6,2},{7,3},{8,12},{9,13},{10,... | collective-permute-start | bytes 983048 | tf_op jit(solution)/shard_map/ppermute | solution.py:565
  (8 other events, 49.4 us)
